TPU v7x, 512 devices: a whole 4x4x16 slice. The times are simulated.
512 devices in a mesh: fsdp: 32 (over y, z_lo), tp: 16 (over z_hi, x, core).
Axes of the slice: x: 4, y: 4, z: 16 (z_hi: 2, z_lo: 8; z = z_hi * 8 + z_lo), core: 2. Of those that a mesh axis runs over, the one named last changes fastest.
Arguments:
- llm_query: bfloat16 [32, 64, 8192], P('fsdp', None, 'tp'), may hold values from -15 to 15
- llm_kv: bfloat16 [32, 2, 320, 1024], P('fsdp', None, 'tp'), may hold values from -15 to 15
- connector: bfloat16 [8192, 6144], P('tp', 'fsdp'), may hold values from -0.75 to 0.75
- self_query: bfloat16 [32, 2, 1024, 3072], P('fsdp', None, 'tp'), may hold values from -15 to 15
- self_key: bfloat16 [32, 2, 1024, 3072], P('fsdp', None, 'tp'), may hold values from -15 to 15
- latent_value: bfloat16 [32, 2, 1024, 3072], P('fsdp', None, 'tp'), may hold values from -6 to 6
- cotangent: bfloat16 [32, 2, 1024, 3072], P('fsdp', None, 'tp'), may hold values from -6 to 6
Outputs:
- latent_out: bfloat16 [32, 2, 1024, 3072], P('fsdp', None, 'tp')
- self_grad: bfloat16 [32, 2, 1024, 3072], P('fsdp', None, 'tp')
- context_grad: bfloat16 [32, 2, 64, 3072], P('fsdp', None, None, 'tp')
All inputs are finite; a program needn't handle non-finite values.
Results may differ from a plain program's by a relative error of at most 0.015.
Values may be sent and summed in bfloat16 or wider, within the bound.
No kernel may reach another device: no remote copies, remote signals or barrier semaphores. Data moves between devices by JAX's collectives and lax.ppermute only.
A program may use at most 128 MiB of HBM per device.

v0:
```python
import jax
import jax.numpy as jnp
from jax import lax
from jax.sharding import PartitionSpec as P

HEAD_SIZE = 128
LLM_HEADS = 64
LLM_KV = 8
DENOISER_HEADS = 24
QUERY_TOKENS = 64
LATENT_TOKENS = 1024
SAMPLE_COUNT = 2
PROMPT = 256


norm_eps = 1e-06


def softmax_rows(scores, axis_index):
    top_value = jnp.max(scores, axis=axis_index, keepdims=True)
    exp_terms = jnp.exp(scores - top_value)
    return exp_terms / jnp.sum(exp_terms, axis=axis_index, keepdims=True)


def llm_hidden(llm_query, llm_kv):
    whole_kv = lax.all_gather(llm_kv, "tp", axis=2, tiled=True)
    query_heads = llm_query.shape[2] // HEAD_SIZE
    group_total = LLM_HEADS // LLM_KV
    kv_heads = max(query_heads // group_total, 1)
    group_size = query_heads // kv_heads
    first_kv = lax.axis_index("tp") * query_heads // group_total
    local_kv = lax.dynamic_slice_in_dim(whole_kv, first_kv * HEAD_SIZE, kv_heads * HEAD_SIZE, 3)
    positions = local_kv.shape[2]
    queries = llm_query[0].reshape(QUERY_TOKENS, kv_heads, group_size, HEAD_SIZE)
    keys_all = local_kv[0, 0].reshape(positions, kv_heads, HEAD_SIZE)
    values_all = local_kv[0, 1].reshape(positions, kv_heads, HEAD_SIZE)
    scores = jnp.einsum(
        "qkgd,pkd->kgqp", queries, keys_all, preferred_element_type=jnp.float32
    ) * HEAD_SIZE ** (-0.5)
    allowed = jnp.arange(positions)[None, :] <= PROMPT + jnp.arange(QUERY_TOKENS)[:, None]
    scores = jnp.where(allowed, scores, -1e30)
    weights = softmax_rows(scores, 3).astype(jnp.bfloat16)
    mixed_heads = jnp.einsum(
        "kgqp,pkd->qkgd", weights, values_all, preferred_element_type=jnp.float32
    )
    return mixed_heads.astype(jnp.bfloat16).reshape(QUERY_TOKENS, query_heads * HEAD_SIZE)


def rms_inverse(incoming_values):
    return lax.rsqrt(jnp.mean(incoming_values * incoming_values, axis=-1, keepdims=True) + norm_eps)


def norm_back(grad_normed, normed, inverse):
    return inverse * (grad_normed - normed * jnp.mean(grad_normed * normed, axis=-1, keepdims=True))


def cross_core(latent_heads, condition_keys, condition_values, gradient_heads):
    score_scale = HEAD_SIZE ** (-0.5)
    self_float = latent_heads.astype(jnp.float32)
    query_inverse = rms_inverse(self_float)
    query_normed = self_float * query_inverse
    query_round = query_normed.astype(jnp.bfloat16)
    key_float = condition_keys.astype(jnp.float32)
    key_inverse = rms_inverse(key_float)
    key_normed = key_float * key_inverse
    key_round = key_normed.astype(jnp.bfloat16)
    scores = (
        jnp.einsum("hrd,chd->hcr", query_round, key_round, preferred_element_type=jnp.float32)
        * score_scale
    )
    exp_terms = jnp.exp(scores)
    attention_weights = exp_terms / jnp.sum(exp_terms, axis=1, keepdims=True)
    weights_round = attention_weights.astype(jnp.bfloat16)
    cross_out = jnp.einsum(
        "hcr,chd->hrd", weights_round, condition_values, preferred_element_type=jnp.float32
    )
    total_heads = self_float + cross_out
    value_gradient = jnp.einsum(
        "hcr,hrd->chd", weights_round, gradient_heads, preferred_element_type=jnp.float32
    )
    weight_grad = jnp.einsum(
        "hrd,chd->hcr", gradient_heads, condition_values, preferred_element_type=jnp.float32
    )
    delta_rows = jnp.sum(attention_weights * weight_grad, axis=1, keepdims=True)
    score_grad = (attention_weights * (weight_grad - delta_rows) * score_scale).astype(jnp.bfloat16)
    query_grad = jnp.einsum(
        "hcr,chd->hrd", score_grad, key_round, preferred_element_type=jnp.float32
    )
    key_grad_normed = jnp.einsum(
        "hcr,hrd->chd", score_grad, query_round, preferred_element_type=jnp.float32
    )
    self_grad = gradient_heads.astype(jnp.float32) + norm_back(
        query_grad, query_normed, query_inverse
    )
    key_gradient = norm_back(key_grad_normed, key_normed, key_inverse)
    return (total_heads, self_grad, key_gradient, value_gradient)


def self_attention(head_query, head_key, head_value):
    block_rows = min(512, LATENT_TOKENS)
    pieces = []
    for block_start in range(0, LATENT_TOKENS, block_rows):
        block_query = head_query[:, block_start : block_start + block_rows]
        scores = jnp.einsum(
            "iqd,ikd->iqk", block_query, head_key, preferred_element_type=jnp.float32
        ) * HEAD_SIZE ** (-0.5)
        weights = softmax_rows(scores, 2).astype(jnp.bfloat16)
        pieces.append(
            jnp.einsum(
                "iqk,ikd->iqd", weights, head_value, preferred_element_type=jnp.float32
            ).astype(jnp.bfloat16)
        )
    return jnp.concatenate(pieces, axis=1)


def shards(llm_query, llm_kv, connector, self_query, self_key, latent_value, cotangent):
    hidden = llm_hidden(llm_query, llm_kv)
    partial_kv = jnp.dot(
        hidden,
        lax.all_gather(connector, "fsdp", axis=1, tiled=True),
        preferred_element_type=jnp.float32,
    )
    condition_tokens = lax.psum(partial_kv, "tp").astype(jnp.bfloat16)
    device_rows = self_query.shape[2]

    def heads_first(incoming_values):
        return (
            incoming_values[0]
            .reshape(SAMPLE_COUNT, device_rows, DENOISER_HEADS, HEAD_SIZE)
            .transpose(0, 2, 1, 3)
            .reshape(SAMPLE_COUNT * DENOISER_HEADS, device_rows, HEAD_SIZE)
        )

    head_query, head_key, head_value = (
        lax.all_to_all(heads_first(self_query), "tp", split_axis=0, concat_axis=1, tiled=True),
        lax.all_to_all(heads_first(self_key), "tp", split_axis=0, concat_axis=1, tiled=True),
        lax.all_to_all(heads_first(latent_value), "tp", split_axis=0, concat_axis=1, tiled=True),
    )
    head_out = self_attention(head_query, head_key, head_value)
    sequence_output = lax.all_to_all(head_out, "tp", split_axis=1, concat_axis=0, tiled=True)
    gathered_rows = SAMPLE_COUNT * device_rows
    latent_heads = (
        sequence_output.reshape(SAMPLE_COUNT, DENOISER_HEADS, device_rows, HEAD_SIZE)
        .transpose(1, 0, 2, 3)
        .reshape(DENOISER_HEADS, gathered_rows, HEAD_SIZE)
    )
    gradient_heads = (
        cotangent[0]
        .reshape(SAMPLE_COUNT, device_rows, DENOISER_HEADS, HEAD_SIZE)
        .transpose(2, 0, 1, 3)
        .reshape(DENOISER_HEADS, gathered_rows, HEAD_SIZE)
    )
    model_width = DENOISER_HEADS * HEAD_SIZE
    condition_keys = condition_tokens[:, :model_width].reshape(
        QUERY_TOKENS, DENOISER_HEADS, HEAD_SIZE
    )
    condition_values = condition_tokens[:, model_width:].reshape(
        QUERY_TOKENS, DENOISER_HEADS, HEAD_SIZE
    )
    total_heads, grad_total, key_gradient, value_gradient = cross_core(
        latent_heads, condition_keys, condition_values, gradient_heads
    )

    def to_rows(incoming_values):
        return (
            incoming_values.reshape(DENOISER_HEADS, SAMPLE_COUNT, device_rows, HEAD_SIZE)
            .transpose(1, 2, 0, 3)
            .reshape(1, SAMPLE_COUNT, device_rows, DENOISER_HEADS * HEAD_SIZE)
            .astype(jnp.bfloat16)
        )

    latent_out = to_rows(total_heads)
    self_grad = to_rows(grad_total)
    partial_grad = jnp.stack(
        [
            key_gradient.reshape(QUERY_TOKENS, model_width),
            value_gradient.reshape(QUERY_TOKENS, model_width),
        ]
    )[None]
    context_grad = lax.psum_scatter(
        partial_grad.astype(jnp.bfloat16), "tp", scatter_dimension=3, tiled=True
    )
    return (latent_out, self_grad, context_grad)


def solution(mesh):
    placed = (
        P("fsdp", None, "tp"),
        P("fsdp", None, "tp", None),
        P("tp", "fsdp"),
        P("fsdp", None, "tp", None),
        P("fsdp", None, "tp", None),
        P("fsdp", None, "tp", None),
        P("fsdp", None, "tp", None),
    )
    return jax.shard_map(
        shards,
        mesh=mesh,
        in_specs=placed,
        out_specs=(
            P("fsdp", None, "tp", None),
            P("fsdp", None, "tp", None),
            P("fsdp", None, None, "tp"),
        ),
        check_vma=False,
    )
```

profile of v0, /device:TPU:8, one launch (start us, length us, event | category | flops | bytes accessed | tf_op | source)
XLA Modules:
  0.0 708.9 jit_solution(14450436883221754212)
XLA Ops:
  7.2 1.3 copy.166
  8.6 1.1 copy.136
  9.6 17.7 %all-to-all-start.2 = ((bf16[48,64,128]{2,1,0:T(8,128)(2,1)}), bf16[48,64,128]{2,1,0:T(8,128)(2,1)S(1)}, u32[]{:S(2)}, u32[]{:S(2)}) async-start(bf16[48,64,128]{2,1,0:T(8,128)(2,1)} %bitcast.11), calls=%async_computation.2 | async-start | bytes 1572864 | tf_op jit(solution)/shard_map/all_to_all | solution.py:137
  28.3 1.1 copy.134
  29.4 25.5 %all-to-all-done.2 = bf16[48,64,128]{2,1,0:T(8,128)(2,1)S(1)} async-done(((bf16[48,64,128]{2,1,0:T(8,128)(2,1)}), bf16[48,64,128]{2,1,0:T(8,128)(2,1)S(1)}, u32[]{:S(2)}, u32[]{:S(2)}) %all-to-all-start.2) | async-done | bytes 786464 | tf_op jit(solution)/shard_map/all_to_all | solution.py:137
  54.9 3.6 all-to-all-start.1
  58.6 0.7 all-gather.5.cloned.1.call-update
  59.5 1.1 copy.132
  60.6 22.8 %all-to-all-done.1 = bf16[48,64,128]{2,1,0:T(8,128)(2,1)S(1)} async-done(((bf16[48,64,128]{2,1,0:T(8,128)(2,1)}), bf16[48,64,128]{2,1,0:T(8,128)(2,1)S(1)}, u32[]{:S(2)}, u32[]{:S(2)}) %all-to-all-start.1) | async-done | bytes 786464 | tf_op jit(solution)/shard_map/all_to_all | solution.py:136
  83.4 12.0 %all-to-all-start = ((bf16[48,64,128]{2,1,0:T(8,128)(2,1)}), bf16[48,64,128]{2,1,0:T(8,128)(2,1)S(1)}, u32[]{:S(2)}, u32[]{:S(2)}) async-start(bf16[48,64,128]{2,1,0:T(8,128)(2,1)} %bitcast.1), calls=%async_computation | async-start | bytes 1572864 | tf_op jit(solution)/shard_map/all_to_all | solution.py:135
  95.5 41.1 %all-to-all-done = bf16[48,64,128]{2,1,0:T(8,128)(2,1)S(1)} async-done(((bf16[48,64,128]{2,1,0:T(8,128)(2,1)}), bf16[48,64,128]{2,1,0:T(8,128)(2,1)S(1)}, u32[]{:S(2)}, u32[]{:S(2)}) %all-to-all-start) | async-done | bytes 786464 | tf_op jit(solution)/shard_map/all_to_all | solution.py:135
  136.7 4.6 fusion.78
  141.4 4.6 fusion.83
  145.9 4.0 fusion.21
  150.5 1.0 fusion.22
  151.7 1.7 copy.138
  153.3 4.4 all-to-all-start.3
  158.5 1.4 constant_dynamic-slice_fusion
  160.8 28.6 %all-to-all-done.3 = bf16[3,1024,128]{2,0,1:T(4,128)(2,1)S(1)} async-done(((bf16[3,1024,128]{2,0,1:T(4,128)(2,1)}), bf16[3,1024,128]{2,0,1:T(4,128)(2,1)S(1)}, u32[]{:S(2)}, u32[]{:S(2)}) %all-to-all-start.3) | async-done | bytes 786464 | tf_op jit(solution)/shard_map/all_to_all | solution.py:140
  190.5 1.4 fusion.15
  191.8 215.4 %all-gather.5.cloned.1.call-done = bf16[512,6144]{0,1:T(8,128)(2,1)} async-done(((bf16[512,192]{0,1:T(8,128)(2,1)}), bf16[512,6144]{0,1:T(8,128)(2,1)}) %all-gather.5.cloned.1.call-update) | async-done | bytes 6291472 | tf_op jit(solution)/shard_map/all_gather | solution.py:120
  407.3 5.9 fusion.66
  413.2 138.0 %all-reduce.1 = bf16[64,6144]{1,0:T(8,128)(2,1)} all-reduce(f32[64,6144]{1,0:T(8,128)} %fusion.66), channel_id=1, replica_groups=mesh['fsdp'=32,'tp'=16] {'tp'}, use_global_device_ids=true, to_apply=%region_6.7 | all-reduce | flops 393216 | bytes 2359296 | tf_op jit(solution)/shard_map/psum | solution.py:123
  551.1 1.3 convert_bitcast_fusion.2
  552.6 0.9 multiply_reduce_fusion.5
  553.5 1.4 copy.146
  554.9 0.7 add_rsqrt_fusion
  555.6 1.8 fusion.19
  557.4 0.9 copy-done.5
  558.3 1.0 fusion.41
  559.3 2.5 fusion.23
  561.8 1.5 fusion.37
  563.6 0.9 stack.8
  564.5 3.4 multiply_reduce_fusion.4
  567.9 1.6 multiply_convert_fusion
  569.8 0.9 stack.7
  570.7 2.1 pad_maximum_fusion.1
  572.8 4.4 copy.157
  577.2 3.9 reshape.199
  581.1 2.7 fusion.14
  583.8 2.5 copy.151
  586.4 2.2 convert_element_type.141
  588.5 4.1 multiply_reduce_fusion.2
  592.6 2.2 add_convert_fusion
  595.3 1.2 convert_element_type.147
  596.5 104.3 %reduce-scatter.4.cloned.1.call-done = bf16[192,128]{1,0:T(8,128)(2,1)} async-done(((bf16[3072,128]{1,0:T(8,128)(2,1)}), bf16[192,128]{1,0:T(8,128)(2,1)}) %reduce-scatter.4.cloned.1.call-update) | async-done | bytes 49168
  700.8 0.9 reshape.200
  701.7 0.7 copy.158
  (60 shorter events, 6.0 us)
Async XLA Ops:
  8.5 19.5 %copy-start.2 = (bf16[1,2,64,3072]{3,2,1,0:T(8,128)(2,1)S(1)}, bf16[1,2,64,3072]{3,2,1,0:T(8,128)(2,1)}, u32[]{:S(2)}) copy-start(bf16[1,2,64,3072]{3,2,1,0:T(8,128)(2,1)} %param.11) | copy-start | bytes 2359300
  9.6 45.3 %all-to-all-start.2 = ((bf16[48,64,128]{2,1,0:T(8,128)(2,1)}), bf16[48,64,128]{2,1,0:T(8,128)(2,1)S(1)}, u32[]{:S(2)}, u32[]{:S(2)}) async-start(bf16[48,64,128]{2,1,0:T(8,128)(2,1)} %bitcast.11), calls=%async_computation.2 | async-start | bytes 1572864 | tf_op jit(solution)/shard_map/all_to_all | solution.py:137
  27.3 131.2 %all-gather.3.cloned.1.call-start = ((), (), s32[]{:S(2)}) async-start(), calls=%async_computation.5 | async-start | bytes 1392640 | tf_op jit(solution)/shard_map/all_gather | solution.py:26
  28.3 31.0 %copy-start.3 = (bf16[1,2,64,3072]{3,2,1,0:T(8,128)(2,1)S(1)}, bf16[1,2,64,3072]{3,2,1,0:T(8,128)(2,1)}, u32[]{:S(2)}) copy-start(bf16[1,2,64,3072]{3,2,1,0:T(8,128)(2,1)} %param.10) | copy-start | bytes 2359300
  54.9 28.5 %all-to-all-start.1 = ((bf16[48,64,128]{2,1,0:T(8,128)(2,1)}), bf16[48,64,128]{2,1,0:T(8,128)(2,1)S(1)}, u32[]{:S(2)}, u32[]{:S(2)}) async-start(bf16[48,64,128]{2,1,0:T(8,128)(2,1)} %bitcast.6), calls=%async_computation.1 | async-start | bytes 1572864 | tf_op jit(solution)/shard_map/all_to_all | solution.py:136
  58.5 348.7 %all-gather.5.cloned.1.call-start = ((), (), s32[]{:S(2)}) async-start(), calls=%async_computation.6 | async-start | bytes 6488064 | tf_op jit(solution)/shard_map/all_gather | solution.py:120
  83.4 53.2 %all-to-all-start = ((bf16[48,64,128]{2,1,0:T(8,128)(2,1)}), bf16[48,64,128]{2,1,0:T(8,128)(2,1)S(1)}, u32[]{:S(2)}, u32[]{:S(2)}) async-start(bf16[48,64,128]{2,1,0:T(8,128)(2,1)} %bitcast.1), calls=%async_computation | async-start | bytes 1572864 | tf_op jit(solution)/shard_map/all_to_all | solution.py:135
  145.9 4.6 copy-start.10
  151.7 6.3 copy-start.9
  153.3 4.7 copy-start.4
  153.3 36.0 %all-to-all-start.3 = ((bf16[3,1024,128]{2,0,1:T(4,128)(2,1)}), bf16[3,1024,128]{2,0,1:T(4,128)(2,1)S(1)}, u32[]{:S(2)}, u32[]{:S(2)}) async-start(bf16[3,1024,128]{2,0,1:T(4,128)(2,1)} %copy.138), calls=%async_computation.3 | async-start | bytes 2097152 | tf_op jit(solution)/shard_map/all_to_all | solution.py:140
  157.7 543.0 %reduce-scatter.4.cloned.1.call-start = ((), (), s32[]{:S(2)}) async-start(), calls=%async_computation.7 | async-start | bytes 835584
  190.5 222.7 %copy-start.7 = (f32[24,128]{1,0:T(8,128)}, f32[24,128]{1,0:T(8,128)S(1)}, u32[]{:S(2)}) copy-start(f32[24,128]{1,0:T(8,128)S(1)} %rsqrt.21) | copy-start | bytes 36868
  552.4 9.3 %copy-start = (bf16[8,24,8,128]{3,2,1,0:T(8,128)(2,1)}, bf16[8,24,8,128]{3,2,1,0:T(8,128)(2,1)S(1)}, u32[]{:S(2)}) copy-start(bf16[8,24,8,128]{3,2,1,0:T(8,128)(2,1)S(1)} %get-tuple-element.8) | copy-start | bytes 1179652
  557.4 0.9 copy-start.5
  561.7 1.5 copy-start.6
  577.2 4.0 copy-start.1
  583.8 4.7 copy-start.8
Sparse Core Ops, SparseCore 0:
  31.4 107.5 all-gather.2
  141.1 266.1 all-gather.4
  581.2 119.4 reduce-scatter.3
where the time goes:
time: 710 us; the launch traced here: 709 us
  waiting for transfers between devices  439 us (62%)
  blocking collectives  138 us (19%)
  starting transfers between devices  37.9 us (5%)
  matrix products  36.7 us (5%)
  local copies, waits for them, and re-layouts  30.9 us (4%)
  between operations  14.2 us (2%)
  other arithmetic  12.1 us (2%)
    all_gather x1, waiting for transfers between devices, shards(): lax.all_gather(connector, 'fsdp', axis=1, tiled=True)  215 us
    psum x1, blocking collectives, shards(): condition_tokens = lax.psum(partial_kv, 'tp').astype(jnp.bfloat16)  138 us
    unnamed x4, waiting for transfers between devices  106 us
    all_to_all x1, waiting for transfers between devices, shards(): lax.all_to_all(heads_first(self_query), 'tp', split_axis=0, concat_axis=1...  41.1 us
    all_to_all x1, waiting for transfers between devices, shards(): lax.all_to_all(head_out, 'tp', split_axis=1, concat_axis=0, tiled=True)  28.6 us
    all_to_all x1, waiting for transfers between devices, shards(): lax.all_to_all(heads_first(latent_value), 'tp', split_axis=0, concat_axis...  25.5 us
    all_to_all x1, waiting for transfers between devices, shards(): lax.all_to_all(heads_first(self_key), 'tp', split_axis=0, concat_axis=1,...  22.8 us
    all_to_all x1, starting transfers between devices, shards(): lax.all_to_all(heads_first(latent_value), 'tp', split_axis=0, concat_axis...  17.7 us
  transfers between devices with their start and end apart: 7, of which 6 were waited for; matrix products, arithmetic and copies ran while one was open for 6% of the time, Pallas kernels for 0%

commit v1 on v0

v1 whole, which is shorter than its diff:
```python
import jax
import jax.numpy as jnp
from jax import lax
from jax.experimental import pallas as pl
from jax.sharding import PartitionSpec as P


HEAD_SIZE = 128
QUERY_TOKENS = 64
LATENT_TOKENS = 1024
SAMPLE_COUNT = 2
PROMPT = 256

SCALE = HEAD_SIZE ** (-0.5)
LOG2E = 1.4426950408889634
norm_eps = 1e-06


HALVES = [list(range(8)), list(range(8, 16))]
SWAP_HALF = [(t, (t + 8) % 16) for t in range(16)]
BLOCK = 3 * HEAD_SIZE


def joint(move):
    pairs = []
    for y in range(4):
        for zl in range(8):
            for h in range(2):
                for m in range(4):
                    for c in range(2):
                        y2, zl2, h2, m2, c2 = move(y, zl, h, m, c)
                        source = (8 * y + zl) * 16 + 8 * h + 2 * m + c
                        target = (8 * y2 + zl2) * 16 + 8 * h2 + 2 * m2 + c2
                        pairs.append((source, target))
    return pairs


def head_block(j):
    return 4 * (j % 2) + j // 2


def copy_blocks(*refs):
    *x_refs, o_ref = refs
    at = 0
    for x_ref in x_refs:
        count = x_ref.shape[0]
        o_ref[0, at : at + count] = x_ref[...]
        at += count


def to_blocks(*parts):
    rows = parts[0].shape[1]
    count = sum(x.shape[0] for x in parts)
    return pl.pallas_call(
        copy_blocks,
        grid=(8,),
        in_specs=[pl.BlockSpec((x.shape[0], rows, BLOCK), lambda j: (0, 0, head_block(j))) for x in parts],
        out_specs=pl.BlockSpec((1, count, rows, BLOCK), lambda j: (j, 0, 0, 0)),
        out_shape=jax.ShapeDtypeStruct((8, count, rows, BLOCK), parts[0].dtype),
        name="to_blocks",
    )(*parts)


def copy_rows(x_ref, y_ref, a_ref, b_ref):
    a_ref[0] = x_ref[0, 0]
    a_ref[1] = y_ref[0, 0]
    b_ref[0] = x_ref[0, 1]
    b_ref[1] = y_ref[0, 1]


def from_blocks(x, y):
    rows = x.shape[2]
    in_spec = pl.BlockSpec((1, 2, rows, BLOCK), lambda j: (j, 0, 0, 0))
    out_spec = pl.BlockSpec((SAMPLE_COUNT, rows, BLOCK), lambda j: (0, 0, head_block(j)))
    return pl.pallas_call(
        copy_rows,
        grid=(8,),
        in_specs=[in_spec] * 2,
        out_specs=[out_spec] * 2,
        out_shape=[jax.ShapeDtypeStruct((SAMPLE_COUNT, rows, 8 * BLOCK), x.dtype)] * 2,
        name="from_blocks",
    )(x, y)


def exchange(x):
    return lax.all_to_all(x, "tp", split_axis=0, concat_axis=0, axis_index_groups=HALVES)


def llm_hidden(llm_query, llm_kv):
    half = lax.axis_index("tp") // 8
    rows = llm_kv.shape[2]
    kv = llm_kv[0]
    keep = lax.dynamic_slice_in_dim(kv, half * 512, 512, 2)
    give = lax.dynamic_slice_in_dim(kv, (1 - half) * 512, 512, 2)
    take = lax.ppermute(give, "tp", SWAP_HALF)
    both = jnp.stack([keep, take])
    both = both.reshape(2, 2, rows, 4, HEAD_SIZE).transpose(3, 0, 1, 2, 4)
    both = jnp.broadcast_to(both[:, None], (4, 2, 2, 2, rows, HEAD_SIZE))
    got = exchange(both.reshape(8, 2, 2, rows, HEAD_SIZE))
    keys = got[:, :, 0].reshape(16 * rows, HEAD_SIZE)
    values = got[:, :, 1].reshape(16 * rows, HEAD_SIZE)
    source_half = jnp.stack([half, 1 - half])
    place = jnp.arange(8)[:, None, None] + 8 * source_half[None, :, None]
    position = (place * rows + jnp.arange(rows)[None, None, :]).reshape(1, 16 * rows)
    heads = llm_query.shape[2] // HEAD_SIZE
    queries = llm_query[0].reshape(QUERY_TOKENS * heads, HEAD_SIZE)
    scores = jnp.dot(queries, keys.T, preferred_element_type=jnp.float32) * SCALE
    token = (jnp.arange(QUERY_TOKENS * heads) // heads)[:, None]
    scores = jnp.where(position <= PROMPT + token, scores, -1e30)
    top = jnp.max(scores, axis=1, keepdims=True)
    terms = jnp.exp(scores - top)
    weights = (terms / jnp.sum(terms, axis=1, keepdims=True)).astype(jnp.bfloat16)
    mixed = jnp.dot(weights, values, preferred_element_type=jnp.float32)
    return mixed.astype(jnp.bfloat16).reshape(QUERY_TOKENS, heads * HEAD_SIZE)


def gather_run(connector):
    got = connector[None]
    for k in (4, 2, 1):
        pairs = [(8 * a + b, 8 * a + (b ^ k)) for a in range(4) for b in range(8)]
        got = jnp.concatenate([got, lax.ppermute(got, "fsdp", pairs)])
    return got


def gather_ring(hidden):
    got = [hidden]
    for k in (1, 2, 3):
        pairs = [(8 * a + b, 8 * (a ^ k) + b) for a in range(4) for b in range(8)]
        got.append(lax.ppermute(hidden, "fsdp", pairs))
    return jnp.concatenate(got)


def context_tokens(rows, columns):
    f = lax.axis_index("fsdp")
    y, zl = f // 8, f % 8
    width = columns.shape[2]
    part = jnp.einsum("rk,skn->rsn", rows, columns, preferred_element_type=jnp.float32)
    part = part.astype(jnp.bfloat16).reshape(2, 2, QUERY_TOKENS, 2, 2, 2, width)
    part = part.transpose(5, 4, 1, 0, 3, 2, 6).reshape(8, 2, 2, QUERY_TOKENS, width)
    got = exchange(part)
    mine = jnp.sum(got.astype(jnp.float32), axis=0).astype(jnp.bfloat16)
    there = lax.ppermute(mine, "tp", SWAP_HALF)
    mine = (mine.astype(jnp.float32) + there.astype(jnp.float32)).astype(jnp.bfloat16)
    got = []
    for a in range(2):
        pairs = joint(lambda y, z, h, m, c: (y ^ (2 * a + c), z, h, m ^ (z // 2), y % 2))
        got.append(lax.ppermute(mine[a], ("fsdp", "tp"), pairs))
    one, two = got
    keys = jnp.where(y < 2, one, two)
    values = jnp.where(y < 2, two, one)
    both = jnp.stack([keys, values])
    first = jnp.where(zl % 2 == 0, both[:, 0], both[:, 1])
    second = jnp.where(zl % 2 == 0, both[:, 1], both[:, 0])
    return jnp.concatenate([first, second], axis=2)


def attention_kernel(q_ref, near_ref, far_ref, o_ref):
    half = LATENT_TOKENS // 2
    near_k = near_ref[:, 0].reshape(half, HEAD_SIZE)
    far_k = far_ref[:, 0].reshape(half, HEAD_SIZE)
    near_v = near_ref[:, 1].reshape(half, HEAD_SIZE)
    far_v = far_ref[:, 1].reshape(half, HEAD_SIZE)
    transposed = (((1,), (1,)), ((), ()))
    for part in range(4):
        q = q_ref[2 * part : 2 * part + 2, 0].reshape(half // 4, HEAD_SIZE)
        near = lax.dot_general(q, near_k, transposed, preferred_element_type=jnp.float32)
        far = lax.dot_general(q, far_k, transposed, preferred_element_type=jnp.float32)
        top = jnp.maximum(jnp.max(near, axis=1, keepdims=True), jnp.max(far, axis=1, keepdims=True))
        near = jnp.exp2((near - top) * (SCALE * LOG2E))
        far = jnp.exp2((far - top) * (SCALE * LOG2E))
        total = jnp.sum(near, axis=1, keepdims=True) + jnp.sum(far, axis=1, keepdims=True)
        out = jnp.dot(near.astype(jnp.bfloat16), near_v, preferred_element_type=jnp.float32)
        out += jnp.dot(far.astype(jnp.bfloat16), far_v, preferred_element_type=jnp.float32)
        out = (out / total).astype(jnp.bfloat16)
        o_ref[2 * part : 2 * part + 2] = out.reshape(2, half // 8, HEAD_SIZE)


def attention(sample, query_gradient, near, far):
    rows = near.shape[2]
    pair_spec = pl.BlockSpec((8, 2, rows, HEAD_SIZE), lambda n: (0, 0, 0, n))
    return pl.pallas_call(
        attention_kernel,
        grid=(3,),
        in_specs=[
            pl.BlockSpec((8, 1, rows, HEAD_SIZE), lambda n: (0, sample, 0, n)),
            pair_spec,
            pair_spec,
        ],
        out_specs=pl.BlockSpec((8, rows, HEAD_SIZE), lambda n: (0, 0, n)),
        out_shape=jax.ShapeDtypeStruct((8, rows, BLOCK), jnp.bfloat16),
        name="latent_attention",
    )(query_gradient, near, far)


def cross_kernel(so_ref, g_ref, context_ref, *refs):
    carry_ref = refs[0] if len(refs) == 3 else None
    out_ref, cgrad_ref = refs[-2:]
    half = LATENT_TOKENS // 2
    transposed = (((1,), (1,)), ((), ()))
    first = (((0,), (0,)), ((), ()))
    so = so_ref[...].reshape(half, HEAD_SIZE).astype(jnp.float32)
    g = g_ref[:, 0].reshape(half, HEAD_SIZE)
    ck = context_ref[0].astype(jnp.float32)
    cv = context_ref[1]
    r = lax.rsqrt(jnp.mean(so * so, axis=1, keepdims=True) + norm_eps)
    yq = so * r
    qn = yq.astype(jnp.bfloat16)
    rk = lax.rsqrt(jnp.mean(ck * ck, axis=1, keepdims=True) + norm_eps)
    yk = ck * rk
    kn = yk.astype(jnp.bfloat16)
    scores = lax.dot_general(kn, qn, transposed, preferred_element_type=jnp.float32) * SCALE
    terms = jnp.exp(scores)
    cw = terms / jnp.sum(terms, axis=0, keepdims=True)
    cb = cw.astype(jnp.bfloat16)
    cross = lax.dot_general(cb, cv, first, preferred_element_type=jnp.float32)
    out_ref[:, 0] = (so + cross).astype(jnp.bfloat16).reshape(8, half // 8, HEAD_SIZE)
    dcv = jnp.dot(cb, g, preferred_element_type=jnp.float32)
    dcw = lax.dot_general(cv, g, transposed, preferred_element_type=jnp.float32)
    delta = jnp.sum(cw * dcw, axis=0, keepdims=True)
    ds = (cw * (dcw - delta) * SCALE).astype(jnp.bfloat16)
    dqn = lax.dot_general(ds, kn, first, preferred_element_type=jnp.float32)
    dkn = jnp.dot(ds, qn, preferred_element_type=jnp.float32)
    inner = jnp.mean(dqn * yq, axis=1, keepdims=True)
    grad = g.astype(jnp.float32) + r * (dqn - yq * inner)
    out_ref[:, 1] = grad.astype(jnp.bfloat16).reshape(8, half // 8, HEAD_SIZE)
    if carry_ref is None:
        cgrad_ref[0] = dkn
        cgrad_ref[1] = dcv
    else:
        total = carry_ref[0] + dkn
        along = jnp.mean(total * yk, axis=1, keepdims=True)
        cgrad_ref[0] = (rk * (total - yk * along)).astype(jnp.bfloat16)
        cgrad_ref[1] = (carry_ref[1] + dcv).astype(jnp.bfloat16)


def cross(sample, so, query_gradient, context, carry):
    rows = so.shape[1]
    context_spec = pl.BlockSpec((2, QUERY_TOKENS, HEAD_SIZE), lambda n: (0, 0, n))
    pair_spec = pl.BlockSpec((8, 2, rows, HEAD_SIZE), lambda n: (0, 0, 0, n))
    return pl.pallas_call(
        cross_kernel,
        grid=(3,),
        in_specs=[
            pl.BlockSpec((8, rows, HEAD_SIZE), lambda n: (0, 0, n)),
            pl.BlockSpec((8, 1, rows, HEAD_SIZE), lambda n: (0, 2 + sample, 0, n)),
            context_spec,
        ]
        + [context_spec] * len(carry),
        out_specs=[pair_spec, context_spec],
        out_shape=[
            jax.ShapeDtypeStruct((8, 2, rows, BLOCK), jnp.bfloat16),
            jax.ShapeDtypeStruct(context.shape, jnp.bfloat16 if carry else jnp.float32),
        ],
        name="cross_attention",
    )(so, query_gradient, context, *carry)


def context_gradient(partial):
    half = lax.axis_index("tp") // 8
    width = BLOCK // 2
    low, high = partial[:, :, :width], partial[:, :, width:]
    first = jnp.where(half == 0, low, high)
    second = jnp.where(half == 0, high, low)
    place = lambda h, m, c: 8 * h + 2 * m + c
    coords = [(h, m, c) for h in range(2) for m in range(4) for c in range(2)]
    one = lax.ppermute(first, "tp", [(place(h, m, c), place(c, m, h)) for h, m, c in coords])
    two = lax.ppermute(second, "tp", [(place(h, m, c), place(c, m, 1 - h)) for h, m, c in coords])
    return (one.astype(jnp.float32) + two.astype(jnp.float32)).astype(jnp.bfloat16)[None]


def shards(llm_query, llm_kv, connector, self_query, self_key, latent_value, cotangent):
    return layer(llm_query, llm_kv, connector, self_query[0], self_key[0], latent_value[0], cotangent[0])


def layer(llm_query, llm_kv, connector, query, key, value, cotangent):
    near, far = [], []
    for s in range(SAMPLE_COUNT):
        near.append(exchange(to_blocks(key[s : s + 1], value[s : s + 1])))
        far.append(lax.ppermute(near[s], "tp", SWAP_HALF))
    columns = gather_run(connector)
    hidden = llm_hidden(llm_query, llm_kv)
    query_gradient = exchange(to_blocks(query, cotangent))
    context = context_tokens(gather_ring(hidden), columns)
    out, carry = [], ()
    for s in range(SAMPLE_COUNT):
        so = attention(s, query_gradient, near[s], far[s])
        result, partial = cross(s, so, query_gradient, context, carry)
        carry = (partial,)
        out.append(exchange(result))
    context_grad = context_gradient(partial)
    latent_out, self_grad = from_blocks(*out)
    return (latent_out[None], self_grad[None], context_grad)


def solution(mesh):
    placed = (
        P("fsdp", None, "tp"),
        P("fsdp", None, "tp", None),
        P("tp", "fsdp"),
        P("fsdp", None, "tp", None),
        P("fsdp", None, "tp", None),
        P("fsdp", None, "tp", None),
        P("fsdp", None, "tp", None),
    )
    return jax.shard_map(
        shards,
        mesh=mesh,
        in_specs=placed,
        out_specs=(
            P("fsdp", None, "tp", None),
            P("fsdp", None, "tp", None),
            P("fsdp", None, None, "tp"),
        ),
        check_vma=False,
    )
```

time: 710 us -> 330 us (0.46)
  the two profiles are of different devices: /device:TPU:8 before, /device:TPU:66 now
where the time goes in v1:
time: 330 us; the launch traced here: 327 us
  waiting for transfers between devices  150 us (45%)
  starting transfers between devices  115 us (35%)
  Pallas kernels  42.4 us (13%)
  local copies, waits for them, and re-layouts  11.7 us (4%)
  other arithmetic  4.11 us (1%)
    ppermute x1, waiting for transfers between devices, context_tokens(): there = lax.ppermute(mine, 'tp', SWAP_HALF)  76 us
    ppermute x2, waiting for transfers between devices, layer(): far.append(lax.ppermute(near[s], 'tp', SWAP_HALF))  38.8 us
    all_to_all x7, starting transfers between devices, exchange(): lax.all_to_all(x, 'tp', split_axis=0, concat_axis=0, axis_index_groups=HA...  34.3 us
    ppermute x3, starting transfers between devices, gather_run(): got = jnp.concatenate([got, lax.ppermute(got, 'fsdp', pairs)])  17.8 us
    all_to_all x7, waiting for transfers between devices, exchange(): lax.all_to_all(x, 'tp', split_axis=0, concat_axis=0, axis_index_groups=HA...  16.8 us
    pallas_call x3, Pallas kernels, to_blocks(): pl.pallas_call(copy_blocks, grid=(8,), in_specs=[pl.BlockSpec((x.shape[0]...  15.1 us
    ppermute x1, starting transfers between devices, llm_hidden(): take = lax.ppermute(give, 'tp', SWAP_HALF)  13.9 us
    pallas_call x2, Pallas kernels, attention(): pl.pallas_call(attention_kernel, grid=(3,), in_specs=[pl.BlockSpec((8, 1,...  12.8 us
  transfers between devices with their start and end apart: 21, of which 9 were waited for; matrix products, arithmetic and copies ran while one was open for 4% of the time, Pallas kernels for 11%

profile of v1, /device:TPU:66, one launch (start us, length us, event | category | flops | bytes accessed | tf_op | source)
XLA Modules:
  0.0 327.2 jit_solution(10297832788821825511)
XLA Ops:
  0.7 0.9 constant_dynamic-slice_fusion
  1.5 13.9 %collective-permute-start.1 = (bf16[2,20,512]{2,0,1:T(2,128)(2,1)S(1)}, bf16[2,20,512]{2,0,1:T(2,128)(2,1)S(1)}, u32[]{:S(2)}, u32[]{:S(2)}) collective-permute-start(bf16[2,20,512]{2,0,1:T(2,128)(2,1)S(1)} %get-tuple-element.30), channel_id=1, source_target_pairs={{0,8},{1,9},{2,10},{3,11},{4,12},{5,13},{6,14},{7,15},{8,0},{9,1},... | collective-permute-start | bytes 122888 | tf_op jit(solution)/shard_map/ppermute | solution.py:95
  15.5 4.4 %collective-permute-start.5 = (bf16[1,512,192]{1,2,0:T(8,128)(2,1)}, bf16[1,512,192]{1,2,0:T(8,128)(2,1)S(1)}, u32[]{:S(2)}, u32[]{:S(2)}) collective-permute-start(bf16[1,512,192]{1,2,0:T(8,128)(2,1)} %bitcast.60), channel_id=1, source_target_pairs={{0,64},{16,80},{32,96},{48,112},{64,0},{80,16},{96,32},{112,48},{1... | collective-permute-start | bytes 589832 | tf_op jit(solution)/shard_map/ppermute | solution.py:121
  19.9 2.5 slice_bitcast_fusion
  22.5 10.1 %collective-permute-done.5 = bf16[1,512,192]{1,2,0:T(8,128)(2,1)S(1)} collective-permute-done((bf16[1,512,192]{1,2,0:T(8,128)(2,1)}, bf16[1,512,192]{1,2,0:T(8,128)(2,1)S(1)}, u32[]{:S(2)}, u32[]{:S(2)}) %collective-permute-start.5) | collective-permute-done | bytes 196640 | tf_op jit(solution)/shard_map/ppermute | solution.py:121
  32.6 11.4 %collective-permute-start.6 = (bf16[2,512,192]{1,2,0:T(8,128)(2,1)S(1)}, bf16[2,512,192]{1,2,0:T(8,128)(2,1)S(1)}, u32[]{:S(2)}, u32[]{:S(2)}) collective-permute-start(bf16[2,512,192]{1,2,0:T(8,128)(2,1)S(1)} %pad_maximum_fusion.2), channel_id=1, source_target_pairs={{0,32},{16,48},{32,0},{48,16},{64,96},{80,112},{96,64},{112,80},{1... | collective-permute-start | bytes 1179656 | tf_op jit(solution)/shard_map/ppermute | solution.py:121
  44.1 4.8 %to_blocks.5 = bf16[8,2,64,384]{3,2,1,0:T(8,128)(2,1)} custom-call(bf16[1,64,3072]{2,1,0:T(8,128)(2,1)} %get-tuple-element.34.refs_0_, bf16[1,64,3072]{2,1,0:T(8,128)(2,1)} %get-tuple-element.17.refs_1_), custom_call_target="tpu_custom_call" | custom-call | tf_op jit(solution)/shard_map/to_blocks/pallas_call | solution.py:54
  49.8 4.8 %all-to-all-start.2 = ((bf16[8,2,2,20,128]{4,2,3,1,0:T(2,128)(2,1)}), bf16[8,2,2,20,128]{4,2,3,1,0:T(2,128)(2,1)S(1)}, u32[]{:S(2)}, u32[]{:S(2)}) async-start(bf16[8,2,2,20,128]{4,2,3,1,0:T(2,128)(2,1)} %bitcast.8), calls=%async_computation.2 | async-start | bytes 327680 | tf_op jit(solution)/shard_map/all_to_all | solution.py:86
  54.7 4.9 %all-to-all-done.2 = bf16[8,2,2,20,128]{4,2,3,1,0:T(2,128)(2,1)S(1)} async-done(((bf16[8,2,2,20,128]{4,2,3,1,0:T(2,128)(2,1)}), bf16[8,2,2,20,128]{4,2,3,1,0:T(2,128)(2,1)S(1)}, u32[]{:S(2)}, u32[]{:S(2)}) %all-to-all-start.2) | async-done | bytes 163872 | tf_op jit(solution)/shard_map/all_to_all | solution.py:86
  59.6 4.9 %all-to-all-start.5 = ((bf16[8,2,64,384]{3,2,1,0:T(8,128)(2,1)}), bf16[8,2,64,384]{3,2,1,0:T(8,128)(2,1)S(1)}, u32[]{:S(2)}, u32[]{:S(2)}) async-start(bf16[8,2,64,384]{3,2,1,0:T(8,128)(2,1)} %to_blocks.5), calls=%async_computation.5 | async-start | bytes 1572864 | tf_op jit(solution)/shard_map/all_to_all | solution.py:86
  64.6 1.9 collective-permute-start.7
  66.7 4.8 %to_blocks.4 = bf16[8,2,64,384]{3,2,1,0:T(8,128)(2,1)} custom-call(bf16[1,64,3072]{2,1,0:T(8,128)(2,1)} %get-tuple-element.33.refs_0_, bf16[1,64,3072]{2,1,0:T(8,128)(2,1)} %get-tuple-element.18.refs_1_), custom_call_target="tpu_custom_call" | custom-call | tf_op jit(solution)/shard_map/to_blocks/pallas_call | solution.py:54
  71.6 0.9 slice_reduce_fusion.1
  73.4 2.9 all-to-all-done.5.near_ref
  76.3 4.9 %all-to-all-start.1 = ((bf16[8,2,64,384]{3,2,1,0:T(8,128)(2,1)}), bf16[8,2,64,384]{3,2,1,0:T(8,128)(2,1)S(1)}, u32[]{:S(2)}, u32[]{:S(2)}) async-start(bf16[8,2,64,384]{3,2,1,0:T(8,128)(2,1)} %to_blocks.4), calls=%async_computation.1 | async-start | bytes 1572864 | tf_op jit(solution)/shard_map/all_to_all | solution.py:86
  81.2 1.6 convolution_convert_fusion
  82.7 0.9 reshape.110
  83.6 4.9 %collective-permute-start.4 = (bf16[64,512]{1,0:T(8,128)(2,1)S(1)}, bf16[64,512]{1,0:T(8,128)(2,1)S(1)}, u32[]{:S(2)}, u32[]{:S(2)}) collective-permute-start(bf16[64,512]{1,0:T(8,128)(2,1)S(1)} %reshape.110), channel_id=1, source_target_pairs={{0,384},{16,400},{32,416},{48,432},{64,448},{80,464},{96,480},{112... | collective-permute-start | bytes 196616 | tf_op jit(solution)/shard_map/ppermute | solution.py:129
  88.6 2.5 collective-permute-start.3
  91.1 2.4 collective-permute-start.2
  93.5 1.3 pad_maximum_fusion
  94.8 1.4 collective-permute-done.3
  96.2 1.0 collective-permute-done.2
  98.5 1.1 copy.17
  99.5 0.9 copy-done.2
  100.4 4.8 %all-to-all-start.3 = ((bf16[8,2,2,64,192]{4,3,2,1,0:T(8,128)(2,1)}), bf16[8,2,2,64,192]{4,3,2,1,0:T(8,128)(2,1)S(1)}, u32[]{:S(2)}, u32[]{:S(2)}) async-start(bf16[8,2,2,64,192]{4,3,2,1,0:T(8,128)(2,1)} %bitcast.59), calls=%async_computation.3 | async-start | bytes 2097152 | tf_op jit(solution)/shard_map/all_to_all | solution.py:86
  105.2 5.5 %to_blocks.3 = bf16[8,4,64,384]{3,2,1,0:T(8,128)(2,1)} custom-call(bf16[2,64,3072]{2,1,0:T(8,128)(2,1)} %bitcast.64, bf16[2,64,3072]{2,1,0:T(8,128)(2,1)} %bitcast.65), custom_call_target="tpu_custom_call" | custom-call | tf_op jit(solution)/shard_map/to_blocks/pallas_call | solution.py:54
  110.8 9.0 %all-to-all-done.3 = bf16[8,2,2,64,192]{4,3,2,1,0:T(8,128)(2,1)S(1)} async-done(((bf16[8,2,2,64,192]{4,3,2,1,0:T(8,128)(2,1)}), bf16[8,2,2,64,192]{4,3,2,1,0:T(8,128)(2,1)S(1)}, u32[]{:S(2)}, u32[]{:S(2)}) %all-to-all-start.3) | async-done | bytes 786464 | tf_op jit(solution)/shard_map/all_to_all | solution.py:86
  119.7 5.0 %all-to-all-start = ((bf16[8,4,64,384]{3,2,1,0:T(8,128)(2,1)}), bf16[8,4,64,384]{3,2,1,0:T(8,128)(2,1)S(1)}, u32[]{:S(2)}, u32[]{:S(2)}) async-start(bf16[8,4,64,384]{3,2,1,0:T(8,128)(2,1)} %to_blocks.3), calls=%async_computation | async-start | bytes 3145728 | tf_op jit(solution)/shard_map/all_to_all | solution.py:86
  124.7 4.8 %collective-permute-start = (bf16[8,2,64,384]{3,2,1,0:T(8,128)(2,1)}, bf16[8,2,64,384]{3,2,1,0:T(8,128)(2,1)}, u32[]{:S(2)}, u32[]{:S(2)}) collective-permute-start(bf16[8,2,64,384]{3,2,1,0:T(8,128)(2,1)} %copy-done.2), channel_id=1, source_target_pairs={{0,8},{1,9},{2,10},{3,11},{4,12},{5,13},{6,14},{7,15},{8,0},{9,1},... | collective-permute-start | bytes 2359304 | tf_op jit(solution)/shard_map/ppermute | solution.py:279
  129.7 9.8 %collective-permute-start.8 = (bf16[2,2,64,192]{3,2,1,0:T(8,128)(2,1)S(1)}, bf16[2,2,64,192]{3,2,1,0:T(8,128)(2,1)S(1)}, u32[]{:S(2)}, u32[]{:S(2)}) collective-permute-start(bf16[2,2,64,192]{3,2,1,0:T(8,128)(2,1)S(1)} %reduce_sum.22), channel_id=1, source_target_pairs={{0,8},{1,9},{2,10},{3,11},{4,12},{5,13},{6,14},{7,15},{8,0},{9,1},... | collective-permute-start | bytes 294920 | tf_op jit(solution)/shard_map/ppermute | solution.py:142
  139.4 76.0 %collective-permute-done.8 = bf16[2,2,64,192]{3,2,1,0:T(8,128)(2,1)S(1)} collective-permute-done((bf16[2,2,64,192]{3,2,1,0:T(8,128)(2,1)S(1)}, bf16[2,2,64,192]{3,2,1,0:T(8,128)(2,1)S(1)}, u32[]{:S(2)}, u32[]{:S(2)}) %collective-permute-start.8) | collective-permute-done | bytes 98336 | tf_op jit(solution)/shard_map/ppermute | solution.py:142
  215.5 2.2 collective-permute-start.9
  217.7 5.9 %collective-permute-start.10 = (bf16[2,64,192]{2,1,0:T(8,128)(2,1)S(1)}, bf16[2,64,192]{2,1,0:T(8,128)(2,1)S(1)}, u32[]{:S(2)}, u32[]{:S(2)}) collective-permute-start(bf16[2,64,192]{2,1,0:T(8,128)(2,1)S(1)} %get-tuple-element.26), channel_id=1, source_target_pairs={{0,256},{1,384},{2,258},{3,386},{4,260},{5,388},{6,262},{7,390},{8... | collective-permute-start | bytes 147464 | tf_op jit(solution)/shard_map/ppermute | solution.py:147
  223.7 6.5 %collective-permute-start.11 = (bf16[8,2,64,384]{3,2,1,0:T(8,128)(2,1)S(1)}, bf16[8,2,64,384]{3,2,1,0:T(8,128)(2,1)S(1)}, u32[]{:S(2)}, u32[]{:S(2)}) collective-permute-start(bf16[8,2,64,384]{3,2,1,0:T(8,128)(2,1)S(1)} %all-to-all-done.5.near_ref), channel_id=1, source_target_pairs={{0,8},{1,9},{2,10},{3,11},{4,12},{5,13},{6,14},{7,15},{8,0},{9,1},... | collective-permute-start | bytes 2359304 | tf_op jit(solution)/shard_map/ppermute | solution.py:279
  230.2 1.2 copy-done
  231.3 6.4 %latent_attention.2.so_ref = bf16[8,64,384]{2,1,0:T(8,128)(2,1)} custom-call(bf16[8,4,64,384]{3,2,1,0:T(8,128)(2,1)} %copy-done, bf16[8,2,64,384]{3,2,1,0:T(8,128)(2,1)} %copy-done.2, bf16[8,2,64,384]{3,2,1,0:T(8,128)(2,1)} %collective-permute-done.far_ref), custom_call_target="tpu_custom_call" | custom-call | tf_op jit(solution)/shard_map/latent_attention/pallas_call | solution.py:181
  238.5 4.5 %cross_attention.2 = (bf16[8,2,64,384]{3,2,1,0:T(8,128)(2,1)}, f32[2,64,384]{2,1,0:T(8,128)}) custom-call(bf16[8,64,384]{2,1,0:T(8,128)(2,1)} %latent_attention.2.so_ref, bf16[8,4,64,384]{3,2,1,0:T(8,128)(2,1)} %copy-done, bf16[2,64,384]{2,1,0:T(8,128)(2,1)} %pad_maximum_fusion.3.context_ref), custom_call_target="tpu_custom_call" | custom-call | tf_op jit(solution)/shard_map/cross_attention/pallas_call | solution.py:240
  243.0 4.9 %all-to-all-start.4 = ((bf16[8,2,64,384]{3,2,1,0:T(8,128)(2,1)}), bf16[8,2,64,384]{3,2,1,0:T(8,128)(2,1)S(1)}, u32[]{:S(2)}, u32[]{:S(2)}) async-start(bf16[8,2,64,384]{3,2,1,0:T(8,128)(2,1)} %get-tuple-element.9), calls=%async_computation.4 | async-start | bytes 1572864 | tf_op jit(solution)/shard_map/all_to_all | solution.py:86
  247.9 38.8 %collective-permute-done.11.far_ref = bf16[8,2,64,384]{3,2,1,0:T(8,128)(2,1)S(1)} collective-permute-done((bf16[8,2,64,384]{3,2,1,0:T(8,128)(2,1)S(1)}, bf16[8,2,64,384]{3,2,1,0:T(8,128)(2,1)S(1)}, u32[]{:S(2)}, u32[]{:S(2)}) %collective-permute-start.11) | collective-permute-done | bytes 786464 | tf_op jit(solution)/shard_map/ppermute | solution.py:279
  286.7 0.9 copy-done.6
  287.6 6.4 %latent_attention.3.so_ref = bf16[8,64,384]{2,1,0:T(8,128)(2,1)} custom-call(bf16[8,4,64,384]{3,2,1,0:T(8,128)(2,1)} %copy-done, bf16[8,2,64,384]{3,2,1,0:T(8,128)(2,1)} %copy-done.1, bf16[8,2,64,384]{3,2,1,0:T(8,128)(2,1)} %copy-done.6), custom_call_target="tpu_custom_call" | custom-call | tf_op jit(solution)/shard_map/latent_attention/pallas_call | solution.py:181
  294.0 4.5 %cross_attention.3 = (bf16[8,2,64,384]{3,2,1,0:T(8,128)(2,1)}, bf16[2,64,384]{2,1,0:T(8,128)(2,1)}) custom-call(bf16[8,64,384]{2,1,0:T(8,128)(2,1)} %latent_attention.3.so_ref, bf16[8,4,64,384]{3,2,1,0:T(8,128)(2,1)} %copy-done, bf16[2,64,384]{2,1,0:T(8,128)(2,1)} %pad_maximum_fusion.3.context_ref, f32[2,64,384]{2,1,0:T(8,128)} %get-tuple-element.10.refs_0_), custom_call_target="tpu_custom_call" | custom-call | tf_op jit(solution)/shard_map/cross_attention/pallas_call | solution.py:240
  298.5 5.0 %all-to-all-start.6 = ((bf16[8,2,64,384]{3,2,1,0:T(8,128)(2,1)}), bf16[8,2,64,384]{3,2,1,0:T(8,128)(2,1)S(1)}, u32[]{:S(2)}, u32[]{:S(2)}) async-start(bf16[8,2,64,384]{3,2,1,0:T(8,128)(2,1)} %get-tuple-element.11), calls=%async_computation.6 | async-start | bytes 1572864 | tf_op jit(solution)/shard_map/all_to_all | solution.py:86
  304.3 9.5 %collective-permute-start.13 = (bf16[2,64,192]{2,1,0:T(8,128)(2,1)S(1)}, bf16[2,64,192]{2,1,0:T(8,128)(2,1)S(1)}, u32[]{:S(2)}, u32[]{:S(2)}) collective-permute-start(bf16[2,64,192]{2,1,0:T(8,128)(2,1)S(1)} %get-tuple-element.28), channel_id=1, source_target_pairs={{0,1},{1,9},{2,3},{3,11},{4,5},{5,13},{6,7},{7,15},{8,0},{9,8},{10... | collective-permute-start | bytes 147464 | tf_op jit(solution)/shard_map/ppermute | solution.py:267
  313.8 6.3 %collective-permute-done.13 = bf16[2,64,192]{2,1,0:T(8,128)(2,1)S(1)} collective-permute-done((bf16[2,64,192]{2,1,0:T(8,128)(2,1)S(1)}, bf16[2,64,192]{2,1,0:T(8,128)(2,1)S(1)}, u32[]{:S(2)}, u32[]{:S(2)}) %collective-permute-start.13) | collective-permute-done | bytes 49184 | tf_op jit(solution)/shard_map/ppermute | solution.py:267
  320.8 0.9 copy-done.4
  321.7 5.5 %from_blocks.1 = (bf16[2,64,3072]{2,1,0:T(8,128)(2,1)}, bf16[2,64,3072]{2,1,0:T(8,128)(2,1)}) custom-call(bf16[8,2,64,384]{3,2,1,0:T(8,128)(2,1)} %copy-done.3, bf16[8,2,64,384]{3,2,1,0:T(8,128)(2,1)} %copy-done.4), custom_call_target="tpu_custom_call" | custom-call | tf_op jit(solution)/shard_map/from_blocks/pallas_call | solution.py:75
  (57 shorter events, 6.0 us)
Async XLA Ops:
  1.5 47.4 %collective-permute-start.1 = (bf16[2,20,512]{2,0,1:T(2,128)(2,1)S(1)}, bf16[2,20,512]{2,0,1:T(2,128)(2,1)S(1)}, u32[]{:S(2)}, u32[]{:S(2)}) collective-permute-start(bf16[2,20,512]{2,0,1:T(2,128)(2,1)S(1)} %get-tuple-element.30), channel_id=1, source_target_pairs={{0,8},{1,9},{2,10},{3,11},{4,12},{5,13},{6,14},{7,15},{8,0},{9,1},... | collective-permute-start | bytes 122888 | tf_op jit(solution)/shard_map/ppermute | solution.py:95
  15.5 17.1 %copy-start.5 = (bf16[512,192]{0,1:T(8,128)(2,1)S(1)}, bf16[512,192]{0,1:T(8,128)(2,1)}, u32[]{:S(2)}) copy-start(bf16[512,192]{0,1:T(8,128)(2,1)} %param.9) | copy-start | bytes 589828
  15.5 17.1 %collective-permute-start.5 = (bf16[1,512,192]{1,2,0:T(8,128)(2,1)}, bf16[1,512,192]{1,2,0:T(8,128)(2,1)S(1)}, u32[]{:S(2)}, u32[]{:S(2)}) collective-permute-start(bf16[1,512,192]{1,2,0:T(8,128)(2,1)} %bitcast.60), channel_id=1, source_target_pairs={{0,64},{16,80},{32,96},{48,112},{64,0},{80,16},{96,32},{112,48},{1... | collective-permute-start | bytes 589832 | tf_op jit(solution)/shard_map/ppermute | solution.py:121
  32.6 32.0 %collective-permute-start.6 = (bf16[2,512,192]{1,2,0:T(8,128)(2,1)S(1)}, bf16[2,512,192]{1,2,0:T(8,128)(2,1)S(1)}, u32[]{:S(2)}, u32[]{:S(2)}) collective-permute-start(bf16[2,512,192]{1,2,0:T(8,128)(2,1)S(1)} %pad_maximum_fusion.2), channel_id=1, source_target_pairs={{0,32},{16,48},{32,0},{48,16},{64,96},{80,112},{96,64},{112,80},{1... | collective-permute-start | bytes 1179656 | tf_op jit(solution)/shard_map/ppermute | solution.py:121
  49.8 9.8 %all-to-all-start.2 = ((bf16[8,2,2,20,128]{4,2,3,1,0:T(2,128)(2,1)}), bf16[8,2,2,20,128]{4,2,3,1,0:T(2,128)(2,1)S(1)}, u32[]{:S(2)}, u32[]{:S(2)}) async-start(bf16[8,2,2,20,128]{4,2,3,1,0:T(2,128)(2,1)} %bitcast.8), calls=%async_computation.2 | async-start | bytes 327680 | tf_op jit(solution)/shard_map/all_to_all | solution.py:86
  54.7 12.0 %copy-start.8 = (bf16[1,64,512]{2,1,0:T(8,128)(2,1)S(1)}, bf16[1,64,512]{2,1,0:T(8,128)(2,1)}, u32[]{:S(2)}) copy-start(bf16[1,64,512]{2,1,0:T(8,128)(2,1)} %param.7) | copy-start | bytes 196612
  59.6 16.6 %all-to-all-start.5 = ((bf16[8,2,64,384]{3,2,1,0:T(8,128)(2,1)}), bf16[8,2,64,384]{3,2,1,0:T(8,128)(2,1)S(1)}, u32[]{:S(2)}, u32[]{:S(2)}) async-start(bf16[8,2,64,384]{3,2,1,0:T(8,128)(2,1)} %to_blocks.5), calls=%async_computation.5 | async-start | bytes 1572864 | tf_op jit(solution)/shard_map/all_to_all | solution.py:86
  64.6 28.8 %collective-permute-start.7 = (bf16[4,512,192]{1,2,0:T(8,128)(2,1)S(1)}, bf16[4,512,192]{1,2,0:T(8,128)(2,1)}, u32[]{:S(2)}, u32[]{:S(2)}) collective-permute-start(bf16[4,512,192]{1,2,0:T(8,128)(2,1)S(1)} %pad_maximum_fusion.1), channel_id=1, source_target_pairs={{0,16},{16,0},{32,48},{48,32},{64,80},{80,64},{96,112},{112,96},{1... | collective-permute-start | bytes 2359304 | tf_op jit(solution)/shard_map/ppermute | solution.py:121
  72.7 3.6 %copy-start.9 = (f32[256]{0:T(256)}, f32[256]{0:T(256)S(1)}, u32[]{:S(2)}) copy-start(f32[256]{0:T(256)S(1)} %get-tuple-element.31) | copy-start | bytes 3076
  76.3 147.4 %copy-start.1 = (bf16[8,2,64,384]{3,2,1,0:T(8,128)(2,1)}, bf16[8,2,64,384]{3,2,1,0:T(8,128)(2,1)S(1)}, u32[]{:S(2)}) copy-start(bf16[8,2,64,384]{3,2,1,0:T(8,128)(2,1)S(1)} %all-to-all-done.5.near_ref) | copy-start | bytes 2359300
  76.3 23.3 %all-to-all-start.1 = ((bf16[8,2,64,384]{3,2,1,0:T(8,128)(2,1)}), bf16[8,2,64,384]{3,2,1,0:T(8,128)(2,1)S(1)}, u32[]{:S(2)}, u32[]{:S(2)}) async-start(bf16[8,2,64,384]{3,2,1,0:T(8,128)(2,1)} %to_blocks.4), calls=%async_computation.1 | async-start | bytes 1572864 | tf_op jit(solution)/shard_map/all_to_all | solution.py:86
  83.6 11.1 %collective-permute-start.4 = (bf16[64,512]{1,0:T(8,128)(2,1)S(1)}, bf16[64,512]{1,0:T(8,128)(2,1)S(1)}, u32[]{:S(2)}, u32[]{:S(2)}) collective-permute-start(bf16[64,512]{1,0:T(8,128)(2,1)S(1)} %reshape.110), channel_id=1, source_target_pairs={{0,384},{16,400},{32,416},{48,432},{64,448},{80,464},{96,480},{112... | collective-permute-start | bytes 196616 | tf_op jit(solution)/shard_map/ppermute | solution.py:129
  88.6 7.7 %collective-permute-start.3 = (bf16[64,512]{1,0:T(8,128)(2,1)S(1)}, bf16[64,512]{1,0:T(8,128)(2,1)S(1)}, u32[]{:S(2)}, u32[]{:S(2)}) collective-permute-start(bf16[64,512]{1,0:T(8,128)(2,1)S(1)} %reshape.110), channel_id=1, source_target_pairs={{0,256},{16,272},{32,288},{48,304},{64,320},{80,336},{96,352},{112... | collective-permute-start | bytes 196616 | tf_op jit(solution)/shard_map/ppermute | solution.py:129
  91.1 6.2 %collective-permute-start.2 = (bf16[64,512]{1,0:T(8,128)(2,1)S(1)}, bf16[64,512]{1,0:T(8,128)(2,1)S(1)}, u32[]{:S(2)}, u32[]{:S(2)}) collective-permute-start(bf16[64,512]{1,0:T(8,128)(2,1)S(1)} %reshape.110), channel_id=1, source_target_pairs={{0,128},{16,144},{32,160},{48,176},{64,192},{80,208},{96,224},{112... | collective-permute-start | bytes 196616 | tf_op jit(solution)/shard_map/ppermute | solution.py:129
  99.5 0.9 copy-start.2
  100.4 19.3 %all-to-all-start.3 = ((bf16[8,2,2,64,192]{4,3,2,1,0:T(8,128)(2,1)}), bf16[8,2,2,64,192]{4,3,2,1,0:T(8,128)(2,1)S(1)}, u32[]{:S(2)}, u32[]{:S(2)}) async-start(bf16[8,2,2,64,192]{4,3,2,1,0:T(8,128)(2,1)} %bitcast.59), calls=%async_computation.3 | async-start | bytes 2097152 | tf_op jit(solution)/shard_map/all_to_all | solution.py:86
  119.7 110.4 %all-to-all-start = ((bf16[8,4,64,384]{3,2,1,0:T(8,128)(2,1)}), bf16[8,4,64,384]{3,2,1,0:T(8,128)(2,1)S(1)}, u32[]{:S(2)}, u32[]{:S(2)}) async-start(bf16[8,4,64,384]{3,2,1,0:T(8,128)(2,1)} %to_blocks.3), calls=%async_computation | async-start | bytes 3145728 | tf_op jit(solution)/shard_map/all_to_all | solution.py:86
  124.7 105.5 %collective-permute-start = (bf16[8,2,64,384]{3,2,1,0:T(8,128)(2,1)}, bf16[8,2,64,384]{3,2,1,0:T(8,128)(2,1)}, u32[]{:S(2)}, u32[]{:S(2)}) collective-permute-start(bf16[8,2,64,384]{3,2,1,0:T(8,128)(2,1)} %copy-done.2), channel_id=1, source_target_pairs={{0,8},{1,9},{2,10},{3,11},{4,12},{5,13},{6,14},{7,15},{8,0},{9,1},... | collective-permute-start | bytes 2359304 | tf_op jit(solution)/shard_map/ppermute | solution.py:279
  129.7 85.8 %collective-permute-start.8 = (bf16[2,2,64,192]{3,2,1,0:T(8,128)(2,1)S(1)}, bf16[2,2,64,192]{3,2,1,0:T(8,128)(2,1)S(1)}, u32[]{:S(2)}, u32[]{:S(2)}) collective-permute-start(bf16[2,2,64,192]{3,2,1,0:T(8,128)(2,1)S(1)} %reduce_sum.22), channel_id=1, source_target_pairs={{0,8},{1,9},{2,10},{3,11},{4,12},{5,13},{6,14},{7,15},{8,0},{9,1},... | collective-permute-start | bytes 294920 | tf_op jit(solution)/shard_map/ppermute | solution.py:142
  215.5 22.3 %collective-permute-start.9 = (bf16[2,64,192]{2,1,0:T(8,128)(2,1)S(1)}, bf16[2,64,192]{2,1,0:T(8,128)(2,1)S(1)}, u32[]{:S(2)}, u32[]{:S(2)}) collective-permute-start(bf16[2,64,192]{2,1,0:T(8,128)(2,1)S(1)} %get-tuple-element.25), channel_id=1, source_target_pairs={{0,0},{1,128},{2,2},{3,130},{4,4},{5,132},{6,6},{7,134},{8,8},{9,1... | collective-permute-start | bytes 147464 | tf_op jit(solution)/shard_map/ppermute | solution.py:147
  217.7 20.1 %collective-permute-start.10 = (bf16[2,64,192]{2,1,0:T(8,128)(2,1)S(1)}, bf16[2,64,192]{2,1,0:T(8,128)(2,1)S(1)}, u32[]{:S(2)}, u32[]{:S(2)}) collective-permute-start(bf16[2,64,192]{2,1,0:T(8,128)(2,1)S(1)} %get-tuple-element.26), channel_id=1, source_target_pairs={{0,256},{1,384},{2,258},{3,386},{4,260},{5,388},{6,262},{7,390},{8... | collective-permute-start | bytes 147464 | tf_op jit(solution)/shard_map/ppermute | solution.py:147
  223.7 63.0 %collective-permute-start.11 = (bf16[8,2,64,384]{3,2,1,0:T(8,128)(2,1)S(1)}, bf16[8,2,64,384]{3,2,1,0:T(8,128)(2,1)S(1)}, u32[]{:S(2)}, u32[]{:S(2)}) collective-permute-start(bf16[8,2,64,384]{3,2,1,0:T(8,128)(2,1)S(1)} %all-to-all-done.5.near_ref), channel_id=1, source_target_pairs={{0,8},{1,9},{2,10},{3,11},{4,12},{5,13},{6,14},{7,15},{8,0},{9,1},... | collective-permute-start | bytes 2359304 | tf_op jit(solution)/shard_map/ppermute | solution.py:279
  230.1 1.2 copy-start
  243.0 55.5 %all-to-all-start.4 = ((bf16[8,2,64,384]{3,2,1,0:T(8,128)(2,1)}), bf16[8,2,64,384]{3,2,1,0:T(8,128)(2,1)S(1)}, u32[]{:S(2)}, u32[]{:S(2)}) async-start(bf16[8,2,64,384]{3,2,1,0:T(8,128)(2,1)} %get-tuple-element.9), calls=%async_computation.4 | async-start | bytes 1572864 | tf_op jit(solution)/shard_map/all_to_all | solution.py:86
  286.7 0.9 copy-start.6
  298.5 5.0 %copy-start.7 = (bf16[2,64,384]{2,1,0:T(8,128)(2,1)S(1)}, bf16[2,64,384]{2,1,0:T(8,128)(2,1)}, u32[]{:S(2)}) copy-start(bf16[2,64,384]{2,1,0:T(8,128)(2,1)} %get-tuple-element.14) | copy-start | bytes 294916
  298.5 22.2 %copy-start.3 = (bf16[8,2,64,384]{3,2,1,0:T(8,128)(2,1)}, bf16[8,2,64,384]{3,2,1,0:T(8,128)(2,1)S(1)}, u32[]{:S(2)}) copy-start(bf16[8,2,64,384]{3,2,1,0:T(8,128)(2,1)S(1)} %all-to-all-done.4.x_ref) | copy-start | bytes 2359300
  298.5 22.2 %all-to-all-start.6 = ((bf16[8,2,64,384]{3,2,1,0:T(8,128)(2,1)}), bf16[8,2,64,384]{3,2,1,0:T(8,128)(2,1)S(1)}, u32[]{:S(2)}, u32[]{:S(2)}) async-start(bf16[8,2,64,384]{3,2,1,0:T(8,128)(2,1)} %get-tuple-element.11), calls=%async_computation.6 | async-start | bytes 1572864 | tf_op jit(solution)/shard_map/all_to_all | solution.py:86
  303.6 10.2 %collective-permute-start.12 = (bf16[2,64,192]{2,1,0:T(8,128)(2,1)S(1)}, bf16[2,64,192]{2,1,0:T(8,128)(2,1)S(1)}, u32[]{:S(2)}, u32[]{:S(2)}) collective-permute-start(bf16[2,64,192]{2,1,0:T(8,128)(2,1)S(1)} %get-tuple-element.27), channel_id=1, source_target_pairs={{0,0},{1,8},{2,2},{3,10},{4,4},{5,12},{6,6},{7,14},{8,1},{9,9},{10... | collective-permute-start | bytes 147464 | tf_op jit(solution)/shard_map/ppermute | solution.py:266
  304.3 15.8 %collective-permute-start.13 = (bf16[2,64,192]{2,1,0:T(8,128)(2,1)S(1)}, bf16[2,64,192]{2,1,0:T(8,128)(2,1)S(1)}, u32[]{:S(2)}, u32[]{:S(2)}) collective-permute-start(bf16[2,64,192]{2,1,0:T(8,128)(2,1)S(1)} %get-tuple-element.28), channel_id=1, source_target_pairs={{0,1},{1,9},{2,3},{3,11},{4,5},{5,13},{6,7},{7,15},{8,0},{9,8},{10... | collective-permute-start | bytes 147464 | tf_op jit(solution)/shard_map/ppermute | solution.py:267
  320.8 0.9 copy-start.4

commit v2 on v1

--- a/solution.py
+++ b/solution.py
@@ -35,51 +35,48 @@
     return pairs
 
 
-def head_block(j):
-    return 4 * (j % 2) + j // 2
-
-
 def copy_blocks(*refs):
     *x_refs, o_ref = refs
     at = 0
     for x_ref in x_refs:
         count = x_ref.shape[0]
-        o_ref[0, at : at + count] = x_ref[...]
+        for m in range(4):
+            o_ref[m, 0, at : at + count] = x_ref[:, :, BLOCK * m : BLOCK * (m + 1)]
         at += count
 
 
-def to_blocks(*parts):
+def to_blocks(first, count, *parts):
     rows = parts[0].shape[1]
-    count = sum(x.shape[0] for x in parts)
-    return pl.pallas_call(
+    total = count * len(parts)
+    out = pl.pallas_call(
         copy_blocks,
-        grid=(8,),
-        in_specs=[pl.BlockSpec((x.shape[0], rows, BLOCK), lambda j: (0, 0, head_block(j))) for x in parts],
-        out_specs=pl.BlockSpec((1, count, rows, BLOCK), lambda j: (j, 0, 0, 0)),
-        out_shape=jax.ShapeDtypeStruct((8, count, rows, BLOCK), parts[0].dtype),
+        grid=(2,),
+        in_specs=[pl.BlockSpec((count, rows, 4 * BLOCK), lambda c: (first, 0, c))] * len(parts),
+        out_specs=pl.BlockSpec((4, 1, total, rows, BLOCK), lambda c: (0, c, 0, 0, 0)),
+        out_shape=jax.ShapeDtypeStruct((4, 2, total, rows, BLOCK), parts[0].dtype),
         name="to_blocks",
     )(*parts)
-
-
-def copy_rows(x_ref, y_ref, a_ref, b_ref):
-    a_ref[0] = x_ref[0, 0]
-    a_ref[1] = y_ref[0, 0]
-    b_ref[0] = x_ref[0, 1]
-    b_ref[1] = y_ref[0, 1]
-
-
-def from_blocks(x, y):
-    rows = x.shape[2]
-    in_spec = pl.BlockSpec((1, 2, rows, BLOCK), lambda j: (j, 0, 0, 0))
-    out_spec = pl.BlockSpec((SAMPLE_COUNT, rows, BLOCK), lambda j: (0, 0, head_block(j)))
+    return out.reshape(8, total, rows, BLOCK)
+
+
+def copy_rows(*refs):
+    *in_refs, a_ref, b_ref = refs
+    for s, x_ref in enumerate(in_refs):
+        for m in range(4):
+            a_ref[s, :, BLOCK * m : BLOCK * (m + 1)] = x_ref[m, 0, 0]
+            b_ref[s, :, BLOCK * m : BLOCK * (m + 1)] = x_ref[m, 0, 1]
+
+
+def from_blocks(*parts):
+    rows = parts[0].shape[2]
     return pl.pallas_call(
         copy_rows,
-        grid=(8,),
-        in_specs=[in_spec] * 2,
-        out_specs=[out_spec] * 2,
-        out_shape=[jax.ShapeDtypeStruct((SAMPLE_COUNT, rows, 8 * BLOCK), x.dtype)] * 2,
+        grid=(2,),
+        in_specs=[pl.BlockSpec((4, 1, 2, rows, BLOCK), lambda c: (0, c, 0, 0, 0))] * SAMPLE_COUNT,
+        out_specs=[pl.BlockSpec((SAMPLE_COUNT, rows, 4 * BLOCK), lambda c: (0, 0, c))] * 2,
+        out_shape=[jax.ShapeDtypeStruct((SAMPLE_COUNT, rows, 8 * BLOCK), parts[0].dtype)] * 2,
         name="from_blocks",
-    )(x, y)
+    )(*(x.reshape(4, 2, 2, rows, BLOCK) for x in parts))
 
 
 def exchange(x):
@@ -275,11 +272,11 @@
 def layer(llm_query, llm_kv, connector, query, key, value, cotangent):
     near, far = [], []
     for s in range(SAMPLE_COUNT):
-        near.append(exchange(to_blocks(key[s : s + 1], value[s : s + 1])))
+        near.append(exchange(to_blocks(s, 1, key, value)))
         far.append(lax.ppermute(near[s], "tp", SWAP_HALF))
     columns = gather_run(connector)
     hidden = llm_hidden(llm_query, llm_kv)
-    query_gradient = exchange(to_blocks(query, cotangent))
+    query_gradient = exchange(to_blocks(0, 2, query, cotangent))
     context = context_tokens(gather_ring(hidden), columns)
     out, carry = [], ()
     for s in range(SAMPLE_COUNT):

time: 330 us -> 348 us (1.055)
  the two profiles are of different devices: /device:TPU:66 before, /device:TPU:178 now
where the time goes in v2:
time: 348 us; the launch traced here: 347 us
  waiting for transfers between devices  168 us (48%)
  starting transfers between devices  115 us (33%)
  Pallas kernels  30.6 us (9%)
  blocking collectives  16.8 us (5%)
  local copies, waits for them, and re-layouts  8.26 us (2%)
  other arithmetic  5.06 us (1%)
    ppermute x1, waiting for transfers between devices, context_tokens(): there = lax.ppermute(mine, 'tp', SWAP_HALF)  135 us
    all_to_all x6, starting transfers between devices, exchange(): lax.all_to_all(x, 'tp', split_axis=0, concat_axis=0, axis_index_groups=HA...  29.3 us
    all_to_all x6, waiting for transfers between devices, exchange(): lax.all_to_all(x, 'tp', split_axis=0, concat_axis=0, axis_index_groups=HA...  22.6 us
    ppermute x3, starting transfers between devices, gather_run(): got = jnp.concatenate([got, lax.ppermute(got, 'fsdp', pairs)])  19.5 us
    all_to_all x1, blocking collectives, exchange(): lax.all_to_all(x, 'tp', split_axis=0, concat_axis=0, axis_index_groups=HA...  16.8 us
    ppermute x2, starting transfers between devices, layer(): far.append(lax.ppermute(near[s], 'tp', SWAP_HALF))  14.5 us
    ppermute x1, starting transfers between devices, llm_hidden(): take = lax.ppermute(give, 'tp', SWAP_HALF)  13.6 us
    pallas_call x2, Pallas kernels, attention(): pl.pallas_call(attention_kernel, grid=(3,), in_specs=[pl.BlockSpec((8, 1,...  12.8 us
  transfers between devices with their start and end apart: 20, of which 8 were waited for; matrix products, arithmetic and copies ran while one was open for 3% of the time, Pallas kernels for 6%

profile of v2, /device:TPU:178, one launch (start us, length us, event | category | flops | bytes accessed | tf_op | source)
XLA Modules:
  0.0 346.8 jit_solution(16315716565296007829)
XLA Ops:
  0.6 1.9 collective-permute-start.5
  2.6 0.9 constant_dynamic-slice_fusion
  3.5 13.6 %collective-permute-start.1 = (bf16[2,20,512]{2,0,1:T(2,128)(2,1)S(1)}, bf16[2,20,512]{2,0,1:T(2,128)(2,1)S(1)}, u32[]{:S(2)}, u32[]{:S(2)}) collective-permute-start(bf16[2,20,512]{2,0,1:T(2,128)(2,1)S(1)} %get-tuple-element.26), channel_id=1, source_target_pairs={{0,8},{1,9},{2,10},{3,11},{4,12},{5,13},{6,14},{7,15},{8,0},{9,1},... | collective-permute-start | bytes 122888 | tf_op jit(solution)/shard_map/ppermute | solution.py:92
  17.7 1.0 pad_maximum_fusion.2
  18.6 15.6 %collective-permute-start.6 = (bf16[2,512,192]{1,2,0:T(8,128)(2,1)S(1)}, bf16[2,512,192]{1,2,0:T(8,128)(2,1)S(1)}, u32[]{:S(2)}, u32[]{:S(2)}) collective-permute-start(bf16[2,512,192]{1,2,0:T(8,128)(2,1)S(1)} %pad_maximum_fusion.2), channel_id=1, source_target_pairs={{0,32},{16,48},{32,0},{48,16},{64,96},{80,112},{96,64},{112,80},{1... | collective-permute-start | bytes 1179656 | tf_op jit(solution)/shard_map/ppermute | solution.py:118
  34.3 2.0 to_blocks.4
  36.5 0.8 broadcast_in_dim.14
  37.2 4.8 %all-to-all-start.2 = ((bf16[8,2,2,20,128]{4,2,3,1,0:T(2,128)(2,1)}), bf16[8,2,2,20,128]{4,2,3,1,0:T(2,128)(2,1)S(1)}, u32[]{:S(2)}, u32[]{:S(2)}) async-start(bf16[8,2,2,20,128]{4,2,3,1,0:T(2,128)(2,1)} %bitcast.10), calls=%async_computation.2 | async-start | bytes 327680 | tf_op jit(solution)/shard_map/all_to_all | solution.py:83
  42.1 4.9 %all-to-all-done.2 = bf16[8,2,2,20,128]{4,2,3,1,0:T(2,128)(2,1)S(1)} async-done(((bf16[8,2,2,20,128]{4,2,3,1,0:T(2,128)(2,1)}), bf16[8,2,2,20,128]{4,2,3,1,0:T(2,128)(2,1)S(1)}, u32[]{:S(2)}, u32[]{:S(2)}) %all-to-all-start.2) | async-done | bytes 163872 | tf_op jit(solution)/shard_map/all_to_all | solution.py:83
  47.1 4.9 %all-to-all-start.1 = ((bf16[8,2,64,384]{3,2,1,0:T(8,128)(2,1)}), bf16[8,2,64,384]{3,2,1,0:T(8,128)(2,1)S(1)}, u32[]{:S(2)}, u32[]{:S(2)}) async-start(bf16[8,2,64,384]{3,2,1,0:T(8,128)(2,1)} %bitcast.62), calls=%async_computation.1 | async-start | bytes 1572864 | tf_op jit(solution)/shard_map/all_to_all | solution.py:83
  52.1 2.1 collective-permute-start.7
  54.2 2.0 to_blocks.5
  56.3 0.9 slice_reduce_fusion.1
  57.5 0.7 fusion.2
  58.2 5.5 %all-to-all-done.1.near_ref = bf16[8,2,64,384]{3,2,1,0:T(8,128)(2,1)S(1)} async-done(((bf16[8,2,64,384]{3,2,1,0:T(8,128)(2,1)}), bf16[8,2,64,384]{3,2,1,0:T(8,128)(2,1)S(1)}, u32[]{:S(2)}, u32[]{:S(2)}) %all-to-all-start.1) | async-done | bytes 786464 | tf_op jit(solution)/shard_map/all_to_all | solution.py:83
  63.7 4.9 %all-to-all-start.5 = ((bf16[8,2,64,384]{3,2,1,0:T(8,128)(2,1)}), bf16[8,2,64,384]{3,2,1,0:T(8,128)(2,1)S(1)}, u32[]{:S(2)}, u32[]{:S(2)}) async-start(bf16[8,2,64,384]{3,2,1,0:T(8,128)(2,1)} %bitcast.27), calls=%async_computation.5 | async-start | bytes 1572864 | tf_op jit(solution)/shard_map/all_to_all | solution.py:83
  68.6 1.6 convolution_convert_fusion
  70.2 0.9 reshape.123
  71.1 3.2 collective-permute-start.2
  74.3 2.5 collective-permute-start.3
  76.8 3.5 %collective-permute-start.4 = (bf16[64,512]{1,0:T(8,128)(2,1)S(1)}, bf16[64,512]{1,0:T(8,128)(2,1)S(1)}, u32[]{:S(2)}, u32[]{:S(2)}) collective-permute-start(bf16[64,512]{1,0:T(8,128)(2,1)S(1)} %reshape.123), channel_id=1, source_target_pairs={{0,384},{16,400},{32,416},{48,432},{64,448},{80,464},{96,480},{112... | collective-permute-start | bytes 196616 | tf_op jit(solution)/shard_map/ppermute | solution.py:126
  80.3 1.3 pad_maximum_fusion
  82.0 0.9 collective-permute-done.4
  84.2 1.1 copy.17
  85.2 0.9 copy-done.2
  86.1 4.8 %all-to-all-start.3 = ((bf16[8,2,2,64,192]{4,3,2,1,0:T(8,128)(2,1)}), bf16[8,2,2,64,192]{4,3,2,1,0:T(8,128)(2,1)S(1)}, u32[]{:S(2)}, u32[]{:S(2)}) async-start(bf16[8,2,2,64,192]{4,3,2,1,0:T(8,128)(2,1)} %bitcast.59), calls=%async_computation.3 | async-start | bytes 2097152 | tf_op jit(solution)/shard_map/all_to_all | solution.py:83
  90.9 2.4 to_blocks.3
  93.3 12.1 %all-to-all-done.3 = bf16[8,2,2,64,192]{4,3,2,1,0:T(8,128)(2,1)S(1)} async-done(((bf16[8,2,2,64,192]{4,3,2,1,0:T(8,128)(2,1)}), bf16[8,2,2,64,192]{4,3,2,1,0:T(8,128)(2,1)S(1)}, u32[]{:S(2)}, u32[]{:S(2)}) %all-to-all-start.3) | async-done | bytes 786464 | tf_op jit(solution)/shard_map/all_to_all | solution.py:83
  105.4 5.0 %all-to-all-start = ((bf16[8,4,64,384]{3,2,1,0:T(8,128)(2,1)}), bf16[8,4,64,384]{3,2,1,0:T(8,128)(2,1)S(1)}, u32[]{:S(2)}, u32[]{:S(2)}) async-start(bf16[8,4,64,384]{3,2,1,0:T(8,128)(2,1)} %bitcast.55), calls=%async_computation | async-start | bytes 3145728 | tf_op jit(solution)/shard_map/all_to_all | solution.py:83
  110.4 9.1 %collective-permute-start = (bf16[8,2,64,384]{3,2,1,0:T(8,128)(2,1)S(1)}, bf16[8,2,64,384]{3,2,1,0:T(8,128)(2,1)}, u32[]{:S(2)}, u32[]{:S(2)}) collective-permute-start(bf16[8,2,64,384]{3,2,1,0:T(8,128)(2,1)S(1)} %all-to-all-done.1.near_ref), channel_id=1, source_target_pairs={{0,8},{1,9},{2,10},{3,11},{4,12},{5,13},{6,14},{7,15},{8,0},{9,1},... | collective-permute-start | bytes 2359304 | tf_op jit(solution)/shard_map/ppermute | solution.py:276
  119.5 5.4 %collective-permute-start.11 = (bf16[8,2,64,384]{3,2,1,0:T(8,128)(2,1)}, bf16[8,2,64,384]{3,2,1,0:T(8,128)(2,1)}, u32[]{:S(2)}, u32[]{:S(2)}) collective-permute-start(bf16[8,2,64,384]{3,2,1,0:T(8,128)(2,1)} %copy-done.2), channel_id=1, source_target_pairs={{0,8},{1,9},{2,10},{3,11},{4,12},{5,13},{6,14},{7,15},{8,0},{9,1},... | collective-permute-start | bytes 2359304 | tf_op jit(solution)/shard_map/ppermute | solution.py:276
  125.1 9.1 %collective-permute-start.8 = (bf16[2,2,64,192]{3,2,1,0:T(8,128)(2,1)S(1)}, bf16[2,2,64,192]{3,2,1,0:T(8,128)(2,1)S(1)}, u32[]{:S(2)}, u32[]{:S(2)}) collective-permute-start(bf16[2,2,64,192]{3,2,1,0:T(8,128)(2,1)S(1)} %reduce_sum.22), channel_id=1, source_target_pairs={{0,8},{1,9},{2,10},{3,11},{4,12},{5,13},{6,14},{7,15},{8,0},{9,1},... | collective-permute-start | bytes 294920 | tf_op jit(solution)/shard_map/ppermute | solution.py:139
  134.3 135.5 %collective-permute-done.8 = bf16[2,2,64,192]{3,2,1,0:T(8,128)(2,1)S(1)} collective-permute-done((bf16[2,2,64,192]{3,2,1,0:T(8,128)(2,1)S(1)}, bf16[2,2,64,192]{3,2,1,0:T(8,128)(2,1)S(1)}, u32[]{:S(2)}, u32[]{:S(2)}) %collective-permute-start.8) | collective-permute-done | bytes 98336 | tf_op jit(solution)/shard_map/ppermute | solution.py:139
  269.8 7.6 %collective-permute-start.10 = (bf16[2,64,192]{2,1,0:T(8,128)(2,1)S(1)}, bf16[2,64,192]{2,1,0:T(8,128)(2,1)S(1)}, u32[]{:S(2)}, u32[]{:S(2)}) collective-permute-start(bf16[2,64,192]{2,1,0:T(8,128)(2,1)S(1)} %get-tuple-element.22), channel_id=1, source_target_pairs={{0,256},{1,384},{2,258},{3,386},{4,260},{5,388},{6,262},{7,390},{8... | collective-permute-start | bytes 147464 | tf_op jit(solution)/shard_map/ppermute | solution.py:144
  277.4 3.3 collective-permute-start.9
  280.8 1.2 copy-done
  282.0 6.4 %latent_attention.2.so_ref = bf16[8,64,384]{2,1,0:T(8,128)(2,1)} custom-call(bf16[8,4,64,384]{3,2,1,0:T(8,128)(2,1)} %copy-done, bf16[8,2,64,384]{3,2,1,0:T(8,128)(2,1)} %copy-done.1, bf16[8,2,64,384]{3,2,1,0:T(8,128)(2,1)} %collective-permute-done.far_ref), custom_call_target="tpu_custom_call" | custom-call | tf_op jit(solution)/shard_map/latent_attention/pallas_call | solution.py:178
  288.4 6.4 %latent_attention.3.so_ref = bf16[8,64,384]{2,1,0:T(8,128)(2,1)} custom-call(bf16[8,4,64,384]{3,2,1,0:T(8,128)(2,1)} %copy-done, bf16[8,2,64,384]{3,2,1,0:T(8,128)(2,1)} %copy-done.2, bf16[8,2,64,384]{3,2,1,0:T(8,128)(2,1)} %collective-permute-done.11.far_ref), custom_call_target="tpu_custom_call" | custom-call | tf_op jit(solution)/shard_map/latent_attention/pallas_call | solution.py:178
  294.9 0.7 pad_maximum_fusion.3.context_ref
  295.6 4.5 %cross_attention.2 = (bf16[8,2,64,384]{3,2,1,0:T(8,128)(2,1)}, f32[2,64,384]{2,1,0:T(8,128)}) custom-call(bf16[8,64,384]{2,1,0:T(8,128)(2,1)} %latent_attention.2.so_ref, bf16[8,4,64,384]{3,2,1,0:T(8,128)(2,1)} %copy-done, bf16[2,64,384]{2,1,0:T(8,128)(2,1)} %pad_maximum_fusion.3.context_ref), custom_call_target="tpu_custom_call" | custom-call | tf_op jit(solution)/shard_map/cross_attention/pallas_call | solution.py:237
  300.1 4.5 %cross_attention.3 = (bf16[8,2,64,384]{3,2,1,0:T(8,128)(2,1)}, bf16[2,64,384]{2,1,0:T(8,128)(2,1)}) custom-call(bf16[8,64,384]{2,1,0:T(8,128)(2,1)} %latent_attention.3.so_ref, bf16[8,4,64,384]{3,2,1,0:T(8,128)(2,1)} %copy-done, bf16[2,64,384]{2,1,0:T(8,128)(2,1)} %pad_maximum_fusion.3.context_ref, f32[2,64,384]{2,1,0:T(8,128)} %get-tuple-element.10.refs_0_), custom_call_target="tpu_custom_call" | custom-call | tf_op jit(solution)/shard_map/cross_attention/pallas_call | solution.py:237
  304.6 16.8 %all_to_all.35 = bf16[8,2,64,384]{3,2,1,0:T(8,128)(2,1)} all-to-all(bf16[8,2,64,384]{3,2,1,0:T(8,128)(2,1)} %get-tuple-element.11), channel_id=1, replica_groups={{0,1,2,3,4,5,6,7},{8,9,10,11,12,13,14,15},{16,17,18,19,20,21,22,23},{24..., dimensions={0} | all-to-all | bytes 1572864 | tf_op jit(solution)/shard_map/all_to_all | solution.py:83
  321.4 4.9 %all-to-all-start.4 = ((bf16[8,2,64,384]{3,2,1,0:T(8,128)(2,1)}), bf16[8,2,64,384]{3,2,1,0:T(8,128)(2,1)S(1)}, u32[]{:S(2)}, u32[]{:S(2)}) async-start(bf16[8,2,64,384]{3,2,1,0:T(8,128)(2,1)} %get-tuple-element.9), calls=%async_computation.4 | async-start | bytes 1572864 | tf_op jit(solution)/shard_map/all_to_all | solution.py:83
  326.4 0.7 collective-permute-start.12
  327.1 7.6 %collective-permute-start.13 = (bf16[2,64,192]{2,1,0:T(8,128)(2,1)S(1)}, bf16[2,64,192]{2,1,0:T(8,128)(2,1)S(1)}, u32[]{:S(2)}, u32[]{:S(2)}) collective-permute-start(bf16[2,64,192]{2,1,0:T(8,128)(2,1)S(1)} %get-tuple-element.24), channel_id=1, source_target_pairs={{0,1},{1,9},{2,3},{3,11},{4,5},{5,13},{6,7},{7,15},{8,0},{9,8},{10... | collective-permute-start | bytes 147464 | tf_op jit(solution)/shard_map/ppermute | solution.py:264
  334.7 8.2 %collective-permute-done.13 = bf16[2,64,192]{2,1,0:T(8,128)(2,1)S(1)} collective-permute-done((bf16[2,64,192]{2,1,0:T(8,128)(2,1)S(1)}, bf16[2,64,192]{2,1,0:T(8,128)(2,1)S(1)}, u32[]{:S(2)}, u32[]{:S(2)}) %collective-permute-start.13) | collective-permute-done | bytes 49184 | tf_op jit(solution)/shard_map/ppermute | solution.py:264
  343.6 0.9 copy-done.3
  344.5 2.3 from_blocks.1
  (51 shorter events, 4.1 us)
Async XLA Ops:
  0.6 17.1 %collective-permute-start.5 = (bf16[1,512,192]{1,2,0:T(8,128)(2,1)}, bf16[1,512,192]{1,2,0:T(8,128)(2,1)S(1)}, u32[]{:S(2)}, u32[]{:S(2)}) collective-permute-start(bf16[1,512,192]{1,2,0:T(8,128)(2,1)} %bitcast.67), channel_id=1, source_target_pairs={{0,64},{16,80},{32,96},{48,112},{64,0},{80,16},{96,32},{112,48},{1... | collective-permute-start | bytes 589832 | tf_op jit(solution)/shard_map/ppermute | solution.py:118
  3.5 32.8 %collective-permute-start.1 = (bf16[2,20,512]{2,0,1:T(2,128)(2,1)S(1)}, bf16[2,20,512]{2,0,1:T(2,128)(2,1)S(1)}, u32[]{:S(2)}, u32[]{:S(2)}) collective-permute-start(bf16[2,20,512]{2,0,1:T(2,128)(2,1)S(1)} %get-tuple-element.26), channel_id=1, source_target_pairs={{0,8},{1,9},{2,10},{3,11},{4,12},{5,13},{6,14},{7,15},{8,0},{9,1},... | collective-permute-start | bytes 122888 | tf_op jit(solution)/shard_map/ppermute | solution.py:92
  18.6 33.3 %collective-permute-start.6 = (bf16[2,512,192]{1,2,0:T(8,128)(2,1)S(1)}, bf16[2,512,192]{1,2,0:T(8,128)(2,1)S(1)}, u32[]{:S(2)}, u32[]{:S(2)}) collective-permute-start(bf16[2,512,192]{1,2,0:T(8,128)(2,1)S(1)} %pad_maximum_fusion.2), channel_id=1, source_target_pairs={{0,32},{16,48},{32,0},{48,16},{64,96},{80,112},{96,64},{112,80},{1... | collective-permute-start | bytes 1179656 | tf_op jit(solution)/shard_map/ppermute | solution.py:118
  36.3 15.7 %copy-start.4 = (bf16[512,192]{0,1:T(8,128)(2,1)S(1)}, bf16[512,192]{0,1:T(8,128)(2,1)}, u32[]{:S(2)}) copy-start(bf16[512,192]{0,1:T(8,128)(2,1)} %param.9) | copy-start | bytes 589828
  37.2 9.8 %all-to-all-start.2 = ((bf16[8,2,2,20,128]{4,2,3,1,0:T(2,128)(2,1)}), bf16[8,2,2,20,128]{4,2,3,1,0:T(2,128)(2,1)S(1)}, u32[]{:S(2)}, u32[]{:S(2)}) async-start(bf16[8,2,2,20,128]{4,2,3,1,0:T(2,128)(2,1)} %bitcast.10), calls=%async_computation.2 | async-start | bytes 327680 | tf_op jit(solution)/shard_map/all_to_all | solution.py:83
  47.1 16.6 %all-to-all-start.1 = ((bf16[8,2,64,384]{3,2,1,0:T(8,128)(2,1)}), bf16[8,2,64,384]{3,2,1,0:T(8,128)(2,1)S(1)}, u32[]{:S(2)}, u32[]{:S(2)}) async-start(bf16[8,2,64,384]{3,2,1,0:T(8,128)(2,1)} %bitcast.62), calls=%async_computation.1 | async-start | bytes 1572864 | tf_op jit(solution)/shard_map/all_to_all | solution.py:83
  52.1 4.2 %copy-start.6 = (bf16[1,64,512]{2,1,0:T(8,128)(2,1)S(1)}, bf16[1,64,512]{2,1,0:T(8,128)(2,1)}, u32[]{:S(2)}) copy-start(bf16[1,64,512]{2,1,0:T(8,128)(2,1)} %param.7) | copy-start | bytes 196612
  52.1 28.2 %collective-permute-start.7 = (bf16[4,512,192]{1,2,0:T(8,128)(2,1)S(1)}, bf16[4,512,192]{1,2,0:T(8,128)(2,1)}, u32[]{:S(2)}, u32[]{:S(2)}) collective-permute-start(bf16[4,512,192]{1,2,0:T(8,128)(2,1)S(1)} %pad_maximum_fusion.1), channel_id=1, source_target_pairs={{0,16},{16,0},{32,48},{48,32},{64,80},{80,64},{96,112},{112,96},{1... | collective-permute-start | bytes 2359304 | tf_op jit(solution)/shard_map/ppermute | solution.py:118
  57.5 6.2 %copy-start.7 = (f32[256]{0:T(256)}, f32[256]{0:T(256)S(1)}, u32[]{:S(2)}) copy-start(f32[256]{0:T(256)S(1)} %get-tuple-element.27) | copy-start | bytes 3076
  63.7 46.7 %copy-start.1 = (bf16[8,2,64,384]{3,2,1,0:T(8,128)(2,1)}, bf16[8,2,64,384]{3,2,1,0:T(8,128)(2,1)S(1)}, u32[]{:S(2)}) copy-start(bf16[8,2,64,384]{3,2,1,0:T(8,128)(2,1)S(1)} %all-to-all-done.1.near_ref) | copy-start | bytes 2359300
  63.7 21.6 %all-to-all-start.5 = ((bf16[8,2,64,384]{3,2,1,0:T(8,128)(2,1)}), bf16[8,2,64,384]{3,2,1,0:T(8,128)(2,1)S(1)}, u32[]{:S(2)}, u32[]{:S(2)}) async-start(bf16[8,2,64,384]{3,2,1,0:T(8,128)(2,1)} %bitcast.27), calls=%async_computation.5 | async-start | bytes 1572864 | tf_op jit(solution)/shard_map/all_to_all | solution.py:83
  71.1 10.5 %collective-permute-start.2 = (bf16[64,512]{1,0:T(8,128)(2,1)S(1)}, bf16[64,512]{1,0:T(8,128)(2,1)S(1)}, u32[]{:S(2)}, u32[]{:S(2)}) collective-permute-start(bf16[64,512]{1,0:T(8,128)(2,1)S(1)} %reshape.123), channel_id=1, source_target_pairs={{0,128},{16,144},{32,160},{48,176},{64,192},{80,208},{96,224},{112... | collective-permute-start | bytes 196616 | tf_op jit(solution)/shard_map/ppermute | solution.py:126
  74.3 7.8 %collective-permute-start.3 = (bf16[64,512]{1,0:T(8,128)(2,1)S(1)}, bf16[64,512]{1,0:T(8,128)(2,1)S(1)}, u32[]{:S(2)}, u32[]{:S(2)}) collective-permute-start(bf16[64,512]{1,0:T(8,128)(2,1)S(1)} %reshape.123), channel_id=1, source_target_pairs={{0,256},{16,272},{32,288},{48,304},{64,320},{80,336},{96,352},{112... | collective-permute-start | bytes 196616 | tf_op jit(solution)/shard_map/ppermute | solution.py:126
  76.8 6.2 %collective-permute-start.4 = (bf16[64,512]{1,0:T(8,128)(2,1)S(1)}, bf16[64,512]{1,0:T(8,128)(2,1)S(1)}, u32[]{:S(2)}, u32[]{:S(2)}) collective-permute-start(bf16[64,512]{1,0:T(8,128)(2,1)S(1)} %reshape.123), channel_id=1, source_target_pairs={{0,384},{16,400},{32,416},{48,432},{64,448},{80,464},{96,480},{112... | collective-permute-start | bytes 196616 | tf_op jit(solution)/shard_map/ppermute | solution.py:126
  85.2 0.9 copy-start.2
  86.1 19.3 %all-to-all-start.3 = ((bf16[8,2,2,64,192]{4,3,2,1,0:T(8,128)(2,1)}), bf16[8,2,2,64,192]{4,3,2,1,0:T(8,128)(2,1)S(1)}, u32[]{:S(2)}, u32[]{:S(2)}) async-start(bf16[8,2,2,64,192]{4,3,2,1,0:T(8,128)(2,1)} %bitcast.59), calls=%async_computation.3 | async-start | bytes 2097152 | tf_op jit(solution)/shard_map/all_to_all | solution.py:83
  105.4 175.4 %all-to-all-start = ((bf16[8,4,64,384]{3,2,1,0:T(8,128)(2,1)}), bf16[8,4,64,384]{3,2,1,0:T(8,128)(2,1)S(1)}, u32[]{:S(2)}, u32[]{:S(2)}) async-start(bf16[8,4,64,384]{3,2,1,0:T(8,128)(2,1)} %bitcast.55), calls=%async_computation | async-start | bytes 3145728 | tf_op jit(solution)/shard_map/all_to_all | solution.py:83
  110.4 170.4 %collective-permute-start = (bf16[8,2,64,384]{3,2,1,0:T(8,128)(2,1)S(1)}, bf16[8,2,64,384]{3,2,1,0:T(8,128)(2,1)}, u32[]{:S(2)}, u32[]{:S(2)}) collective-permute-start(bf16[8,2,64,384]{3,2,1,0:T(8,128)(2,1)S(1)} %all-to-all-done.1.near_ref), channel_id=1, source_target_pairs={{0,8},{1,9},{2,10},{3,11},{4,12},{5,13},{6,14},{7,15},{8,0},{9,1},... | collective-permute-start | bytes 2359304 | tf_op jit(solution)/shard_map/ppermute | solution.py:276
  119.5 168.9 %collective-permute-start.11 = (bf16[8,2,64,384]{3,2,1,0:T(8,128)(2,1)}, bf16[8,2,64,384]{3,2,1,0:T(8,128)(2,1)}, u32[]{:S(2)}, u32[]{:S(2)}) collective-permute-start(bf16[8,2,64,384]{3,2,1,0:T(8,128)(2,1)} %copy-done.2), channel_id=1, source_target_pairs={{0,8},{1,9},{2,10},{3,11},{4,12},{5,13},{6,14},{7,15},{8,0},{9,1},... | collective-permute-start | bytes 2359304 | tf_op jit(solution)/shard_map/ppermute | solution.py:276
  125.1 144.6 %collective-permute-start.8 = (bf16[2,2,64,192]{3,2,1,0:T(8,128)(2,1)S(1)}, bf16[2,2,64,192]{3,2,1,0:T(8,128)(2,1)S(1)}, u32[]{:S(2)}, u32[]{:S(2)}) collective-permute-start(bf16[2,2,64,192]{3,2,1,0:T(8,128)(2,1)S(1)} %reduce_sum.22), channel_id=1, source_target_pairs={{0,8},{1,9},{2,10},{3,11},{4,12},{5,13},{6,14},{7,15},{8,0},{9,1},... | collective-permute-start | bytes 294920 | tf_op jit(solution)/shard_map/ppermute | solution.py:139
  269.8 25.0 %collective-permute-start.10 = (bf16[2,64,192]{2,1,0:T(8,128)(2,1)S(1)}, bf16[2,64,192]{2,1,0:T(8,128)(2,1)S(1)}, u32[]{:S(2)}, u32[]{:S(2)}) collective-permute-start(bf16[2,64,192]{2,1,0:T(8,128)(2,1)S(1)} %get-tuple-element.22), channel_id=1, source_target_pairs={{0,256},{1,384},{2,258},{3,386},{4,260},{5,388},{6,262},{7,390},{8... | collective-permute-start | bytes 147464 | tf_op jit(solution)/shard_map/ppermute | solution.py:144
  277.4 17.4 %collective-permute-start.9 = (bf16[2,64,192]{2,1,0:T(8,128)(2,1)S(1)}, bf16[2,64,192]{2,1,0:T(8,128)(2,1)S(1)}, u32[]{:S(2)}, u32[]{:S(2)}) collective-permute-start(bf16[2,64,192]{2,1,0:T(8,128)(2,1)S(1)} %get-tuple-element.21), channel_id=1, source_target_pairs={{0,0},{1,128},{2,2},{3,130},{4,4},{5,132},{6,6},{7,134},{8,8},{9,1... | collective-permute-start | bytes 147464 | tf_op jit(solution)/shard_map/ppermute | solution.py:144
  280.8 1.2 copy-start
  304.6 21.7 %copy-start.5 = (bf16[2,64,384]{2,1,0:T(8,128)(2,1)S(1)}, bf16[2,64,384]{2,1,0:T(8,128)(2,1)}, u32[]{:S(2)}) copy-start(bf16[2,64,384]{2,1,0:T(8,128)(2,1)} %get-tuple-element.14) | copy-start | bytes 294916
  321.4 22.2 %all-to-all-start.4 = ((bf16[8,2,64,384]{3,2,1,0:T(8,128)(2,1)}), bf16[8,2,64,384]{3,2,1,0:T(8,128)(2,1)S(1)}, u32[]{:S(2)}, u32[]{:S(2)}) async-start(bf16[8,2,64,384]{3,2,1,0:T(8,128)(2,1)} %get-tuple-element.9), calls=%async_computation.4 | async-start | bytes 1572864 | tf_op jit(solution)/shard_map/all_to_all | solution.py:83
  326.4 8.3 %collective-permute-start.12 = (bf16[2,64,192]{2,1,0:T(8,128)(2,1)S(1)}, bf16[2,64,192]{2,1,0:T(8,128)(2,1)S(1)}, u32[]{:S(2)}, u32[]{:S(2)}) collective-permute-start(bf16[2,64,192]{2,1,0:T(8,128)(2,1)S(1)} %get-tuple-element.23), channel_id=1, source_target_pairs={{0,0},{1,8},{2,2},{3,10},{4,4},{5,12},{6,6},{7,14},{8,1},{9,9},{10... | collective-permute-start | bytes 147464 | tf_op jit(solution)/shard_map/ppermute | solution.py:263
  327.1 15.9 %collective-permute-start.13 = (bf16[2,64,192]{2,1,0:T(8,128)(2,1)S(1)}, bf16[2,64,192]{2,1,0:T(8,128)(2,1)S(1)}, u32[]{:S(2)}, u32[]{:S(2)}) collective-permute-start(bf16[2,64,192]{2,1,0:T(8,128)(2,1)S(1)} %get-tuple-element.24), channel_id=1, source_target_pairs={{0,1},{1,9},{2,3},{3,11},{4,5},{5,13},{6,7},{7,15},{8,0},{9,8},{10... | collective-permute-start | bytes 147464 | tf_op jit(solution)/shard_map/ppermute | solution.py:264
  343.6 0.9 copy-start.3

commit v3 on v2

--- a/solution.py
+++ b/solution.py
@@ -111,19 +111,20 @@
     return mixed.astype(jnp.bfloat16).reshape(QUERY_TOKENS, heads * HEAD_SIZE)
 
 
-def gather_run(connector):
+def gather_columns(connector):
     got = connector[None]
-    for k in (4, 2, 1):
+    for k in (2, 1):
         pairs = [(8 * a + b, 8 * a + (b ^ k)) for a in range(4) for b in range(8)]
         got = jnp.concatenate([got, lax.ppermute(got, "fsdp", pairs)])
     return got
 
 
-def gather_ring(hidden):
-    got = [hidden]
+def gather_rows(hidden):
+    pairs = [(8 * a + b, 8 * a + (b ^ 4)) for a in range(4) for b in range(8)]
+    got = [jnp.concatenate([hidden, lax.ppermute(hidden, "fsdp", pairs)])]
     for k in (1, 2, 3):
         pairs = [(8 * a + b, 8 * (a ^ k) + b) for a in range(4) for b in range(8)]
-        got.append(lax.ppermute(hidden, "fsdp", pairs))
+        got.append(lax.ppermute(got[0], "fsdp", pairs))
     return jnp.concatenate(got)
 
 
@@ -132,15 +133,23 @@
     y, zl = f // 8, f % 8
     width = columns.shape[2]
     part = jnp.einsum("rk,skn->rsn", rows, columns, preferred_element_type=jnp.float32)
-    part = part.astype(jnp.bfloat16).reshape(2, 2, QUERY_TOKENS, 2, 2, 2, width)
-    part = part.transpose(5, 4, 1, 0, 3, 2, 6).reshape(8, 2, 2, QUERY_TOKENS, width)
+    part = part.astype(jnp.bfloat16).reshape(2, 2, 2, QUERY_TOKENS, 2, 2, width)
+    part = part.transpose(2, 5, 1, 0, 4, 3, 6).reshape(8, 2, 2, QUERY_TOKENS, width)
     got = exchange(part)
     mine = jnp.sum(got.astype(jnp.float32), axis=0).astype(jnp.bfloat16)
     there = lax.ppermute(mine, "tp", SWAP_HALF)
     mine = (mine.astype(jnp.float32) + there.astype(jnp.float32)).astype(jnp.bfloat16)
     got = []
     for a in range(2):
-        pairs = joint(lambda y, z, h, m, c: (y ^ (2 * a + c), z, h, m ^ (z // 2), y % 2))
+        pairs = joint(
+            lambda y, z, h, m, c: (
+                y ^ (2 * a + c),
+                z ^ (4 * (m // 2)),
+                h,
+                2 * (z // 4) + (z // 2 % 2 ^ m % 2),
+                y % 2,
+            )
+        )
         got.append(lax.ppermute(mine[a], ("fsdp", "tp"), pairs))
     one, two = got
     keys = jnp.where(y < 2, one, two)
@@ -151,12 +160,12 @@
     return jnp.concatenate([first, second], axis=2)
 
 
-def attention_kernel(q_ref, near_ref, far_ref, o_ref):
+def attention_kernel(q_ref, near_ref, fk_ref, fv_ref, o_ref):
     half = LATENT_TOKENS // 2
     near_k = near_ref[:, 0].reshape(half, HEAD_SIZE)
-    far_k = far_ref[:, 0].reshape(half, HEAD_SIZE)
+    far_k = fk_ref[...].reshape(half, HEAD_SIZE)
     near_v = near_ref[:, 1].reshape(half, HEAD_SIZE)
-    far_v = far_ref[:, 1].reshape(half, HEAD_SIZE)
+    far_v = fv_ref[...].reshape(half, HEAD_SIZE)
     transposed = (((1,), (1,)), ((), ()))
     for part in range(4):
         q = q_ref[2 * part : 2 * part + 2, 0].reshape(half // 4, HEAD_SIZE)
@@ -172,21 +181,22 @@
         o_ref[2 * part : 2 * part + 2] = out.reshape(2, half // 8, HEAD_SIZE)
 
 
-def attention(sample, query_gradient, near, far):
+def attention(sample, query_gradient, near, far_k, far_v):
     rows = near.shape[2]
-    pair_spec = pl.BlockSpec((8, 2, rows, HEAD_SIZE), lambda n: (0, 0, 0, n))
+    spec = pl.BlockSpec((8, rows, HEAD_SIZE), lambda n: (0, 0, n))
     return pl.pallas_call(
         attention_kernel,
         grid=(3,),
         in_specs=[
             pl.BlockSpec((8, 1, rows, HEAD_SIZE), lambda n: (0, sample, 0, n)),
-            pair_spec,
-            pair_spec,
+            pl.BlockSpec((8, 2, rows, HEAD_SIZE), lambda n: (0, 0, 0, n)),
+            spec,
+            spec,
         ],
-        out_specs=pl.BlockSpec((8, rows, HEAD_SIZE), lambda n: (0, 0, n)),
+        out_specs=spec,
         out_shape=jax.ShapeDtypeStruct((8, rows, BLOCK), jnp.bfloat16),
         name="latent_attention",
-    )(query_gradient, near, far)
+    )(query_gradient, near, far_k, far_v)
 
 
 def cross_kernel(so_ref, g_ref, context_ref, *refs):
@@ -273,14 +283,14 @@
     near, far = [], []
     for s in range(SAMPLE_COUNT):
         near.append(exchange(to_blocks(s, 1, key, value)))
-        far.append(lax.ppermute(near[s], "tp", SWAP_HALF))
-    columns = gather_run(connector)
+        far.append([lax.ppermute(near[s][:, i], "tp", SWAP_HALF) for i in range(2)])
+    columns = gather_columns(connector)
     hidden = llm_hidden(llm_query, llm_kv)
     query_gradient = exchange(to_blocks(0, 2, query, cotangent))
-    context = context_tokens(gather_ring(hidden), columns)
+    context = context_tokens(gather_rows(hidden), columns)
     out, carry = [], ()
     for s in range(SAMPLE_COUNT):
-        so = attention(s, query_gradient, near[s], far[s])
+        so = attention(s, query_gradient, near[s], *far[s])
         result, partial = cross(s, so, query_gradient, context, carry)
         carry = (partial,)
         out.append(exchange(result))

time: 348 us -> 336 us (0.966)
  the two profiles are of different devices: /device:TPU:178 before, /device:TPU:2 now
where the time goes in v3:
time: 336 us; the launch traced here: 334 us
  waiting for transfers between devices  138 us (41%)
  starting transfers between devices  116 us (35%)
  Pallas kernels  30.6 us (9%)
  blocking collectives  26.6 us (8%)
  local copies, waits for them, and re-layouts  15.6 us (5%)
  other arithmetic  4.39 us (1%)
    ppermute x4, waiting for transfers between devices, layer(): far.append([lax.ppermute(near[s][:, i], 'tp', SWAP_HALF) for i in range(2)])  83.2 us
    all_to_all x6, starting transfers between devices, exchange(): lax.all_to_all(x, 'tp', split_axis=0, concat_axis=0, axis_index_groups=HA...  29.3 us
    ppermute x4, starting transfers between devices, layer(): far.append([lax.ppermute(near[s][:, i], 'tp', SWAP_HALF) for i in range(2)])  29.1 us
    all_to_all x1, blocking collectives, exchange(): lax.all_to_all(x, 'tp', split_axis=0, concat_axis=0, axis_index_groups=HA...  26.6 us
    all_to_all x6, waiting for transfers between devices, exchange(): lax.all_to_all(x, 'tp', split_axis=0, concat_axis=0, axis_index_groups=HA...  18.6 us
    ppermute x1, starting transfers between devices, llm_hidden(): take = lax.ppermute(give, 'tp', SWAP_HALF)  15.7 us
    ppermute x1, waiting for transfers between devices, context_tokens(): there = lax.ppermute(mine, 'tp', SWAP_HALF)  15.4 us
    pallas_call x2, Pallas kernels, attention(): pl.pallas_call(attention_kernel, grid=(3,), in_specs=[pl.BlockSpec((8, 1,...  12.9 us
  transfers between devices with their start and end apart: 22, of which 9 were waited for; matrix products, arithmetic and copies ran while one was open for 5% of the time, Pallas kernels for 6%

profile of v3, /device:TPU:2, one launch (start us, length us, event | category | flops | bytes accessed | tf_op | source)
XLA Modules:
  0.0 334.3 jit_solution(14733745904139029805)
XLA Ops:
  1.5 15.7 %collective-permute-start.2 = (bf16[2,20,512]{2,0,1:T(2,128)(2,1)S(1)}, bf16[2,20,512]{2,0,1:T(2,128)(2,1)S(1)}, u32[]{:S(2)}, u32[]{:S(2)}) collective-permute-start(bf16[2,20,512]{2,0,1:T(2,128)(2,1)S(1)} %get-tuple-element.30), channel_id=1, source_target_pairs={{0,8},{1,9},{2,10},{3,11},{4,12},{5,13},{6,14},{7,15},{8,0},{9,1},... | collective-permute-start | bytes 122888 | tf_op jit(solution)/shard_map/ppermute | solution.py:92
  17.3 3.4 %collective-permute-start.7 = (bf16[1,512,192]{1,2,0:T(8,128)(2,1)}, bf16[1,512,192]{1,2,0:T(8,128)(2,1)S(1)}, u32[]{:S(2)}, u32[]{:S(2)}) collective-permute-start(bf16[1,512,192]{1,2,0:T(8,128)(2,1)} %bitcast.85), channel_id=1, source_target_pairs={{0,32},{16,48},{32,0},{48,16},{64,96},{80,112},{96,64},{112,80},{1... | collective-permute-start | bytes 589832 | tf_op jit(solution)/shard_map/ppermute | solution.py:118
  21.7 4.8 %all-to-all-start.2 = ((bf16[8,2,2,20,128]{4,2,3,1,0:T(2,128)(2,1)}), bf16[8,2,2,20,128]{4,2,3,1,0:T(2,128)(2,1)S(1)}, u32[]{:S(2)}, u32[]{:S(2)}) async-start(bf16[8,2,2,20,128]{4,2,3,1,0:T(2,128)(2,1)} %bitcast.12), calls=%async_computation.2 | async-start | bytes 327680 | tf_op jit(solution)/shard_map/all_to_all | solution.py:83
  27.6 2.0 to_blocks.4
  29.6 1.9 all-to-all-done.2
  31.6 4.9 %all-to-all-start.1 = ((bf16[8,2,64,384]{3,2,1,0:T(8,128)(2,1)}), bf16[8,2,64,384]{3,2,1,0:T(8,128)(2,1)S(1)}, u32[]{:S(2)}, u32[]{:S(2)}) async-start(bf16[8,2,64,384]{3,2,1,0:T(8,128)(2,1)} %bitcast.78), calls=%async_computation.1 | async-start | bytes 1572864 | tf_op jit(solution)/shard_map/all_to_all | solution.py:83
  38.1 4.6 %collective-permute-start.3 = (bf16[64,512]{1,0:T(8,128)(2,1)S(1)}, bf16[64,512]{1,0:T(8,128)(2,1)S(1)}, u32[]{:S(2)}, u32[]{:S(2)}) collective-permute-start(bf16[64,512]{1,0:T(8,128)(2,1)S(1)} %reshape.123), channel_id=1, source_target_pairs={{0,64},{16,80},{32,96},{48,112},{64,0},{80,16},{96,32},{112,48},{1... | collective-permute-start | bytes 196616 | tf_op jit(solution)/shard_map/ppermute | solution.py:124
  43.3 8.9 %collective-permute-done.3 = bf16[64,512]{1,0:T(8,128)(2,1)S(1)} collective-permute-done((bf16[64,512]{1,0:T(8,128)(2,1)S(1)}, bf16[64,512]{1,0:T(8,128)(2,1)S(1)}, u32[]{:S(2)}, u32[]{:S(2)}) %collective-permute-start.3) | collective-permute-done | bytes 65568 | tf_op jit(solution)/shard_map/ppermute | solution.py:124
  52.8 3.4 %collective-permute-start.4 = (bf16[128,512]{1,0:T(8,128)(2,1)}, bf16[128,512]{1,0:T(8,128)(2,1)S(1)}, u32[]{:S(2)}, u32[]{:S(2)}) collective-permute-start(bf16[128,512]{1,0:T(8,128)(2,1)} %get-tuple-element.31), channel_id=1, source_target_pairs={{0,128},{16,144},{32,160},{48,176},{64,192},{80,208},{96,224},{112... | collective-permute-start | bytes 393224 | tf_op jit(solution)/shard_map/ppermute | solution.py:127
  56.4 1.9 collective-permute-start.8
  58.3 4.8 %collective-permute-start.5 = (bf16[128,512]{1,0:T(8,128)(2,1)}, bf16[128,512]{1,0:T(8,128)(2,1)}, u32[]{:S(2)}, u32[]{:S(2)}) collective-permute-start(bf16[128,512]{1,0:T(8,128)(2,1)} %get-tuple-element.31), channel_id=1, source_target_pairs={{0,256},{16,272},{32,288},{48,304},{64,320},{80,336},{96,352},{112... | collective-permute-start | bytes 393224 | tf_op jit(solution)/shard_map/ppermute | solution.py:127
  63.1 2.1 to_blocks.5
  65.2 2.2 collective-permute-start.6
  67.3 4.8 %all-to-all-start.5 = ((bf16[8,2,64,384]{3,2,1,0:T(8,128)(2,1)}), bf16[8,2,64,384]{3,2,1,0:T(8,128)(2,1)S(1)}, u32[]{:S(2)}, u32[]{:S(2)}) async-start(bf16[8,2,64,384]{3,2,1,0:T(8,128)(2,1)} %bitcast.79), calls=%async_computation.5 | async-start | bytes 1572864 | tf_op jit(solution)/shard_map/all_to_all | solution.py:83
  72.2 0.9 constant_dynamic-update-slice_fusion.3
  74.2 1.6 fusion.7
  75.9 1.0 convert_element_type.31
  76.9 1.4 copy.26
  78.3 1.1 copy.27
  79.3 4.5 %all-to-all-done.5.near_ref = bf16[8,2,64,384]{3,2,1,0:T(8,128)(2,1)S(1)} async-done(((bf16[8,2,64,384]{3,2,1,0:T(8,128)(2,1)}), bf16[8,2,64,384]{3,2,1,0:T(8,128)(2,1)S(1)}, u32[]{:S(2)}, u32[]{:S(2)}) %all-to-all-start.5) | async-done | bytes 786464 | tf_op jit(solution)/shard_map/all_to_all | solution.py:83
  83.8 4.9 %all-to-all-start.3 = ((bf16[8,2,2,64,192]{4,3,2,1,0:T(8,128)(2,1)}), bf16[8,2,2,64,192]{4,3,2,1,0:T(8,128)(2,1)S(1)}, u32[]{:S(2)}, u32[]{:S(2)}) async-start(bf16[8,2,2,64,192]{4,3,2,1,0:T(8,128)(2,1)} %bitcast.75), calls=%async_computation.3 | async-start | bytes 2097152 | tf_op jit(solution)/shard_map/all_to_all | solution.py:83
  88.8 2.4 to_blocks.3
  91.1 12.1 %all-to-all-done.3 = bf16[8,2,2,64,192]{4,3,2,1,0:T(8,128)(2,1)S(1)} async-done(((bf16[8,2,2,64,192]{4,3,2,1,0:T(8,128)(2,1)}), bf16[8,2,2,64,192]{4,3,2,1,0:T(8,128)(2,1)S(1)}, u32[]{:S(2)}, u32[]{:S(2)}) %all-to-all-start.3) | async-done | bytes 786464 | tf_op jit(solution)/shard_map/all_to_all | solution.py:83
  103.3 1.0 copy-done.3
  104.3 4.9 %all-to-all-start = ((bf16[8,4,64,384]{3,2,1,0:T(8,128)(2,1)}), bf16[8,4,64,384]{3,2,1,0:T(8,128)(2,1)S(1)}, u32[]{:S(2)}, u32[]{:S(2)}) async-start(bf16[8,4,64,384]{3,2,1,0:T(8,128)(2,1)} %bitcast.72), calls=%async_computation | async-start | bytes 3145728 | tf_op jit(solution)/shard_map/all_to_all | solution.py:83
  109.2 1.0 slice_bitcast_fusion.2
  110.2 11.7 %collective-permute-start = (bf16[8,64,384]{2,1,0:T(8,128)(2,1)}, bf16[8,64,384]{2,1,0:T(8,128)(2,1)S(1)}, u32[]{:S(2)}, u32[]{:S(2)}) collective-permute-start(bf16[8,64,384]{2,1,0:T(8,128)(2,1)} %get-tuple-element.20), channel_id=1, source_target_pairs={{0,8},{1,9},{2,10},{3,11},{4,12},{5,13},{6,14},{7,15},{8,0},{9,1},... | collective-permute-start | bytes 1179656 | tf_op jit(solution)/shard_map/ppermute | solution.py:286
  121.9 2.8 collective-permute-start.1
  124.7 1.4 reduce_sum.22
  126.1 11.8 %collective-permute-start.9 = (bf16[2,2,64,192]{3,2,1,0:T(8,128)(2,1)S(1)}, bf16[2,2,64,192]{3,2,1,0:T(8,128)(2,1)S(1)}, u32[]{:S(2)}, u32[]{:S(2)}) collective-permute-start(bf16[2,2,64,192]{3,2,1,0:T(8,128)(2,1)S(1)} %reduce_sum.22), channel_id=1, source_target_pairs={{0,8},{1,9},{2,10},{3,11},{4,12},{5,13},{6,14},{7,15},{8,0},{9,1},... | collective-permute-start | bytes 294920 | tf_op jit(solution)/shard_map/ppermute | solution.py:140
  137.9 1.0 slice_bitcast_fusion
  138.9 2.8 collective-permute-start.12
  141.7 11.8 %collective-permute-start.13 = (bf16[8,64,384]{2,1,0:T(8,128)(2,1)}, bf16[8,64,384]{2,1,0:T(8,128)(2,1)S(1)}, u32[]{:S(2)}, u32[]{:S(2)}) collective-permute-start(bf16[8,64,384]{2,1,0:T(8,128)(2,1)} %get-tuple-element.17), channel_id=1, source_target_pairs={{0,8},{1,9},{2,10},{3,11},{4,12},{5,13},{6,14},{7,15},{8,0},{9,1},... | collective-permute-start | bytes 1179656 | tf_op jit(solution)/shard_map/ppermute | solution.py:286
  153.4 15.4 %collective-permute-done.9 = bf16[2,2,64,192]{3,2,1,0:T(8,128)(2,1)S(1)} collective-permute-done((bf16[2,2,64,192]{3,2,1,0:T(8,128)(2,1)S(1)}, bf16[2,2,64,192]{3,2,1,0:T(8,128)(2,1)S(1)}, u32[]{:S(2)}, u32[]{:S(2)}) %collective-permute-start.9) | collective-permute-done | bytes 98336 | tf_op jit(solution)/shard_map/ppermute | solution.py:140
  169.6 4.0 %collective-permute-start.11 = (bf16[2,64,192]{2,1,0:T(8,128)(2,1)S(1)}, bf16[2,64,192]{2,1,0:T(8,128)(2,1)S(1)}, u32[]{:S(2)}, u32[]{:S(2)}) collective-permute-start(bf16[2,64,192]{2,1,0:T(8,128)(2,1)S(1)} %get-tuple-element.26), channel_id=1, source_target_pairs={{0,256},{1,384},{2,258},{3,386},{4,320},{5,448},{6,322},{7,450},{8... | collective-permute-start | bytes 147464 | tf_op jit(solution)/shard_map/ppermute | solution.py:153
  174.4 1.2 copy-done
  175.6 6.4 %latent_attention.2.so_ref = bf16[8,64,384]{2,1,0:T(8,128)(2,1)} custom-call(bf16[8,4,64,384]{3,2,1,0:T(8,128)(2,1)} %copy-done, bf16[8,2,64,384]{3,2,1,0:T(8,128)(2,1)} %copy-done.1, bf16[8,64,384]{2,1,0:T(8,128)(2,1)} %copy-done.7, bf16[8,64,384]{2,1,0:T(8,128)(2,1)} %copy-done.8), custom_call_target="tpu_custom_call" | custom-call | tf_op jit(solution)/shard_map/latent_attention/pallas_call | solution.py:187
  182.1 8.3 %collective-permute-done.12.fk_ref = bf16[8,64,384]{2,1,0:T(8,128)(2,1)S(1)} collective-permute-done((bf16[8,64,384]{2,1,0:T(8,128)(2,1)}, bf16[8,64,384]{2,1,0:T(8,128)(2,1)S(1)}, u32[]{:S(2)}, u32[]{:S(2)}) %collective-permute-start.12) | collective-permute-done | bytes 393248 | tf_op jit(solution)/shard_map/ppermute | solution.py:286
  190.3 74.9 %collective-permute-done.13.fv_ref = bf16[8,64,384]{2,1,0:T(8,128)(2,1)S(1)} collective-permute-done((bf16[8,64,384]{2,1,0:T(8,128)(2,1)}, bf16[8,64,384]{2,1,0:T(8,128)(2,1)S(1)}, u32[]{:S(2)}, u32[]{:S(2)}) %collective-permute-start.13) | collective-permute-done | bytes 393248 | tf_op jit(solution)/shard_map/ppermute | solution.py:286
  266.0 6.4 %latent_attention.3.so_ref = bf16[8,64,384]{2,1,0:T(8,128)(2,1)} custom-call(bf16[8,4,64,384]{3,2,1,0:T(8,128)(2,1)} %copy-done, bf16[8,2,64,384]{3,2,1,0:T(8,128)(2,1)} %copy-done.2, bf16[8,64,384]{2,1,0:T(8,128)(2,1)} %copy-done.9, bf16[8,64,384]{2,1,0:T(8,128)(2,1)} %copy-done.10), custom_call_target="tpu_custom_call" | custom-call | tf_op jit(solution)/shard_map/latent_attention/pallas_call | solution.py:187
  273.3 4.5 %cross_attention.2 = (bf16[8,2,64,384]{3,2,1,0:T(8,128)(2,1)}, f32[2,64,384]{2,1,0:T(8,128)}) custom-call(bf16[8,64,384]{2,1,0:T(8,128)(2,1)} %latent_attention.2.so_ref, bf16[8,4,64,384]{3,2,1,0:T(8,128)(2,1)} %copy-done, bf16[2,64,384]{2,1,0:T(8,128)(2,1)} %pad_maximum_fusion.2.context_ref), custom_call_target="tpu_custom_call" | custom-call | tf_op jit(solution)/shard_map/cross_attention/pallas_call | solution.py:247
  277.8 4.5 %cross_attention.3 = (bf16[8,2,64,384]{3,2,1,0:T(8,128)(2,1)}, bf16[2,64,384]{2,1,0:T(8,128)(2,1)}) custom-call(bf16[8,64,384]{2,1,0:T(8,128)(2,1)} %latent_attention.3.so_ref, bf16[8,4,64,384]{3,2,1,0:T(8,128)(2,1)} %copy-done, bf16[2,64,384]{2,1,0:T(8,128)(2,1)} %pad_maximum_fusion.2.context_ref, f32[2,64,384]{2,1,0:T(8,128)} %get-tuple-element.10.refs_0_), custom_call_target="tpu_custom_call" | custom-call | tf_op jit(solution)/shard_map/cross_attention/pallas_call | solution.py:247
  282.3 26.6 %all_to_all.35 = bf16[8,2,64,384]{3,2,1,0:T(8,128)(2,1)} all-to-all(bf16[8,2,64,384]{3,2,1,0:T(8,128)(2,1)} %get-tuple-element.11), channel_id=1, replica_groups={{0,1,2,3,4,5,6,7},{8,9,10,11,12,13,14,15},{16,17,18,19,20,21,22,23},{24..., dimensions={0} | all-to-all | bytes 1572864 | tf_op jit(solution)/shard_map/all_to_all | solution.py:83
  308.9 4.9 %all-to-all-start.4 = ((bf16[8,2,64,384]{3,2,1,0:T(8,128)(2,1)}), bf16[8,2,64,384]{3,2,1,0:T(8,128)(2,1)S(1)}, u32[]{:S(2)}, u32[]{:S(2)}) async-start(bf16[8,2,64,384]{3,2,1,0:T(8,128)(2,1)} %get-tuple-element.9), calls=%async_computation.4 | async-start | bytes 1572864 | tf_op jit(solution)/shard_map/all_to_all | solution.py:83
  314.5 4.4 %collective-permute-start.15 = (bf16[2,64,192]{2,1,0:T(8,128)(2,1)S(1)}, bf16[2,64,192]{2,1,0:T(8,128)(2,1)S(1)}, u32[]{:S(2)}, u32[]{:S(2)}) collective-permute-start(bf16[2,64,192]{2,1,0:T(8,128)(2,1)S(1)} %get-tuple-element.28), channel_id=1, source_target_pairs={{0,1},{1,9},{2,3},{3,11},{4,5},{5,13},{6,7},{7,15},{8,0},{9,8},{10... | collective-permute-start | bytes 147464 | tf_op jit(solution)/shard_map/ppermute | solution.py:274
  318.9 11.4 %collective-permute-done.15 = bf16[2,64,192]{2,1,0:T(8,128)(2,1)S(1)} collective-permute-done((bf16[2,64,192]{2,1,0:T(8,128)(2,1)S(1)}, bf16[2,64,192]{2,1,0:T(8,128)(2,1)S(1)}, u32[]{:S(2)}, u32[]{:S(2)}) %collective-permute-start.15) | collective-permute-done | bytes 49184 | tf_op jit(solution)/shard_map/ppermute | solution.py:274
  331.0 0.9 copy-done.4
  331.9 2.3 from_blocks.1
  (69 shorter events, 11.3 us)
Async XLA Ops:
  1.5 19.2 %collective-permute-start.2 = (bf16[2,20,512]{2,0,1:T(2,128)(2,1)S(1)}, bf16[2,20,512]{2,0,1:T(2,128)(2,1)S(1)}, u32[]{:S(2)}, u32[]{:S(2)}) collective-permute-start(bf16[2,20,512]{2,0,1:T(2,128)(2,1)S(1)} %get-tuple-element.30), channel_id=1, source_target_pairs={{0,8},{1,9},{2,10},{3,11},{4,12},{5,13},{6,14},{7,15},{8,0},{9,1},... | collective-permute-start | bytes 122888 | tf_op jit(solution)/shard_map/ppermute | solution.py:92
  17.3 39.0 %collective-permute-start.7 = (bf16[1,512,192]{1,2,0:T(8,128)(2,1)}, bf16[1,512,192]{1,2,0:T(8,128)(2,1)S(1)}, u32[]{:S(2)}, u32[]{:S(2)}) collective-permute-start(bf16[1,512,192]{1,2,0:T(8,128)(2,1)} %bitcast.85), channel_id=1, source_target_pairs={{0,32},{16,48},{32,0},{48,16},{64,96},{80,112},{96,64},{112,80},{1... | collective-permute-start | bytes 589832 | tf_op jit(solution)/shard_map/ppermute | solution.py:118
  21.7 9.9 %all-to-all-start.2 = ((bf16[8,2,2,20,128]{4,2,3,1,0:T(2,128)(2,1)}), bf16[8,2,2,20,128]{4,2,3,1,0:T(2,128)(2,1)S(1)}, u32[]{:S(2)}, u32[]{:S(2)}) async-start(bf16[8,2,2,20,128]{4,2,3,1,0:T(2,128)(2,1)} %bitcast.12), calls=%async_computation.2 | async-start | bytes 327680 | tf_op jit(solution)/shard_map/all_to_all | solution.py:83
  31.6 35.7 %all-to-all-start.1 = ((bf16[8,2,64,384]{3,2,1,0:T(8,128)(2,1)}), bf16[8,2,64,384]{3,2,1,0:T(8,128)(2,1)S(1)}, u32[]{:S(2)}, u32[]{:S(2)}) async-start(bf16[8,2,64,384]{3,2,1,0:T(8,128)(2,1)} %bitcast.78), calls=%async_computation.1 | async-start | bytes 1572864 | tf_op jit(solution)/shard_map/all_to_all | solution.py:83
  37.3 19.0 %copy-start.5 = (bf16[512,192]{0,1:T(8,128)(2,1)S(1)}, bf16[512,192]{0,1:T(8,128)(2,1)}, u32[]{:S(2)}) copy-start(bf16[512,192]{0,1:T(8,128)(2,1)} %param.9) | copy-start | bytes 589828
  38.1 14.1 %collective-permute-start.3 = (bf16[64,512]{1,0:T(8,128)(2,1)S(1)}, bf16[64,512]{1,0:T(8,128)(2,1)S(1)}, u32[]{:S(2)}, u32[]{:S(2)}) collective-permute-start(bf16[64,512]{1,0:T(8,128)(2,1)S(1)} %reshape.123), channel_id=1, source_target_pairs={{0,64},{16,80},{32,96},{48,112},{64,0},{80,16},{96,32},{112,48},{1... | collective-permute-start | bytes 196616 | tf_op jit(solution)/shard_map/ppermute | solution.py:124
  52.8 19.3 %collective-permute-start.4 = (bf16[128,512]{1,0:T(8,128)(2,1)}, bf16[128,512]{1,0:T(8,128)(2,1)S(1)}, u32[]{:S(2)}, u32[]{:S(2)}) collective-permute-start(bf16[128,512]{1,0:T(8,128)(2,1)} %get-tuple-element.31), channel_id=1, source_target_pairs={{0,128},{16,144},{32,160},{48,176},{64,192},{80,208},{96,224},{112... | collective-permute-start | bytes 393224 | tf_op jit(solution)/shard_map/ppermute | solution.py:127
  56.4 17.1 %collective-permute-start.8 = (bf16[2,512,192]{1,2,0:T(8,128)(2,1)S(1)}, bf16[2,512,192]{1,2,0:T(8,128)(2,1)S(1)}, u32[]{:S(2)}, u32[]{:S(2)}) collective-permute-start(bf16[2,512,192]{1,2,0:T(8,128)(2,1)S(1)} %pad_maximum_fusion.1), channel_id=1, source_target_pairs={{0,16},{16,0},{32,48},{48,32},{64,80},{80,64},{96,112},{112,96},{1... | collective-permute-start | bytes 1179656 | tf_op jit(solution)/shard_map/ppermute | solution.py:118
  58.3 13.9 %collective-permute-start.5 = (bf16[128,512]{1,0:T(8,128)(2,1)}, bf16[128,512]{1,0:T(8,128)(2,1)}, u32[]{:S(2)}, u32[]{:S(2)}) collective-permute-start(bf16[128,512]{1,0:T(8,128)(2,1)} %get-tuple-element.31), channel_id=1, source_target_pairs={{0,256},{16,272},{32,288},{48,304},{64,320},{80,336},{96,352},{112... | collective-permute-start | bytes 393224 | tf_op jit(solution)/shard_map/ppermute | solution.py:127
  65.2 8.3 %collective-permute-start.6 = (bf16[128,512]{1,0:T(8,128)(2,1)}, bf16[128,512]{1,0:T(8,128)(2,1)S(1)}, u32[]{:S(2)}, u32[]{:S(2)}) collective-permute-start(bf16[128,512]{1,0:T(8,128)(2,1)} %get-tuple-element.31), channel_id=1, source_target_pairs={{0,384},{16,400},{32,416},{48,432},{64,448},{80,464},{96,480},{112... | collective-permute-start | bytes 393224 | tf_op jit(solution)/shard_map/ppermute | solution.py:127
  67.3 41.9 %copy-start.1 = (bf16[8,2,64,384]{3,2,1,0:T(8,128)(2,1)}, bf16[8,2,64,384]{3,2,1,0:T(8,128)(2,1)S(1)}, u32[]{:S(2)}) copy-start(bf16[8,2,64,384]{3,2,1,0:T(8,128)(2,1)S(1)} %all-to-all-done.1.near_ref) | copy-start | bytes 2359300
  67.3 16.5 %all-to-all-start.5 = ((bf16[8,2,64,384]{3,2,1,0:T(8,128)(2,1)}), bf16[8,2,64,384]{3,2,1,0:T(8,128)(2,1)S(1)}, u32[]{:S(2)}, u32[]{:S(2)}) async-start(bf16[8,2,64,384]{3,2,1,0:T(8,128)(2,1)} %bitcast.79), calls=%async_computation.5 | async-start | bytes 1572864 | tf_op jit(solution)/shard_map/all_to_all | solution.py:83
  73.4 0.8 copy-start.6
  83.8 54.1 %copy-start.2 = (bf16[8,2,64,384]{3,2,1,0:T(8,128)(2,1)}, bf16[8,2,64,384]{3,2,1,0:T(8,128)(2,1)S(1)}, u32[]{:S(2)}) copy-start(bf16[8,2,64,384]{3,2,1,0:T(8,128)(2,1)S(1)} %all-to-all-done.5.near_ref) | copy-start | bytes 2359300
  83.8 19.4 %all-to-all-start.3 = ((bf16[8,2,2,64,192]{4,3,2,1,0:T(8,128)(2,1)}), bf16[8,2,2,64,192]{4,3,2,1,0:T(8,128)(2,1)S(1)}, u32[]{:S(2)}, u32[]{:S(2)}) async-start(bf16[8,2,2,64,192]{4,3,2,1,0:T(8,128)(2,1)} %bitcast.75), calls=%async_computation.3 | async-start | bytes 2097152 | tf_op jit(solution)/shard_map/all_to_all | solution.py:83
  103.3 1.0 copy-start.3
  104.3 69.4 %all-to-all-start = ((bf16[8,4,64,384]{3,2,1,0:T(8,128)(2,1)}), bf16[8,4,64,384]{3,2,1,0:T(8,128)(2,1)S(1)}, u32[]{:S(2)}, u32[]{:S(2)}) async-start(bf16[8,4,64,384]{3,2,1,0:T(8,128)(2,1)} %bitcast.72), calls=%async_computation | async-start | bytes 3145728 | tf_op jit(solution)/shard_map/all_to_all | solution.py:83
  110.2 59.4 %collective-permute-start = (bf16[8,64,384]{2,1,0:T(8,128)(2,1)}, bf16[8,64,384]{2,1,0:T(8,128)(2,1)S(1)}, u32[]{:S(2)}, u32[]{:S(2)}) collective-permute-start(bf16[8,64,384]{2,1,0:T(8,128)(2,1)} %get-tuple-element.20), channel_id=1, source_target_pairs={{0,8},{1,9},{2,10},{3,11},{4,12},{5,13},{6,14},{7,15},{8,0},{9,1},... | collective-permute-start | bytes 1179656 | tf_op jit(solution)/shard_map/ppermute | solution.py:286
  121.9 51.8 %collective-permute-start.1 = (bf16[8,64,384]{2,1,0:T(8,128)(2,1)}, bf16[8,64,384]{2,1,0:T(8,128)(2,1)S(1)}, u32[]{:S(2)}, u32[]{:S(2)}) collective-permute-start(bf16[8,64,384]{2,1,0:T(8,128)(2,1)} %get-tuple-element.19), channel_id=1, source_target_pairs={{0,8},{1,9},{2,10},{3,11},{4,12},{5,13},{6,14},{7,15},{8,0},{9,1},... | collective-permute-start | bytes 1179656 | tf_op jit(solution)/shard_map/ppermute | solution.py:286
  126.1 42.7 %collective-permute-start.9 = (bf16[2,2,64,192]{3,2,1,0:T(8,128)(2,1)S(1)}, bf16[2,2,64,192]{3,2,1,0:T(8,128)(2,1)S(1)}, u32[]{:S(2)}, u32[]{:S(2)}) collective-permute-start(bf16[2,2,64,192]{3,2,1,0:T(8,128)(2,1)S(1)} %reduce_sum.22), channel_id=1, source_target_pairs={{0,8},{1,9},{2,10},{3,11},{4,12},{5,13},{6,14},{7,15},{8,0},{9,1},... | collective-permute-start | bytes 294920 | tf_op jit(solution)/shard_map/ppermute | solution.py:140
  138.9 51.5 %collective-permute-start.12 = (bf16[8,64,384]{2,1,0:T(8,128)(2,1)}, bf16[8,64,384]{2,1,0:T(8,128)(2,1)S(1)}, u32[]{:S(2)}, u32[]{:S(2)}) collective-permute-start(bf16[8,64,384]{2,1,0:T(8,128)(2,1)} %get-tuple-element.18), channel_id=1, source_target_pairs={{0,8},{1,9},{2,10},{3,11},{4,12},{5,13},{6,14},{7,15},{8,0},{9,1},... | collective-permute-start | bytes 1179656 | tf_op jit(solution)/shard_map/ppermute | solution.py:286
  141.7 123.6 %collective-permute-start.13 = (bf16[8,64,384]{2,1,0:T(8,128)(2,1)}, bf16[8,64,384]{2,1,0:T(8,128)(2,1)S(1)}, u32[]{:S(2)}, u32[]{:S(2)}) collective-permute-start(bf16[8,64,384]{2,1,0:T(8,128)(2,1)} %get-tuple-element.17), channel_id=1, source_target_pairs={{0,8},{1,9},{2,10},{3,11},{4,12},{5,13},{6,14},{7,15},{8,0},{9,1},... | collective-permute-start | bytes 1179656 | tf_op jit(solution)/shard_map/ppermute | solution.py:286
  168.9 103.5 %collective-permute-start.10 = (bf16[2,64,192]{2,1,0:T(8,128)(2,1)S(1)}, bf16[2,64,192]{2,1,0:T(8,128)(2,1)S(1)}, u32[]{:S(2)}, u32[]{:S(2)}) collective-permute-start(bf16[2,64,192]{2,1,0:T(8,128)(2,1)S(1)} %get-tuple-element.25), channel_id=1, source_target_pairs={{0,0},{1,128},{2,2},{3,130},{4,64},{5,192},{6,66},{7,194},{8,8},{9... | collective-permute-start | bytes 147464 | tf_op jit(solution)/shard_map/ppermute | solution.py:153
  169.6 4.1 %copy-start.7 = (bf16[8,64,384]{2,1,0:T(8,128)(2,1)}, bf16[8,64,384]{2,1,0:T(8,128)(2,1)S(1)}, u32[]{:S(2)}) copy-start(bf16[8,64,384]{2,1,0:T(8,128)(2,1)S(1)} %collective-permute-done.fk_ref) | copy-start | bytes 1179652
  169.6 102.9 %collective-permute-start.11 = (bf16[2,64,192]{2,1,0:T(8,128)(2,1)S(1)}, bf16[2,64,192]{2,1,0:T(8,128)(2,1)S(1)}, u32[]{:S(2)}, u32[]{:S(2)}) collective-permute-start(bf16[2,64,192]{2,1,0:T(8,128)(2,1)S(1)} %get-tuple-element.26), channel_id=1, source_target_pairs={{0,256},{1,384},{2,258},{3,386},{4,320},{5,448},{6,322},{7,450},{8... | collective-permute-start | bytes 147464 | tf_op jit(solution)/shard_map/ppermute | solution.py:153
  173.7 0.7 copy-start.8
  174.4 1.2 copy-start
  190.3 74.9 %copy-start.9 = (bf16[8,64,384]{2,1,0:T(8,128)(2,1)}, bf16[8,64,384]{2,1,0:T(8,128)(2,1)S(1)}, u32[]{:S(2)}) copy-start(bf16[8,64,384]{2,1,0:T(8,128)(2,1)S(1)} %collective-permute-done.12.fk_ref) | copy-start | bytes 1179652
  265.3 0.7 copy-start.10
  282.3 31.5 %copy-start.11 = (bf16[2,64,384]{2,1,0:T(8,128)(2,1)S(1)}, bf16[2,64,384]{2,1,0:T(8,128)(2,1)}, u32[]{:S(2)}) copy-start(bf16[2,64,384]{2,1,0:T(8,128)(2,1)} %get-tuple-element.14) | copy-start | bytes 294916
  308.9 22.2 %all-to-all-start.4 = ((bf16[8,2,64,384]{3,2,1,0:T(8,128)(2,1)}), bf16[8,2,64,384]{3,2,1,0:T(8,128)(2,1)S(1)}, u32[]{:S(2)}, u32[]{:S(2)}) async-start(bf16[8,2,64,384]{3,2,1,0:T(8,128)(2,1)} %get-tuple-element.9), calls=%async_computation.4 | async-start | bytes 1572864 | tf_op jit(solution)/shard_map/all_to_all | solution.py:83
  313.9 5.1 %collective-permute-start.14 = (bf16[2,64,192]{2,1,0:T(8,128)(2,1)S(1)}, bf16[2,64,192]{2,1,0:T(8,128)(2,1)S(1)}, u32[]{:S(2)}, u32[]{:S(2)}) collective-permute-start(bf16[2,64,192]{2,1,0:T(8,128)(2,1)S(1)} %get-tuple-element.27), channel_id=1, source_target_pairs={{0,0},{1,8},{2,2},{3,10},{4,4},{5,12},{6,6},{7,14},{8,1},{9,9},{10... | collective-permute-start | bytes 147464 | tf_op jit(solution)/shard_map/ppermute | solution.py:273
  314.5 15.9 %collective-permute-start.15 = (bf16[2,64,192]{2,1,0:T(8,128)(2,1)S(1)}, bf16[2,64,192]{2,1,0:T(8,128)(2,1)S(1)}, u32[]{:S(2)}, u32[]{:S(2)}) collective-permute-start(bf16[2,64,192]{2,1,0:T(8,128)(2,1)S(1)} %get-tuple-element.28), channel_id=1, source_target_pairs={{0,1},{1,9},{2,3},{3,11},{4,5},{5,13},{6,7},{7,15},{8,0},{9,8},{10... | collective-permute-start | bytes 147464 | tf_op jit(solution)/shard_map/ppermute | solution.py:274
  331.0 0.9 copy-start.4

commit v4 on v2

--- a/solution.py
+++ b/solution.py
@@ -151,12 +151,12 @@
     return jnp.concatenate([first, second], axis=2)
 
 
-def attention_kernel(q_ref, near_ref, far_ref, o_ref):
+def attention_kernel(q_ref, near_ref, fk_ref, fv_ref, o_ref):
     half = LATENT_TOKENS // 2
     near_k = near_ref[:, 0].reshape(half, HEAD_SIZE)
-    far_k = far_ref[:, 0].reshape(half, HEAD_SIZE)
+    far_k = fk_ref[...].reshape(half, HEAD_SIZE)
     near_v = near_ref[:, 1].reshape(half, HEAD_SIZE)
-    far_v = far_ref[:, 1].reshape(half, HEAD_SIZE)
+    far_v = fv_ref[...].reshape(half, HEAD_SIZE)
     transposed = (((1,), (1,)), ((), ()))
     for part in range(4):
         q = q_ref[2 * part : 2 * part + 2, 0].reshape(half // 4, HEAD_SIZE)
@@ -172,21 +172,22 @@
         o_ref[2 * part : 2 * part + 2] = out.reshape(2, half // 8, HEAD_SIZE)
 
 
-def attention(sample, query_gradient, near, far):
+def attention(sample, query_gradient, near, far_k, far_v):
     rows = near.shape[2]
-    pair_spec = pl.BlockSpec((8, 2, rows, HEAD_SIZE), lambda n: (0, 0, 0, n))
+    spec = pl.BlockSpec((8, rows, HEAD_SIZE), lambda n: (0, 0, n))
     return pl.pallas_call(
         attention_kernel,
         grid=(3,),
         in_specs=[
             pl.BlockSpec((8, 1, rows, HEAD_SIZE), lambda n: (0, sample, 0, n)),
-            pair_spec,
-            pair_spec,
+            pl.BlockSpec((8, 2, rows, HEAD_SIZE), lambda n: (0, 0, 0, n)),
+            spec,
+            spec,
         ],
-        out_specs=pl.BlockSpec((8, rows, HEAD_SIZE), lambda n: (0, 0, n)),
+        out_specs=spec,
         out_shape=jax.ShapeDtypeStruct((8, rows, BLOCK), jnp.bfloat16),
         name="latent_attention",
-    )(query_gradient, near, far)
+    )(query_gradient, near, far_k, far_v)
 
 
 def cross_kernel(so_ref, g_ref, context_ref, *refs):
@@ -270,17 +271,19 @@
 
 
 def layer(llm_query, llm_kv, connector, query, key, value, cotangent):
-    near, far = [], []
-    for s in range(SAMPLE_COUNT):
-        near.append(exchange(to_blocks(s, 1, key, value)))
-        far.append(lax.ppermute(near[s], "tp", SWAP_HALF))
+    swap = lambda x: lax.ppermute(x, "tp", SWAP_HALF)
+    raw = swap(key[:1])
+    near = [exchange(to_blocks(s, 1, key, value)) for s in range(SAMPLE_COUNT)]
+    far = [[None, swap(near[0][:, 1])]]
+    far.append([swap(near[1][:, i]) for i in range(2)])
+    far[0][0] = exchange(to_blocks(0, 1, raw))[:, 0]
     columns = gather_run(connector)
     hidden = llm_hidden(llm_query, llm_kv)
     query_gradient = exchange(to_blocks(0, 2, query, cotangent))
     context = context_tokens(gather_ring(hidden), columns)
     out, carry = [], ()
     for s in range(SAMPLE_COUNT):
-        so = attention(s, query_gradient, near[s], far[s])
+        so = attention(s, query_gradient, near[s], *far[s])
         result, partial = cross(s, so, query_gradient, context, carry)
         carry = (partial,)
         out.append(exchange(result))

time: 348 us -> 338 us (0.971)
  the two profiles are of different devices: /device:TPU:178 before, /device:TPU:162 now
where the time goes in v4:
time: 338 us; the launch traced here: 337 us
  starting transfers between devices  141 us (42%)
  waiting for transfers between devices  123 us (36%)
  Pallas kernels  32.3 us (10%)
  blocking collectives  17 us (5%)
  local copies, waits for them, and re-layouts  13.8 us (4%)
  other arithmetic  5.75 us (2%)
    ppermute x1, waiting for transfers between devices, context_tokens(): there = lax.ppermute(mine, 'tp', SWAP_HALF)  76.8 us
    ppermute x3, starting transfers between devices, gather_run(): got = jnp.concatenate([got, lax.ppermute(got, 'fsdp', pairs)])  37.4 us
    all_to_all x7, starting transfers between devices, exchange(): lax.all_to_all(x, 'tp', split_axis=0, concat_axis=0, axis_index_groups=HA...  34.1 us
    ppermute x3, waiting for transfers between devices, gather_run(): got = jnp.concatenate([got, lax.ppermute(got, 'fsdp', pairs)])  25.2 us
    ppermute x4, starting transfers between devices, layer(): swap = lambda x: lax.ppermute(x, 'tp', SWAP_HALF)  23.3 us
    all_to_all x1, blocking collectives, exchange(): lax.all_to_all(x, 'tp', split_axis=0, concat_axis=0, axis_index_groups=HA...  17 us
    all_to_all x7, waiting for transfers between devices, exchange(): lax.all_to_all(x, 'tp', split_axis=0, concat_axis=0, axis_index_groups=HA...  13.3 us
    pallas_call x2, Pallas kernels, attention(): pl.pallas_call(attention_kernel, grid=(3,), in_specs=[pl.BlockSpec((8, 1,...  12.9 us
  transfers between devices with their start and end apart: 23, of which 7 were waited for; matrix products, arithmetic and copies ran while one was open for 5% of the time, Pallas kernels for 6%

profile of v4, /device:TPU:162, one launch (start us, length us, event | category | flops | bytes accessed | tf_op | source)
XLA Modules:
  0.0 336.6 jit_solution(12883800783232360974)
XLA Ops:
  1.5 10.0 %collective-permute-start.2 = (bf16[2,20,512]{2,0,1:T(2,128)(2,1)S(1)}, bf16[2,20,512]{2,0,1:T(2,128)(2,1)S(1)}, u32[]{:S(2)}, u32[]{:S(2)}) collective-permute-start(bf16[2,20,512]{2,0,1:T(2,128)(2,1)S(1)} %get-tuple-element.28), channel_id=1, source_target_pairs={{0,8},{1,9},{2,10},{3,11},{4,12},{5,13},{6,14},{7,15},{8,0},{9,1},... | collective-permute-start | bytes 122888 | tf_op jit(solution)/shard_map/ppermute | solution.py:92
  11.5 5.5 %collective-permute-start.6 = (bf16[1,512,192]{1,2,0:T(8,128)(2,1)}, bf16[1,512,192]{1,2,0:T(8,128)(2,1)S(1)}, u32[]{:S(2)}, u32[]{:S(2)}) collective-permute-start(bf16[1,512,192]{1,2,0:T(8,128)(2,1)} %bitcast.86), channel_id=1, source_target_pairs={{0,64},{16,80},{32,96},{48,112},{64,0},{80,16},{96,32},{112,48},{1... | collective-permute-start | bytes 589832 | tf_op jit(solution)/shard_map/ppermute | solution.py:118
  17.0 1.8 slice_bitcast_fusion.3
  18.8 1.9 collective-permute-start
  21.7 4.8 %all-to-all-start.3 = ((bf16[8,2,2,20,128]{4,2,3,1,0:T(2,128)(2,1)}), bf16[8,2,2,20,128]{4,2,3,1,0:T(2,128)(2,1)S(1)}, u32[]{:S(2)}, u32[]{:S(2)}) async-start(bf16[8,2,2,20,128]{4,2,3,1,0:T(2,128)(2,1)} %bitcast.15), calls=%async_computation.3 | async-start | bytes 327680 | tf_op jit(solution)/shard_map/all_to_all | solution.py:83
  26.6 2.0 to_blocks.5
  28.6 18.7 %collective-permute-done.6 = bf16[1,512,192]{1,2,0:T(8,128)(2,1)S(1)} collective-permute-done((bf16[1,512,192]{1,2,0:T(8,128)(2,1)}, bf16[1,512,192]{1,2,0:T(8,128)(2,1)S(1)}, u32[]{:S(2)}, u32[]{:S(2)}) %collective-permute-start.6) | collective-permute-done | bytes 196640 | tf_op jit(solution)/shard_map/ppermute | solution.py:118
  47.4 26.5 %collective-permute-start.7 = (bf16[2,512,192]{1,2,0:T(8,128)(2,1)S(1)}, bf16[2,512,192]{1,2,0:T(8,128)(2,1)S(1)}, u32[]{:S(2)}, u32[]{:S(2)}) collective-permute-start(bf16[2,512,192]{1,2,0:T(8,128)(2,1)S(1)} %pad_maximum_fusion.2), channel_id=1, source_target_pairs={{0,32},{16,48},{32,0},{48,16},{64,96},{80,112},{96,64},{112,80},{1... | collective-permute-start | bytes 1179656 | tf_op jit(solution)/shard_map/ppermute | solution.py:118
  73.9 4.8 %all-to-all-start.1 = ((bf16[8,2,64,384]{3,2,1,0:T(8,128)(2,1)}), bf16[8,2,64,384]{3,2,1,0:T(8,128)(2,1)S(1)}, u32[]{:S(2)}, u32[]{:S(2)}) async-start(bf16[8,2,64,384]{3,2,1,0:T(8,128)(2,1)} %bitcast.83), calls=%async_computation.1 | async-start | bytes 1572864 | tf_op jit(solution)/shard_map/all_to_all | solution.py:83
  78.8 6.5 %collective-permute-done.7 = bf16[2,512,192]{1,2,0:T(8,128)(2,1)S(1)} collective-permute-done((bf16[2,512,192]{1,2,0:T(8,128)(2,1)S(1)}, bf16[2,512,192]{1,2,0:T(8,128)(2,1)S(1)}, u32[]{:S(2)}, u32[]{:S(2)}) %collective-permute-start.7) | collective-permute-done | bytes 393248 | tf_op jit(solution)/shard_map/ppermute | solution.py:118
  85.4 5.5 %collective-permute-start.8 = (bf16[4,512,192]{1,2,0:T(8,128)(2,1)S(1)}, bf16[4,512,192]{1,2,0:T(8,128)(2,1)}, u32[]{:S(2)}, u32[]{:S(2)}) collective-permute-start(bf16[4,512,192]{1,2,0:T(8,128)(2,1)S(1)} %pad_maximum_fusion.1), channel_id=1, source_target_pairs={{0,16},{16,0},{32,48},{48,32},{64,80},{80,64},{96,112},{112,96},{1... | collective-permute-start | bytes 2359304 | tf_op jit(solution)/shard_map/ppermute | solution.py:118
  90.9 2.0 to_blocks.7
  93.7 4.8 %all-to-all-start.6 = ((bf16[8,2,64,384]{3,2,1,0:T(8,128)(2,1)}), bf16[8,2,64,384]{3,2,1,0:T(8,128)(2,1)S(1)}, u32[]{:S(2)}, u32[]{:S(2)}) async-start(bf16[8,2,64,384]{3,2,1,0:T(8,128)(2,1)} %bitcast.82), calls=%async_computation.6 | async-start | bytes 1572864 | tf_op jit(solution)/shard_map/all_to_all | solution.py:83
  99.4 1.1 fusion.15
  101.5 3.5 %collective-permute-start.3 = (bf16[64,512]{1,0:T(8,128)(2,1)}, bf16[64,512]{1,0:T(8,128)(2,1)}, u32[]{:S(2)}, u32[]{:S(2)}) collective-permute-start(bf16[64,512]{1,0:T(8,128)(2,1)} %reshape.128), channel_id=1, source_target_pairs={{0,128},{16,144},{32,160},{48,176},{64,192},{80,208},{96,224},{112... | collective-permute-start | bytes 196616 | tf_op jit(solution)/shard_map/ppermute | solution.py:126
  105.0 4.8 %collective-permute-start.4 = (bf16[64,512]{1,0:T(8,128)(2,1)}, bf16[64,512]{1,0:T(8,128)(2,1)}, u32[]{:S(2)}, u32[]{:S(2)}) collective-permute-start(bf16[64,512]{1,0:T(8,128)(2,1)} %reshape.128), channel_id=1, source_target_pairs={{0,256},{16,272},{32,288},{48,304},{64,320},{80,336},{96,352},{112... | collective-permute-start | bytes 196616 | tf_op jit(solution)/shard_map/ppermute | solution.py:126
  109.8 2.1 collective-permute-start.5
  112.0 1.7 to_blocks.6
  113.7 4.8 %all-to-all-start.2 = ((bf16[8,1,64,384]{3,2,1,0:T(8,128)(2,1)}), bf16[8,1,64,384]{3,2,1,0:T(8,128)(2,1)}, u32[]{:S(2)}, u32[]{:S(2)}) async-start(bf16[8,1,64,384]{3,2,1,0:T(8,128)(2,1)} %bitcast.90), calls=%async_computation.2 | async-start | bytes 786432 | tf_op jit(solution)/shard_map/all_to_all | solution.py:83
  118.5 1.4 pad_maximum_fusion
  119.9 1.5 fusion.3
  121.5 1.0 convert_element_type.31
  122.5 1.4 copy.26
  123.9 1.1 copy.27
  125.0 1.1 all-to-all-done.2
  126.1 4.9 %all-to-all-start.4 = ((bf16[8,2,2,64,192]{4,3,2,1,0:T(8,128)(2,1)}), bf16[8,2,2,64,192]{4,3,2,1,0:T(8,128)(2,1)S(1)}, u32[]{:S(2)}, u32[]{:S(2)}) async-start(bf16[8,2,2,64,192]{4,3,2,1,0:T(8,128)(2,1)} %bitcast.79), calls=%async_computation.4 | async-start | bytes 2097152 | tf_op jit(solution)/shard_map/all_to_all | solution.py:83
  131.0 2.3 to_blocks.4
  133.3 12.2 %all-to-all-done.4 = bf16[8,2,2,64,192]{4,3,2,1,0:T(8,128)(2,1)S(1)} async-done(((bf16[8,2,2,64,192]{4,3,2,1,0:T(8,128)(2,1)}), bf16[8,2,2,64,192]{4,3,2,1,0:T(8,128)(2,1)S(1)}, u32[]{:S(2)}, u32[]{:S(2)}) %all-to-all-start.4) | async-done | bytes 786464 | tf_op jit(solution)/shard_map/all_to_all | solution.py:83
  145.5 1.0 copy-done.3
  146.5 4.9 %all-to-all-start = ((bf16[8,4,64,384]{3,2,1,0:T(8,128)(2,1)}), bf16[8,4,64,384]{3,2,1,0:T(8,128)(2,1)S(1)}, u32[]{:S(2)}, u32[]{:S(2)}) async-start(bf16[8,4,64,384]{3,2,1,0:T(8,128)(2,1)} %bitcast.73), calls=%async_computation | async-start | bytes 3145728 | tf_op jit(solution)/shard_map/all_to_all | solution.py:83
  151.5 6.9 %collective-permute-start.1 = (bf16[8,64,384]{2,1,0:T(8,128)(2,1)S(1)}, bf16[8,64,384]{2,1,0:T(8,128)(2,1)S(1)}, u32[]{:S(2)}, u32[]{:S(2)}) collective-permute-start(bf16[8,64,384]{2,1,0:T(8,128)(2,1)S(1)} %slice_bitcast_fusion.2), channel_id=1, source_target_pairs={{0,8},{1,9},{2,10},{3,11},{4,12},{5,13},{6,14},{7,15},{8,0},{9,1},... | collective-permute-start | bytes 1179656 | tf_op jit(solution)/shard_map/ppermute | solution.py:274
  158.4 1.4 reduce_sum.22
  159.8 7.7 %collective-permute-start.9 = (bf16[2,2,64,192]{3,2,1,0:T(8,128)(2,1)S(1)}, bf16[2,2,64,192]{3,2,1,0:T(8,128)(2,1)S(1)}, u32[]{:S(2)}, u32[]{:S(2)}) collective-permute-start(bf16[2,2,64,192]{3,2,1,0:T(8,128)(2,1)S(1)} %reduce_sum.22), channel_id=1, source_target_pairs={{0,8},{1,9},{2,10},{3,11},{4,12},{5,13},{6,14},{7,15},{8,0},{9,1},... | collective-permute-start | bytes 294920 | tf_op jit(solution)/shard_map/ppermute | solution.py:139
  167.5 1.0 slice_bitcast_fusion
  168.5 6.8 %collective-permute-start.12 = (bf16[8,64,384]{2,1,0:T(8,128)(2,1)}, bf16[8,64,384]{2,1,0:T(8,128)(2,1)S(1)}, u32[]{:S(2)}, u32[]{:S(2)}) collective-permute-start(bf16[8,64,384]{2,1,0:T(8,128)(2,1)} %get-tuple-element.18), channel_id=1, source_target_pairs={{0,8},{1,9},{2,10},{3,11},{4,12},{5,13},{6,14},{7,15},{8,0},{9,1},... | collective-permute-start | bytes 1179656 | tf_op jit(solution)/shard_map/ppermute | solution.py:274
  175.3 7.7 %collective-permute-start.13 = (bf16[8,64,384]{2,1,0:T(8,128)(2,1)}, bf16[8,64,384]{2,1,0:T(8,128)(2,1)S(1)}, u32[]{:S(2)}, u32[]{:S(2)}) collective-permute-start(bf16[8,64,384]{2,1,0:T(8,128)(2,1)} %get-tuple-element.17), channel_id=1, source_target_pairs={{0,8},{1,9},{2,10},{3,11},{4,12},{5,13},{6,14},{7,15},{8,0},{9,1},... | collective-permute-start | bytes 1179656 | tf_op jit(solution)/shard_map/ppermute | solution.py:274
  183.0 76.8 %collective-permute-done.9 = bf16[2,2,64,192]{3,2,1,0:T(8,128)(2,1)S(1)} collective-permute-done((bf16[2,2,64,192]{3,2,1,0:T(8,128)(2,1)S(1)}, bf16[2,2,64,192]{3,2,1,0:T(8,128)(2,1)S(1)}, u32[]{:S(2)}, u32[]{:S(2)}) %collective-permute-start.9) | collective-permute-done | bytes 98336 | tf_op jit(solution)/shard_map/ppermute | solution.py:139
  259.9 4.0 %collective-permute-start.10 = (bf16[2,64,192]{2,1,0:T(8,128)(2,1)S(1)}, bf16[2,64,192]{2,1,0:T(8,128)(2,1)S(1)}, u32[]{:S(2)}, u32[]{:S(2)}) collective-permute-start(bf16[2,64,192]{2,1,0:T(8,128)(2,1)S(1)} %get-tuple-element.23), channel_id=1, source_target_pairs={{0,0},{1,128},{2,2},{3,130},{4,4},{5,132},{6,6},{7,134},{8,8},{9,1... | collective-permute-start | bytes 147464 | tf_op jit(solution)/shard_map/ppermute | solution.py:144
  263.9 4.8 %collective-permute-start.11 = (bf16[2,64,192]{2,1,0:T(8,128)(2,1)S(1)}, bf16[2,64,192]{2,1,0:T(8,128)(2,1)S(1)}, u32[]{:S(2)}, u32[]{:S(2)}) collective-permute-start(bf16[2,64,192]{2,1,0:T(8,128)(2,1)S(1)} %get-tuple-element.24), channel_id=1, source_target_pairs={{0,256},{1,384},{2,258},{3,386},{4,260},{5,388},{6,262},{7,390},{8... | collective-permute-start | bytes 147464 | tf_op jit(solution)/shard_map/ppermute | solution.py:144
  270.1 6.4 %latent_attention.2.so_ref = bf16[8,64,384]{2,1,0:T(8,128)(2,1)} custom-call(bf16[8,4,64,384]{3,2,1,0:T(8,128)(2,1)} %copy-done, bf16[8,2,64,384]{3,2,1,0:T(8,128)(2,1)} %copy-done.2, bf16[8,64,384]{2,1,0:T(8,128)(2,1)} %bitcast.9.fk_ref, bf16[8,64,384]{2,1,0:T(8,128)(2,1)} %copy-done.7), custom_call_target="tpu_custom_call" | custom-call | tf_op jit(solution)/shard_map/latent_attention/pallas_call | solution.py:178
  278.0 6.4 %latent_attention.3.so_ref = bf16[8,64,384]{2,1,0:T(8,128)(2,1)} custom-call(bf16[8,4,64,384]{3,2,1,0:T(8,128)(2,1)} %copy-done, bf16[8,2,64,384]{3,2,1,0:T(8,128)(2,1)} %copy-done.1, bf16[8,64,384]{2,1,0:T(8,128)(2,1)} %copy-done.8, bf16[8,64,384]{2,1,0:T(8,128)(2,1)} %copy-done.9), custom_call_target="tpu_custom_call" | custom-call | tf_op jit(solution)/shard_map/latent_attention/pallas_call | solution.py:178
  285.3 4.5 %cross_attention.2 = (bf16[8,2,64,384]{3,2,1,0:T(8,128)(2,1)}, f32[2,64,384]{2,1,0:T(8,128)}) custom-call(bf16[8,64,384]{2,1,0:T(8,128)(2,1)} %latent_attention.2.so_ref, bf16[8,4,64,384]{3,2,1,0:T(8,128)(2,1)} %copy-done, bf16[2,64,384]{2,1,0:T(8,128)(2,1)} %pad_maximum_fusion.3.context_ref), custom_call_target="tpu_custom_call" | custom-call | tf_op jit(solution)/shard_map/cross_attention/pallas_call | solution.py:238
  289.8 4.5 %cross_attention.3 = (bf16[8,2,64,384]{3,2,1,0:T(8,128)(2,1)}, bf16[2,64,384]{2,1,0:T(8,128)(2,1)}) custom-call(bf16[8,64,384]{2,1,0:T(8,128)(2,1)} %latent_attention.3.so_ref, bf16[8,4,64,384]{3,2,1,0:T(8,128)(2,1)} %copy-done, bf16[2,64,384]{2,1,0:T(8,128)(2,1)} %pad_maximum_fusion.3.context_ref, f32[2,64,384]{2,1,0:T(8,128)} %get-tuple-element.10.refs_0_), custom_call_target="tpu_custom_call" | custom-call | tf_op jit(solution)/shard_map/cross_attention/pallas_call | solution.py:238
  294.3 17.0 %all_to_all.40 = bf16[8,2,64,384]{3,2,1,0:T(8,128)(2,1)} all-to-all(bf16[8,2,64,384]{3,2,1,0:T(8,128)(2,1)} %get-tuple-element.11), channel_id=1, replica_groups={{0,1,2,3,4,5,6,7},{8,9,10,11,12,13,14,15},{16,17,18,19,20,21,22,23},{24..., dimensions={0} | all-to-all | bytes 1572864 | tf_op jit(solution)/shard_map/all_to_all | solution.py:83
  311.3 4.9 %all-to-all-start.5 = ((bf16[8,2,64,384]{3,2,1,0:T(8,128)(2,1)}), bf16[8,2,64,384]{3,2,1,0:T(8,128)(2,1)S(1)}, u32[]{:S(2)}, u32[]{:S(2)}) async-start(bf16[8,2,64,384]{3,2,1,0:T(8,128)(2,1)} %get-tuple-element.9), calls=%async_computation.5 | async-start | bytes 1572864 | tf_op jit(solution)/shard_map/all_to_all | solution.py:83
  316.9 8.1 %collective-permute-start.15 = (bf16[2,64,192]{2,1,0:T(8,128)(2,1)S(1)}, bf16[2,64,192]{2,1,0:T(8,128)(2,1)S(1)}, u32[]{:S(2)}, u32[]{:S(2)}) collective-permute-start(bf16[2,64,192]{2,1,0:T(8,128)(2,1)S(1)} %get-tuple-element.26), channel_id=1, source_target_pairs={{0,1},{1,9},{2,3},{3,11},{4,5},{5,13},{6,7},{7,15},{8,0},{9,8},{10... | collective-permute-start | bytes 147464 | tf_op jit(solution)/shard_map/ppermute | solution.py:265
  325.1 7.7 %collective-permute-done.15 = bf16[2,64,192]{2,1,0:T(8,128)(2,1)S(1)} collective-permute-done((bf16[2,64,192]{2,1,0:T(8,128)(2,1)S(1)}, bf16[2,64,192]{2,1,0:T(8,128)(2,1)S(1)}, u32[]{:S(2)}, u32[]{:S(2)}) %collective-permute-start.15) | collective-permute-done | bytes 49184 | tf_op jit(solution)/shard_map/ppermute | solution.py:265
  334.3 2.3 from_blocks.1
  (69 shorter events, 10.7 us)
Async XLA Ops:
  1.5 19.2 %collective-permute-start.2 = (bf16[2,20,512]{2,0,1:T(2,128)(2,1)S(1)}, bf16[2,20,512]{2,0,1:T(2,128)(2,1)S(1)}, u32[]{:S(2)}, u32[]{:S(2)}) collective-permute-start(bf16[2,20,512]{2,0,1:T(2,128)(2,1)S(1)} %get-tuple-element.28), channel_id=1, source_target_pairs={{0,8},{1,9},{2,10},{3,11},{4,12},{5,13},{6,14},{7,15},{8,0},{9,1},... | collective-permute-start | bytes 122888 | tf_op jit(solution)/shard_map/ppermute | solution.py:92
  11.5 35.8 %collective-permute-start.6 = (bf16[1,512,192]{1,2,0:T(8,128)(2,1)}, bf16[1,512,192]{1,2,0:T(8,128)(2,1)S(1)}, u32[]{:S(2)}, u32[]{:S(2)}) collective-permute-start(bf16[1,512,192]{1,2,0:T(8,128)(2,1)} %bitcast.86), channel_id=1, source_target_pairs={{0,64},{16,80},{32,96},{48,112},{64,0},{80,16},{96,32},{112,48},{1... | collective-permute-start | bytes 589832 | tf_op jit(solution)/shard_map/ppermute | solution.py:118
  18.8 93.2 %collective-permute-start = (bf16[1,64,3072]{2,1,0:T(8,128)(2,1)}, bf16[1,64,3072]{2,1,0:T(8,128)(2,1)}, u32[]{:S(2)}, u32[]{:S(2)}) collective-permute-start(bf16[1,64,3072]{2,1,0:T(8,128)(2,1)} %slice_bitcast_fusion.3), channel_id=1, source_target_pairs={{0,8},{1,9},{2,10},{3,11},{4,12},{5,13},{6,14},{7,15},{8,0},{9,1},... | collective-permute-start | bytes 1179656 | tf_op jit(solution)/shard_map/ppermute | solution.py:274
  20.9 26.5 %copy-start.5 = (bf16[512,192]{0,1:T(8,128)(2,1)S(1)}, bf16[512,192]{0,1:T(8,128)(2,1)}, u32[]{:S(2)}) copy-start(bf16[512,192]{0,1:T(8,128)(2,1)} %param.9) | copy-start | bytes 589828
  21.7 52.2 %all-to-all-start.3 = ((bf16[8,2,2,20,128]{4,2,3,1,0:T(2,128)(2,1)}), bf16[8,2,2,20,128]{4,2,3,1,0:T(2,128)(2,1)S(1)}, u32[]{:S(2)}, u32[]{:S(2)}) async-start(bf16[8,2,2,20,128]{4,2,3,1,0:T(2,128)(2,1)} %bitcast.15), calls=%async_computation.3 | async-start | bytes 327680 | tf_op jit(solution)/shard_map/all_to_all | solution.py:83
  47.4 37.9 %collective-permute-start.7 = (bf16[2,512,192]{1,2,0:T(8,128)(2,1)S(1)}, bf16[2,512,192]{1,2,0:T(8,128)(2,1)S(1)}, u32[]{:S(2)}, u32[]{:S(2)}) collective-permute-start(bf16[2,512,192]{1,2,0:T(8,128)(2,1)S(1)} %pad_maximum_fusion.2), channel_id=1, source_target_pairs={{0,32},{16,48},{32,0},{48,16},{64,96},{80,112},{96,64},{112,80},{1... | collective-permute-start | bytes 1179656 | tf_op jit(solution)/shard_map/ppermute | solution.py:118
  73.9 19.8 %all-to-all-start.1 = ((bf16[8,2,64,384]{3,2,1,0:T(8,128)(2,1)}), bf16[8,2,64,384]{3,2,1,0:T(8,128)(2,1)S(1)}, u32[]{:S(2)}, u32[]{:S(2)}) async-start(bf16[8,2,64,384]{3,2,1,0:T(8,128)(2,1)} %bitcast.83), calls=%async_computation.1 | async-start | bytes 1572864 | tf_op jit(solution)/shard_map/all_to_all | solution.py:83
  85.3 7.6 %copy-start.6 = (bf16[2,512,192]{1,2,0:T(8,128)(2,1)}, bf16[2,512,192]{1,2,0:T(8,128)(2,1)S(1)}, u32[]{:S(2)}) copy-start(bf16[2,512,192]{1,2,0:T(8,128)(2,1)S(1)} %collective-permute-done.7) | copy-start | bytes 1179652
  85.4 7.6 %copy-start.11 = (bf16[1,64,512]{2,1,0:T(8,128)(2,1)S(1)}, bf16[1,64,512]{2,1,0:T(8,128)(2,1)}, u32[]{:S(2)}) copy-start(bf16[1,64,512]{2,1,0:T(8,128)(2,1)} %param.7) | copy-start | bytes 196612
  85.4 33.2 %collective-permute-start.8 = (bf16[4,512,192]{1,2,0:T(8,128)(2,1)S(1)}, bf16[4,512,192]{1,2,0:T(8,128)(2,1)}, u32[]{:S(2)}, u32[]{:S(2)}) collective-permute-start(bf16[4,512,192]{1,2,0:T(8,128)(2,1)S(1)} %pad_maximum_fusion.1), channel_id=1, source_target_pairs={{0,16},{16,0},{32,48},{48,32},{64,80},{80,64},{96,112},{112,96},{1... | collective-permute-start | bytes 2359304 | tf_op jit(solution)/shard_map/ppermute | solution.py:118
  93.7 57.8 %copy-start.2 = (bf16[8,2,64,384]{3,2,1,0:T(8,128)(2,1)}, bf16[8,2,64,384]{3,2,1,0:T(8,128)(2,1)S(1)}, u32[]{:S(2)}) copy-start(bf16[8,2,64,384]{3,2,1,0:T(8,128)(2,1)S(1)} %all-to-all-done.1.near_ref) | copy-start | bytes 2359300
  93.7 20.0 %all-to-all-start.6 = ((bf16[8,2,64,384]{3,2,1,0:T(8,128)(2,1)}), bf16[8,2,64,384]{3,2,1,0:T(8,128)(2,1)S(1)}, u32[]{:S(2)}, u32[]{:S(2)}) async-start(bf16[8,2,64,384]{3,2,1,0:T(8,128)(2,1)} %bitcast.82), calls=%async_computation.6 | async-start | bytes 1572864 | tf_op jit(solution)/shard_map/all_to_all | solution.py:83
  101.5 18.4 %collective-permute-start.3 = (bf16[64,512]{1,0:T(8,128)(2,1)}, bf16[64,512]{1,0:T(8,128)(2,1)}, u32[]{:S(2)}, u32[]{:S(2)}) collective-permute-start(bf16[64,512]{1,0:T(8,128)(2,1)} %reshape.128), channel_id=1, source_target_pairs={{0,128},{16,144},{32,160},{48,176},{64,192},{80,208},{96,224},{112... | collective-permute-start | bytes 196616 | tf_op jit(solution)/shard_map/ppermute | solution.py:126
  105.0 14.9 %collective-permute-start.4 = (bf16[64,512]{1,0:T(8,128)(2,1)}, bf16[64,512]{1,0:T(8,128)(2,1)}, u32[]{:S(2)}, u32[]{:S(2)}) collective-permute-start(bf16[64,512]{1,0:T(8,128)(2,1)} %reshape.128), channel_id=1, source_target_pairs={{0,256},{16,272},{32,288},{48,304},{64,320},{80,336},{96,352},{112... | collective-permute-start | bytes 196616 | tf_op jit(solution)/shard_map/ppermute | solution.py:126
  109.8 10.1 %collective-permute-start.5 = (bf16[64,512]{1,0:T(8,128)(2,1)}, bf16[64,512]{1,0:T(8,128)(2,1)}, u32[]{:S(2)}, u32[]{:S(2)}) collective-permute-start(bf16[64,512]{1,0:T(8,128)(2,1)} %reshape.128), channel_id=1, source_target_pairs={{0,384},{16,400},{32,416},{48,432},{64,448},{80,464},{96,480},{112... | collective-permute-start | bytes 196616 | tf_op jit(solution)/shard_map/ppermute | solution.py:126
  113.7 53.8 %copy-start.1 = (bf16[8,2,64,384]{3,2,1,0:T(8,128)(2,1)}, bf16[8,2,64,384]{3,2,1,0:T(8,128)(2,1)S(1)}, u32[]{:S(2)}) copy-start(bf16[8,2,64,384]{3,2,1,0:T(8,128)(2,1)S(1)} %all-to-all-done.6.near_ref) | copy-start | bytes 2359300
  113.7 12.4 %all-to-all-start.2 = ((bf16[8,1,64,384]{3,2,1,0:T(8,128)(2,1)}), bf16[8,1,64,384]{3,2,1,0:T(8,128)(2,1)}, u32[]{:S(2)}, u32[]{:S(2)}) async-start(bf16[8,1,64,384]{3,2,1,0:T(8,128)(2,1)} %bitcast.90), calls=%async_computation.2 | async-start | bytes 786432 | tf_op jit(solution)/shard_map/all_to_all | solution.py:83
  126.1 19.4 %all-to-all-start.4 = ((bf16[8,2,2,64,192]{4,3,2,1,0:T(8,128)(2,1)}), bf16[8,2,2,64,192]{4,3,2,1,0:T(8,128)(2,1)S(1)}, u32[]{:S(2)}, u32[]{:S(2)}) async-start(bf16[8,2,2,64,192]{4,3,2,1,0:T(8,128)(2,1)} %bitcast.79), calls=%async_computation.4 | async-start | bytes 2097152 | tf_op jit(solution)/shard_map/all_to_all | solution.py:83
  145.5 1.0 copy-start.3
  146.5 122.3 %all-to-all-start = ((bf16[8,4,64,384]{3,2,1,0:T(8,128)(2,1)}), bf16[8,4,64,384]{3,2,1,0:T(8,128)(2,1)S(1)}, u32[]{:S(2)}, u32[]{:S(2)}) async-start(bf16[8,4,64,384]{3,2,1,0:T(8,128)(2,1)} %bitcast.73), calls=%async_computation | async-start | bytes 3145728 | tf_op jit(solution)/shard_map/all_to_all | solution.py:83
  151.5 117.3 %collective-permute-start.1 = (bf16[8,64,384]{2,1,0:T(8,128)(2,1)S(1)}, bf16[8,64,384]{2,1,0:T(8,128)(2,1)S(1)}, u32[]{:S(2)}, u32[]{:S(2)}) collective-permute-start(bf16[8,64,384]{2,1,0:T(8,128)(2,1)S(1)} %slice_bitcast_fusion.2), channel_id=1, source_target_pairs={{0,8},{1,9},{2,10},{3,11},{4,12},{5,13},{6,14},{7,15},{8,0},{9,1},... | collective-permute-start | bytes 1179656 | tf_op jit(solution)/shard_map/ppermute | solution.py:274
  159.8 100.1 %collective-permute-start.9 = (bf16[2,2,64,192]{3,2,1,0:T(8,128)(2,1)S(1)}, bf16[2,2,64,192]{3,2,1,0:T(8,128)(2,1)S(1)}, u32[]{:S(2)}, u32[]{:S(2)}) collective-permute-start(bf16[2,2,64,192]{3,2,1,0:T(8,128)(2,1)S(1)} %reduce_sum.22), channel_id=1, source_target_pairs={{0,8},{1,9},{2,10},{3,11},{4,12},{5,13},{6,14},{7,15},{8,0},{9,1},... | collective-permute-start | bytes 294920 | tf_op jit(solution)/shard_map/ppermute | solution.py:139
  168.5 108.1 %collective-permute-start.12 = (bf16[8,64,384]{2,1,0:T(8,128)(2,1)}, bf16[8,64,384]{2,1,0:T(8,128)(2,1)S(1)}, u32[]{:S(2)}, u32[]{:S(2)}) collective-permute-start(bf16[8,64,384]{2,1,0:T(8,128)(2,1)} %get-tuple-element.18), channel_id=1, source_target_pairs={{0,8},{1,9},{2,10},{3,11},{4,12},{5,13},{6,14},{7,15},{8,0},{9,1},... | collective-permute-start | bytes 1179656 | tf_op jit(solution)/shard_map/ppermute | solution.py:274
  175.3 101.4 %collective-permute-start.13 = (bf16[8,64,384]{2,1,0:T(8,128)(2,1)}, bf16[8,64,384]{2,1,0:T(8,128)(2,1)S(1)}, u32[]{:S(2)}, u32[]{:S(2)}) collective-permute-start(bf16[8,64,384]{2,1,0:T(8,128)(2,1)} %get-tuple-element.17), channel_id=1, source_target_pairs={{0,8},{1,9},{2,10},{3,11},{4,12},{5,13},{6,14},{7,15},{8,0},{9,1},... | collective-permute-start | bytes 1179656 | tf_op jit(solution)/shard_map/ppermute | solution.py:274
  259.9 24.5 %collective-permute-start.10 = (bf16[2,64,192]{2,1,0:T(8,128)(2,1)S(1)}, bf16[2,64,192]{2,1,0:T(8,128)(2,1)S(1)}, u32[]{:S(2)}, u32[]{:S(2)}) collective-permute-start(bf16[2,64,192]{2,1,0:T(8,128)(2,1)S(1)} %get-tuple-element.23), channel_id=1, source_target_pairs={{0,0},{1,128},{2,2},{3,130},{4,4},{5,132},{6,6},{7,134},{8,8},{9,1... | collective-permute-start | bytes 147464 | tf_op jit(solution)/shard_map/ppermute | solution.py:144
  263.9 20.5 %collective-permute-start.11 = (bf16[2,64,192]{2,1,0:T(8,128)(2,1)S(1)}, bf16[2,64,192]{2,1,0:T(8,128)(2,1)S(1)}, u32[]{:S(2)}, u32[]{:S(2)}) collective-permute-start(bf16[2,64,192]{2,1,0:T(8,128)(2,1)S(1)} %get-tuple-element.24), channel_id=1, source_target_pairs={{0,256},{1,384},{2,258},{3,386},{4,260},{5,388},{6,262},{7,390},{8... | collective-permute-start | bytes 147464 | tf_op jit(solution)/shard_map/ppermute | solution.py:144
  268.8 0.7 copy-start.7
  268.8 1.2 copy-start
  276.5 0.7 copy-start.8
  277.3 0.7 copy-start.9
  294.3 21.9 %copy-start.10 = (bf16[2,64,384]{2,1,0:T(8,128)(2,1)S(1)}, bf16[2,64,384]{2,1,0:T(8,128)(2,1)}, u32[]{:S(2)}) copy-start(bf16[2,64,384]{2,1,0:T(8,128)(2,1)} %get-tuple-element.14) | copy-start | bytes 294916
  311.3 22.2 %all-to-all-start.5 = ((bf16[8,2,64,384]{3,2,1,0:T(8,128)(2,1)}), bf16[8,2,64,384]{3,2,1,0:T(8,128)(2,1)S(1)}, u32[]{:S(2)}, u32[]{:S(2)}) async-start(bf16[8,2,64,384]{3,2,1,0:T(8,128)(2,1)} %get-tuple-element.9), calls=%async_computation.5 | async-start | bytes 1572864 | tf_op jit(solution)/shard_map/all_to_all | solution.py:83
  316.2 8.8 %collective-permute-start.14 = (bf16[2,64,192]{2,1,0:T(8,128)(2,1)S(1)}, bf16[2,64,192]{2,1,0:T(8,128)(2,1)S(1)}, u32[]{:S(2)}, u32[]{:S(2)}) collective-permute-start(bf16[2,64,192]{2,1,0:T(8,128)(2,1)S(1)} %get-tuple-element.25), channel_id=1, source_target_pairs={{0,0},{1,8},{2,2},{3,10},{4,4},{5,12},{6,6},{7,14},{8,1},{9,9},{10... | collective-permute-start | bytes 147464 | tf_op jit(solution)/shard_map/ppermute | solution.py:264
  316.9 15.9 %collective-permute-start.15 = (bf16[2,64,192]{2,1,0:T(8,128)(2,1)S(1)}, bf16[2,64,192]{2,1,0:T(8,128)(2,1)S(1)}, u32[]{:S(2)}, u32[]{:S(2)}) collective-permute-start(bf16[2,64,192]{2,1,0:T(8,128)(2,1)S(1)} %get-tuple-element.26), channel_id=1, source_target_pairs={{0,1},{1,9},{2,3},{3,11},{4,5},{5,13},{6,7},{7,15},{8,0},{9,8},{10... | collective-permute-start | bytes 147464 | tf_op jit(solution)/shard_map/ppermute | solution.py:265
  333.4 0.9 copy-start.4

commit v5 on v3

--- a/solution.py
+++ b/solution.py
@@ -280,10 +280,12 @@
 
 
 def layer(llm_query, llm_kv, connector, query, key, value, cotangent):
-    near, far = [], []
-    for s in range(SAMPLE_COUNT):
-        near.append(exchange(to_blocks(s, 1, key, value)))
-        far.append([lax.ppermute(near[s][:, i], "tp", SWAP_HALF) for i in range(2)])
+    swap = lambda x: lax.ppermute(x, "tp", SWAP_HALF)
+    raw = swap(key[:1])
+    near = [exchange(to_blocks(s, 1, key, value)) for s in range(SAMPLE_COUNT)]
+    far = [[None, swap(near[0][:, 1])]]
+    far.append([swap(near[1][:, i]) for i in range(2)])
+    far[0][0] = exchange(to_blocks(0, 1, raw))[:, 0]
     columns = gather_columns(connector)
     hidden = llm_hidden(llm_query, llm_kv)
     query_gradient = exchange(to_blocks(0, 2, query, cotangent))

time: 336 us -> 322 us (0.958)
  the two profiles are of different devices: /device:TPU:2 before, /device:TPU:34 now
where the time goes in v5:
time: 322 us; the launch traced here: 320 us
  starting transfers between devices  114 us (35%)
  waiting for transfers between devices  97.4 us (30%)
  blocking collectives  54.5 us (17%)
  Pallas kernels  32.3 us (10%)
  local copies, waits for them, and re-layouts  12.1 us (4%)
  other arithmetic  6.12 us (2%)
    all_to_all x1, blocking collectives, exchange(): lax.all_to_all(x, 'tp', split_axis=0, concat_axis=0, axis_index_groups=HA...  54.5 us
    ppermute x1, waiting for transfers between devices, context_tokens(): there = lax.ppermute(mine, 'tp', SWAP_HALF)  36.9 us
    all_to_all x7, starting transfers between devices, exchange(): lax.all_to_all(x, 'tp', split_axis=0, concat_axis=0, axis_index_groups=HA...  34.2 us
    ppermute x4, starting transfers between devices, layer(): swap = lambda x: lax.ppermute(x, 'tp', SWAP_HALF)  23.7 us
    all_to_all x7, waiting for transfers between devices, exchange(): lax.all_to_all(x, 'tp', split_axis=0, concat_axis=0, axis_index_groups=HA...  15.6 us
    ppermute x1, starting transfers between devices, llm_hidden(): take = lax.ppermute(give, 'tp', SWAP_HALF)  14.8 us
    ppermute x1, waiting for transfers between devices, gather_rows(): got = [jnp.concatenate([hidden, lax.ppermute(hidden, 'fsdp', pairs)])]  14.2 us
    ppermute x4, waiting for transfers between devices, layer(): swap = lambda x: lax.ppermute(x, 'tp', SWAP_HALF)  14 us
  transfers between devices with their start and end apart: 23, of which 11 were waited for; matrix products, arithmetic and copies ran while one was open for 4% of the time, Pallas kernels for 7%

profile of v5, /device:TPU:34, one launch (start us, length us, event | category | flops | bytes accessed | tf_op | source)
XLA Modules:
  0.0 320.1 jit_solution(421932960155305473)
XLA Ops:
  1.5 14.8 %collective-permute-start.2 = (bf16[2,20,512]{2,0,1:T(2,128)(2,1)S(1)}, bf16[2,20,512]{2,0,1:T(2,128)(2,1)S(1)}, u32[]{:S(2)}, u32[]{:S(2)}) collective-permute-start(bf16[2,20,512]{2,0,1:T(2,128)(2,1)S(1)} %get-tuple-element.28), channel_id=1, source_target_pairs={{0,8},{1,9},{2,10},{3,11},{4,12},{5,13},{6,14},{7,15},{8,0},{9,1},... | collective-permute-start | bytes 122888 | tf_op jit(solution)/shard_map/ppermute | solution.py:92
  16.4 3.4 %collective-permute-start.7 = (bf16[1,512,192]{1,2,0:T(8,128)(2,1)}, bf16[1,512,192]{1,2,0:T(8,128)(2,1)S(1)}, u32[]{:S(2)}, u32[]{:S(2)}) collective-permute-start(bf16[1,512,192]{1,2,0:T(8,128)(2,1)} %bitcast.87), channel_id=1, source_target_pairs={{0,32},{16,48},{32,0},{48,16},{64,96},{80,112},{96,64},{112,80},{1... | collective-permute-start | bytes 589832 | tf_op jit(solution)/shard_map/ppermute | solution.py:118
  19.7 1.0 slice_bitcast_fusion.3
  20.8 1.9 collective-permute-start
  23.8 4.8 %all-to-all-start.3 = ((bf16[8,2,2,20,128]{4,2,3,1,0:T(2,128)(2,1)}), bf16[8,2,2,20,128]{4,2,3,1,0:T(2,128)(2,1)S(1)}, u32[]{:S(2)}, u32[]{:S(2)}) async-start(bf16[8,2,2,20,128]{4,2,3,1,0:T(2,128)(2,1)} %bitcast.15), calls=%async_computation.3 | async-start | bytes 327680 | tf_op jit(solution)/shard_map/all_to_all | solution.py:83
  28.7 2.0 to_blocks.5
  30.7 2.0 to_blocks.7
  33.6 4.9 %all-to-all-start.1 = ((bf16[8,2,64,384]{3,2,1,0:T(8,128)(2,1)}), bf16[8,2,64,384]{3,2,1,0:T(8,128)(2,1)S(1)}, u32[]{:S(2)}, u32[]{:S(2)}) async-start(bf16[8,2,64,384]{3,2,1,0:T(8,128)(2,1)} %bitcast.5), calls=%async_computation.1 | async-start | bytes 1572864 | tf_op jit(solution)/shard_map/all_to_all | solution.py:83
  40.1 8.7 %collective-permute-start.3 = (bf16[64,512]{1,0:T(8,128)(2,1)S(1)}, bf16[64,512]{1,0:T(8,128)(2,1)S(1)}, u32[]{:S(2)}, u32[]{:S(2)}) collective-permute-start(bf16[64,512]{1,0:T(8,128)(2,1)S(1)} %reshape.128), channel_id=1, source_target_pairs={{0,64},{16,80},{32,96},{48,112},{64,0},{80,16},{96,32},{112,48},{1... | collective-permute-start | bytes 196616 | tf_op jit(solution)/shard_map/ppermute | solution.py:124
  48.8 1.4 all-to-all-done.1.near_ref
  50.2 4.9 %all-to-all-start.6 = ((bf16[8,2,64,384]{3,2,1,0:T(8,128)(2,1)}), bf16[8,2,64,384]{3,2,1,0:T(8,128)(2,1)S(1)}, u32[]{:S(2)}, u32[]{:S(2)}) async-start(bf16[8,2,64,384]{3,2,1,0:T(8,128)(2,1)} %bitcast.32), calls=%async_computation.6 | async-start | bytes 1572864 | tf_op jit(solution)/shard_map/all_to_all | solution.py:83
  55.1 14.2 %collective-permute-done.3 = bf16[64,512]{1,0:T(8,128)(2,1)S(1)} collective-permute-done((bf16[64,512]{1,0:T(8,128)(2,1)S(1)}, bf16[64,512]{1,0:T(8,128)(2,1)S(1)}, u32[]{:S(2)}, u32[]{:S(2)}) %collective-permute-start.3) | collective-permute-done | bytes 65568 | tf_op jit(solution)/shard_map/ppermute | solution.py:124
  69.4 3.5 %collective-permute-start.4 = (bf16[128,512]{1,0:T(8,128)(2,1)S(1)}, bf16[128,512]{1,0:T(8,128)(2,1)S(1)}, u32[]{:S(2)}, u32[]{:S(2)}) collective-permute-start(bf16[128,512]{1,0:T(8,128)(2,1)S(1)} %get-tuple-element.29), channel_id=1, source_target_pairs={{0,128},{16,144},{32,160},{48,176},{64,192},{80,208},{96,224},{112... | collective-permute-start | bytes 393224 | tf_op jit(solution)/shard_map/ppermute | solution.py:127
  73.7 1.9 collective-permute-start.8
  75.6 4.8 %collective-permute-start.5 = (bf16[128,512]{1,0:T(8,128)(2,1)S(1)}, bf16[128,512]{1,0:T(8,128)(2,1)S(1)}, u32[]{:S(2)}, u32[]{:S(2)}) collective-permute-start(bf16[128,512]{1,0:T(8,128)(2,1)S(1)} %get-tuple-element.29), channel_id=1, source_target_pairs={{0,256},{16,272},{32,288},{48,304},{64,320},{80,336},{96,352},{112... | collective-permute-start | bytes 393224 | tf_op jit(solution)/shard_map/ppermute | solution.py:127
  80.4 2.1 collective-permute-start.6
  82.6 1.5 collective-permute-done.5
  84.0 4.4 %collective-permute-done.6 = bf16[128,512]{1,0:T(8,128)(2,1)S(1)} collective-permute-done((bf16[128,512]{1,0:T(8,128)(2,1)S(1)}, bf16[128,512]{1,0:T(8,128)(2,1)S(1)}, u32[]{:S(2)}, u32[]{:S(2)}) %collective-permute-start.6) | collective-permute-done | bytes 131104 | tf_op jit(solution)/shard_map/ppermute | solution.py:127
  89.3 1.7 to_blocks.6
  91.0 4.8 %all-to-all-start.2 = ((bf16[8,1,64,384]{3,2,1,0:T(8,128)(2,1)}), bf16[8,1,64,384]{3,2,1,0:T(8,128)(2,1)S(1)}, u32[]{:S(2)}, u32[]{:S(2)}) async-start(bf16[8,1,64,384]{3,2,1,0:T(8,128)(2,1)} %bitcast.86), calls=%async_computation.2 | async-start | bytes 786432 | tf_op jit(solution)/shard_map/all_to_all | solution.py:83
  95.9 1.1 pad_maximum_fusion
  97.0 1.6 fusion.7
  98.6 1.0 convert_element_type.31
  99.6 1.4 copy.26
  101.0 1.0 copy.27
  102.1 1.3 all-to-all-done.2
  103.3 4.9 %all-to-all-start.4 = ((bf16[8,2,2,64,192]{4,3,2,1,0:T(8,128)(2,1)}), bf16[8,2,2,64,192]{4,3,2,1,0:T(8,128)(2,1)S(1)}, u32[]{:S(2)}, u32[]{:S(2)}) async-start(bf16[8,2,2,64,192]{4,3,2,1,0:T(8,128)(2,1)} %bitcast.79), calls=%async_computation.4 | async-start | bytes 2097152 | tf_op jit(solution)/shard_map/all_to_all | solution.py:83
  108.3 2.3 to_blocks.4
  110.6 12.2 %all-to-all-done.4 = bf16[8,2,2,64,192]{4,3,2,1,0:T(8,128)(2,1)S(1)} async-done(((bf16[8,2,2,64,192]{4,3,2,1,0:T(8,128)(2,1)}), bf16[8,2,2,64,192]{4,3,2,1,0:T(8,128)(2,1)S(1)}, u32[]{:S(2)}, u32[]{:S(2)}) %all-to-all-start.4) | async-done | bytes 786464 | tf_op jit(solution)/shard_map/all_to_all | solution.py:83
  123.7 4.9 %all-to-all-start = ((bf16[8,4,64,384]{3,2,1,0:T(8,128)(2,1)}), bf16[8,4,64,384]{3,2,1,0:T(8,128)(2,1)S(1)}, u32[]{:S(2)}, u32[]{:S(2)}) async-start(bf16[8,4,64,384]{3,2,1,0:T(8,128)(2,1)} %bitcast.74), calls=%async_computation | async-start | bytes 3145728 | tf_op jit(solution)/shard_map/all_to_all | solution.py:83
  128.7 7.2 %collective-permute-start.1 = (bf16[8,64,384]{2,1,0:T(8,128)(2,1)S(1)}, bf16[8,64,384]{2,1,0:T(8,128)(2,1)S(1)}, u32[]{:S(2)}, u32[]{:S(2)}) collective-permute-start(bf16[8,64,384]{2,1,0:T(8,128)(2,1)S(1)} %slice_bitcast_fusion.2), channel_id=1, source_target_pairs={{0,8},{1,9},{2,10},{3,11},{4,12},{5,13},{6,14},{7,15},{8,0},{9,1},... | collective-permute-start | bytes 1179656 | tf_op jit(solution)/shard_map/ppermute | solution.py:283
  136.0 1.4 reduce_sum.22
  137.4 7.3 %collective-permute-start.9 = (bf16[2,2,64,192]{3,2,1,0:T(8,128)(2,1)S(1)}, bf16[2,2,64,192]{3,2,1,0:T(8,128)(2,1)S(1)}, u32[]{:S(2)}, u32[]{:S(2)}) collective-permute-start(bf16[2,2,64,192]{3,2,1,0:T(8,128)(2,1)S(1)} %reduce_sum.22), channel_id=1, source_target_pairs={{0,8},{1,9},{2,10},{3,11},{4,12},{5,13},{6,14},{7,15},{8,0},{9,1},... | collective-permute-start | bytes 294920 | tf_op jit(solution)/shard_map/ppermute | solution.py:140
  145.7 7.2 %collective-permute-start.12 = (bf16[8,64,384]{2,1,0:T(8,128)(2,1)}, bf16[8,64,384]{2,1,0:T(8,128)(2,1)S(1)}, u32[]{:S(2)}, u32[]{:S(2)}) collective-permute-start(bf16[8,64,384]{2,1,0:T(8,128)(2,1)} %get-tuple-element.18), channel_id=1, source_target_pairs={{0,8},{1,9},{2,10},{3,11},{4,12},{5,13},{6,14},{7,15},{8,0},{9,1},... | collective-permute-start | bytes 1179656 | tf_op jit(solution)/shard_map/ppermute | solution.py:283
  152.9 7.3 %collective-permute-start.13 = (bf16[8,64,384]{2,1,0:T(8,128)(2,1)}, bf16[8,64,384]{2,1,0:T(8,128)(2,1)S(1)}, u32[]{:S(2)}, u32[]{:S(2)}) collective-permute-start(bf16[8,64,384]{2,1,0:T(8,128)(2,1)} %get-tuple-element.17), channel_id=1, source_target_pairs={{0,8},{1,9},{2,10},{3,11},{4,12},{5,13},{6,14},{7,15},{8,0},{9,1},... | collective-permute-start | bytes 1179656 | tf_op jit(solution)/shard_map/ppermute | solution.py:283
  160.3 36.9 %collective-permute-done.9 = bf16[2,2,64,192]{3,2,1,0:T(8,128)(2,1)S(1)} collective-permute-done((bf16[2,2,64,192]{3,2,1,0:T(8,128)(2,1)S(1)}, bf16[2,2,64,192]{3,2,1,0:T(8,128)(2,1)S(1)}, u32[]{:S(2)}, u32[]{:S(2)}) %collective-permute-start.9) | collective-permute-done | bytes 98336 | tf_op jit(solution)/shard_map/ppermute | solution.py:140
  197.9 1.9 collective-permute-start.11
  201.2 6.4 %latent_attention.2.so_ref = bf16[8,64,384]{2,1,0:T(8,128)(2,1)} custom-call(bf16[8,4,64,384]{3,2,1,0:T(8,128)(2,1)} %copy-done, bf16[8,2,64,384]{3,2,1,0:T(8,128)(2,1)} %copy-done.2, bf16[8,64,384]{2,1,0:T(8,128)(2,1)} %bitcast.85, bf16[8,64,384]{2,1,0:T(8,128)(2,1)} %copy-done.8), custom_call_target="tpu_custom_call" | custom-call | tf_op jit(solution)/shard_map/latent_attention/pallas_call | solution.py:187
  207.6 1.9 collective-permute-done.12.fk_ref
  209.5 12.1 %collective-permute-done.13.fv_ref = bf16[8,64,384]{2,1,0:T(8,128)(2,1)S(1)} collective-permute-done((bf16[8,64,384]{2,1,0:T(8,128)(2,1)}, bf16[8,64,384]{2,1,0:T(8,128)(2,1)S(1)}, u32[]{:S(2)}, u32[]{:S(2)}) %collective-permute-start.13) | collective-permute-done | bytes 393248 | tf_op jit(solution)/shard_map/ppermute | solution.py:283
  222.4 6.4 %latent_attention.3.so_ref = bf16[8,64,384]{2,1,0:T(8,128)(2,1)} custom-call(bf16[8,4,64,384]{3,2,1,0:T(8,128)(2,1)} %copy-done, bf16[8,2,64,384]{3,2,1,0:T(8,128)(2,1)} %copy-done.1, bf16[8,64,384]{2,1,0:T(8,128)(2,1)} %copy-done.9, bf16[8,64,384]{2,1,0:T(8,128)(2,1)} %copy-done.10), custom_call_target="tpu_custom_call" | custom-call | tf_op jit(solution)/shard_map/latent_attention/pallas_call | solution.py:187
  229.6 4.5 %cross_attention.2 = (bf16[8,2,64,384]{3,2,1,0:T(8,128)(2,1)}, f32[2,64,384]{2,1,0:T(8,128)}) custom-call(bf16[8,64,384]{2,1,0:T(8,128)(2,1)} %latent_attention.2.so_ref, bf16[8,4,64,384]{3,2,1,0:T(8,128)(2,1)} %copy-done, bf16[2,64,384]{2,1,0:T(8,128)(2,1)} %pad_maximum_fusion.2.context_ref), custom_call_target="tpu_custom_call" | custom-call | tf_op jit(solution)/shard_map/cross_attention/pallas_call | solution.py:247
  234.1 4.5 %cross_attention.3 = (bf16[8,2,64,384]{3,2,1,0:T(8,128)(2,1)}, bf16[2,64,384]{2,1,0:T(8,128)(2,1)}) custom-call(bf16[8,64,384]{2,1,0:T(8,128)(2,1)} %latent_attention.3.so_ref, bf16[8,4,64,384]{3,2,1,0:T(8,128)(2,1)} %copy-done, bf16[2,64,384]{2,1,0:T(8,128)(2,1)} %pad_maximum_fusion.2.context_ref, f32[2,64,384]{2,1,0:T(8,128)} %get-tuple-element.10.refs_0_), custom_call_target="tpu_custom_call" | custom-call | tf_op jit(solution)/shard_map/cross_attention/pallas_call | solution.py:247
  238.6 54.5 %all_to_all.40 = bf16[8,2,64,384]{3,2,1,0:T(8,128)(2,1)} all-to-all(bf16[8,2,64,384]{3,2,1,0:T(8,128)(2,1)} %get-tuple-element.11), channel_id=1, replica_groups={{0,1,2,3,4,5,6,7},{8,9,10,11,12,13,14,15},{16,17,18,19,20,21,22,23},{24..., dimensions={0} | all-to-all | bytes 1572864 | tf_op jit(solution)/shard_map/all_to_all | solution.py:83
  293.1 4.9 %all-to-all-start.5 = ((bf16[8,2,64,384]{3,2,1,0:T(8,128)(2,1)}), bf16[8,2,64,384]{3,2,1,0:T(8,128)(2,1)S(1)}, u32[]{:S(2)}, u32[]{:S(2)}) async-start(bf16[8,2,64,384]{3,2,1,0:T(8,128)(2,1)} %get-tuple-element.9), calls=%async_computation.5 | async-start | bytes 1572864 | tf_op jit(solution)/shard_map/all_to_all | solution.py:83
  298.8 6.7 %collective-permute-start.15 = (bf16[2,64,192]{2,1,0:T(8,128)(2,1)S(1)}, bf16[2,64,192]{2,1,0:T(8,128)(2,1)S(1)}, u32[]{:S(2)}, u32[]{:S(2)}) collective-permute-start(bf16[2,64,192]{2,1,0:T(8,128)(2,1)S(1)} %get-tuple-element.26), channel_id=1, source_target_pairs={{0,1},{1,9},{2,3},{3,11},{4,5},{5,13},{6,7},{7,15},{8,0},{9,8},{10... | collective-permute-start | bytes 147464 | tf_op jit(solution)/shard_map/ppermute | solution.py:274
  305.5 10.7 %collective-permute-done.15 = bf16[2,64,192]{2,1,0:T(8,128)(2,1)S(1)} collective-permute-done((bf16[2,64,192]{2,1,0:T(8,128)(2,1)S(1)}, bf16[2,64,192]{2,1,0:T(8,128)(2,1)S(1)}, u32[]{:S(2)}, u32[]{:S(2)}) %collective-permute-start.15) | collective-permute-done | bytes 49184 | tf_op jit(solution)/shard_map/ppermute | solution.py:274
  317.8 2.3 from_blocks.1
  (77 shorter events, 13.8 us)
Async XLA Ops:
  1.5 21.3 %collective-permute-start.2 = (bf16[2,20,512]{2,0,1:T(2,128)(2,1)S(1)}, bf16[2,20,512]{2,0,1:T(2,128)(2,1)S(1)}, u32[]{:S(2)}, u32[]{:S(2)}) collective-permute-start(bf16[2,20,512]{2,0,1:T(2,128)(2,1)S(1)} %get-tuple-element.28), channel_id=1, source_target_pairs={{0,8},{1,9},{2,10},{3,11},{4,12},{5,13},{6,14},{7,15},{8,0},{9,1},... | collective-permute-start | bytes 122888 | tf_op jit(solution)/shard_map/ppermute | solution.py:92
  16.4 56.5 %collective-permute-start.7 = (bf16[1,512,192]{1,2,0:T(8,128)(2,1)}, bf16[1,512,192]{1,2,0:T(8,128)(2,1)S(1)}, u32[]{:S(2)}, u32[]{:S(2)}) collective-permute-start(bf16[1,512,192]{1,2,0:T(8,128)(2,1)} %bitcast.87), channel_id=1, source_target_pairs={{0,32},{16,48},{32,0},{48,16},{64,96},{80,112},{96,64},{112,80},{1... | collective-permute-start | bytes 589832 | tf_op jit(solution)/shard_map/ppermute | solution.py:118
  20.8 67.7 %collective-permute-start = (bf16[1,64,3072]{2,1,0:T(8,128)(2,1)S(1)}, bf16[1,64,3072]{2,1,0:T(8,128)(2,1)S(1)}, u32[]{:S(2)}, u32[]{:S(2)}) collective-permute-start(bf16[1,64,3072]{2,1,0:T(8,128)(2,1)S(1)} %slice_bitcast_fusion.3), channel_id=1, source_target_pairs={{0,8},{1,9},{2,10},{3,11},{4,12},{5,13},{6,14},{7,15},{8,0},{9,1},... | collective-permute-start | bytes 1179656 | tf_op jit(solution)/shard_map/ppermute | solution.py:283
  23.8 9.8 %all-to-all-start.3 = ((bf16[8,2,2,20,128]{4,2,3,1,0:T(2,128)(2,1)}), bf16[8,2,2,20,128]{4,2,3,1,0:T(2,128)(2,1)S(1)}, u32[]{:S(2)}, u32[]{:S(2)}) async-start(bf16[8,2,2,20,128]{4,2,3,1,0:T(2,128)(2,1)} %bitcast.15), calls=%async_computation.3 | async-start | bytes 327680 | tf_op jit(solution)/shard_map/all_to_all | solution.py:83
  30.7 2.1 copy-start.13
  33.6 16.6 %all-to-all-start.1 = ((bf16[8,2,64,384]{3,2,1,0:T(8,128)(2,1)}), bf16[8,2,64,384]{3,2,1,0:T(8,128)(2,1)S(1)}, u32[]{:S(2)}, u32[]{:S(2)}) async-start(bf16[8,2,64,384]{3,2,1,0:T(8,128)(2,1)} %bitcast.5), calls=%async_computation.1 | async-start | bytes 1572864 | tf_op jit(solution)/shard_map/all_to_all | solution.py:83
  39.7 33.1 %copy-start.6 = (bf16[512,192]{0,1:T(8,128)(2,1)S(1)}, bf16[512,192]{0,1:T(8,128)(2,1)}, u32[]{:S(2)}) copy-start(bf16[512,192]{0,1:T(8,128)(2,1)} %param.9) | copy-start | bytes 589828
  40.1 29.3 %collective-permute-start.3 = (bf16[64,512]{1,0:T(8,128)(2,1)S(1)}, bf16[64,512]{1,0:T(8,128)(2,1)S(1)}, u32[]{:S(2)}, u32[]{:S(2)}) collective-permute-start(bf16[64,512]{1,0:T(8,128)(2,1)S(1)} %reshape.128), channel_id=1, source_target_pairs={{0,64},{16,80},{32,96},{48,112},{64,0},{80,16},{96,32},{112,48},{1... | collective-permute-start | bytes 196616 | tf_op jit(solution)/shard_map/ppermute | solution.py:124
  50.2 78.5 %copy-start.2 = (bf16[8,2,64,384]{3,2,1,0:T(8,128)(2,1)}, bf16[8,2,64,384]{3,2,1,0:T(8,128)(2,1)S(1)}, u32[]{:S(2)}) copy-start(bf16[8,2,64,384]{3,2,1,0:T(8,128)(2,1)S(1)} %all-to-all-done.1.near_ref) | copy-start | bytes 2359300
  50.2 40.8 %all-to-all-start.6 = ((bf16[8,2,64,384]{3,2,1,0:T(8,128)(2,1)}), bf16[8,2,64,384]{3,2,1,0:T(8,128)(2,1)S(1)}, u32[]{:S(2)}, u32[]{:S(2)}) async-start(bf16[8,2,64,384]{3,2,1,0:T(8,128)(2,1)} %bitcast.32), calls=%async_computation.6 | async-start | bytes 1572864 | tf_op jit(solution)/shard_map/all_to_all | solution.py:83
  69.4 13.2 %collective-permute-start.4 = (bf16[128,512]{1,0:T(8,128)(2,1)S(1)}, bf16[128,512]{1,0:T(8,128)(2,1)S(1)}, u32[]{:S(2)}, u32[]{:S(2)}) collective-permute-start(bf16[128,512]{1,0:T(8,128)(2,1)S(1)} %get-tuple-element.29), channel_id=1, source_target_pairs={{0,128},{16,144},{32,160},{48,176},{64,192},{80,208},{96,224},{112... | collective-permute-start | bytes 393224 | tf_op jit(solution)/shard_map/ppermute | solution.py:127
  73.7 22.2 %collective-permute-start.8 = (bf16[2,512,192]{1,2,0:T(8,128)(2,1)}, bf16[2,512,192]{1,2,0:T(8,128)(2,1)}, u32[]{:S(2)}, u32[]{:S(2)}) collective-permute-start(bf16[2,512,192]{1,2,0:T(8,128)(2,1)} %pad_maximum_fusion.1), channel_id=1, source_target_pairs={{0,16},{16,0},{32,48},{48,32},{64,80},{80,64},{96,112},{112,96},{1... | collective-permute-start | bytes 1179656 | tf_op jit(solution)/shard_map/ppermute | solution.py:118
  75.6 8.4 %collective-permute-start.5 = (bf16[128,512]{1,0:T(8,128)(2,1)S(1)}, bf16[128,512]{1,0:T(8,128)(2,1)S(1)}, u32[]{:S(2)}, u32[]{:S(2)}) collective-permute-start(bf16[128,512]{1,0:T(8,128)(2,1)S(1)} %get-tuple-element.29), channel_id=1, source_target_pairs={{0,256},{16,272},{32,288},{48,304},{64,320},{80,336},{96,352},{112... | collective-permute-start | bytes 393224 | tf_op jit(solution)/shard_map/ppermute | solution.py:127
  80.4 8.1 %collective-permute-start.6 = (bf16[128,512]{1,0:T(8,128)(2,1)S(1)}, bf16[128,512]{1,0:T(8,128)(2,1)S(1)}, u32[]{:S(2)}, u32[]{:S(2)}) collective-permute-start(bf16[128,512]{1,0:T(8,128)(2,1)S(1)} %get-tuple-element.29), channel_id=1, source_target_pairs={{0,384},{16,400},{32,416},{48,432},{64,448},{80,464},{96,480},{112... | collective-permute-start | bytes 393224 | tf_op jit(solution)/shard_map/ppermute | solution.py:127
  88.5 8.5 %copy-start.7 = (bf16[512,512]{1,0:T(8,128)(2,1)}, bf16[512,512]{1,0:T(8,128)(2,1)S(1)}, u32[]{:S(2)}) copy-start(bf16[512,512]{1,0:T(8,128)(2,1)S(1)} %constant_dynamic-update-slice_fusion.2) | copy-start | bytes 1572868
  88.5 0.8 copy-start.11
  91.0 53.7 %copy-start.1 = (bf16[8,2,64,384]{3,2,1,0:T(8,128)(2,1)}, bf16[8,2,64,384]{3,2,1,0:T(8,128)(2,1)S(1)}, u32[]{:S(2)}) copy-start(bf16[8,2,64,384]{3,2,1,0:T(8,128)(2,1)S(1)} %all-to-all-done.6.near_ref) | copy-start | bytes 2359300
  91.0 12.3 %all-to-all-start.2 = ((bf16[8,1,64,384]{3,2,1,0:T(8,128)(2,1)}), bf16[8,1,64,384]{3,2,1,0:T(8,128)(2,1)S(1)}, u32[]{:S(2)}, u32[]{:S(2)}) async-start(bf16[8,1,64,384]{3,2,1,0:T(8,128)(2,1)} %bitcast.86), calls=%async_computation.2 | async-start | bytes 786432 | tf_op jit(solution)/shard_map/all_to_all | solution.py:83
  103.3 7.3 %copy-start.5 = (bf16[8,1,64,384]{3,2,1,0:T(8,128)(2,1)}, bf16[8,1,64,384]{3,2,1,0:T(8,128)(2,1)S(1)}, u32[]{:S(2)}) copy-start(bf16[8,1,64,384]{3,2,1,0:T(8,128)(2,1)S(1)} %all-to-all-done.2) | copy-start | bytes 1179652
  103.3 19.4 %all-to-all-start.4 = ((bf16[8,2,2,64,192]{4,3,2,1,0:T(8,128)(2,1)}), bf16[8,2,2,64,192]{4,3,2,1,0:T(8,128)(2,1)S(1)}, u32[]{:S(2)}, u32[]{:S(2)}) async-start(bf16[8,2,2,64,192]{4,3,2,1,0:T(8,128)(2,1)} %bitcast.79), calls=%async_computation.4 | async-start | bytes 2097152 | tf_op jit(solution)/shard_map/all_to_all | solution.py:83
  122.8 1.0 copy-start.3
  123.7 76.2 %all-to-all-start = ((bf16[8,4,64,384]{3,2,1,0:T(8,128)(2,1)}), bf16[8,4,64,384]{3,2,1,0:T(8,128)(2,1)S(1)}, u32[]{:S(2)}, u32[]{:S(2)}) async-start(bf16[8,4,64,384]{3,2,1,0:T(8,128)(2,1)} %bitcast.74), calls=%async_computation | async-start | bytes 3145728 | tf_op jit(solution)/shard_map/all_to_all | solution.py:83
  128.7 71.1 %collective-permute-start.1 = (bf16[8,64,384]{2,1,0:T(8,128)(2,1)S(1)}, bf16[8,64,384]{2,1,0:T(8,128)(2,1)S(1)}, u32[]{:S(2)}, u32[]{:S(2)}) collective-permute-start(bf16[8,64,384]{2,1,0:T(8,128)(2,1)S(1)} %slice_bitcast_fusion.2), channel_id=1, source_target_pairs={{0,8},{1,9},{2,10},{3,11},{4,12},{5,13},{6,14},{7,15},{8,0},{9,1},... | collective-permute-start | bytes 1179656 | tf_op jit(solution)/shard_map/ppermute | solution.py:283
  137.4 59.8 %collective-permute-start.9 = (bf16[2,2,64,192]{3,2,1,0:T(8,128)(2,1)S(1)}, bf16[2,2,64,192]{3,2,1,0:T(8,128)(2,1)S(1)}, u32[]{:S(2)}, u32[]{:S(2)}) collective-permute-start(bf16[2,2,64,192]{3,2,1,0:T(8,128)(2,1)S(1)} %reduce_sum.22), channel_id=1, source_target_pairs={{0,8},{1,9},{2,10},{3,11},{4,12},{5,13},{6,14},{7,15},{8,0},{9,1},... | collective-permute-start | bytes 294920 | tf_op jit(solution)/shard_map/ppermute | solution.py:140
  145.7 63.8 %collective-permute-start.12 = (bf16[8,64,384]{2,1,0:T(8,128)(2,1)}, bf16[8,64,384]{2,1,0:T(8,128)(2,1)S(1)}, u32[]{:S(2)}, u32[]{:S(2)}) collective-permute-start(bf16[8,64,384]{2,1,0:T(8,128)(2,1)} %get-tuple-element.18), channel_id=1, source_target_pairs={{0,8},{1,9},{2,10},{3,11},{4,12},{5,13},{6,14},{7,15},{8,0},{9,1},... | collective-permute-start | bytes 1179656 | tf_op jit(solution)/shard_map/ppermute | solution.py:283
  152.9 68.7 %collective-permute-start.13 = (bf16[8,64,384]{2,1,0:T(8,128)(2,1)}, bf16[8,64,384]{2,1,0:T(8,128)(2,1)S(1)}, u32[]{:S(2)}, u32[]{:S(2)}) collective-permute-start(bf16[8,64,384]{2,1,0:T(8,128)(2,1)} %get-tuple-element.17), channel_id=1, source_target_pairs={{0,8},{1,9},{2,10},{3,11},{4,12},{5,13},{6,14},{7,15},{8,0},{9,1},... | collective-permute-start | bytes 1179656 | tf_op jit(solution)/shard_map/ppermute | solution.py:283
  197.2 31.6 %collective-permute-start.10 = (bf16[2,64,192]{2,1,0:T(8,128)(2,1)S(1)}, bf16[2,64,192]{2,1,0:T(8,128)(2,1)S(1)}, u32[]{:S(2)}, u32[]{:S(2)}) collective-permute-start(bf16[2,64,192]{2,1,0:T(8,128)(2,1)S(1)} %get-tuple-element.23), channel_id=1, source_target_pairs={{0,0},{1,128},{2,2},{3,130},{4,64},{5,192},{6,66},{7,194},{8,8},{9... | collective-permute-start | bytes 147464 | tf_op jit(solution)/shard_map/ppermute | solution.py:153
  197.9 30.9 %collective-permute-start.11 = (bf16[2,64,192]{2,1,0:T(8,128)(2,1)S(1)}, bf16[2,64,192]{2,1,0:T(8,128)(2,1)S(1)}, u32[]{:S(2)}, u32[]{:S(2)}) collective-permute-start(bf16[2,64,192]{2,1,0:T(8,128)(2,1)S(1)} %get-tuple-element.24), channel_id=1, source_target_pairs={{0,256},{1,384},{2,258},{3,386},{4,320},{5,448},{6,322},{7,450},{8... | collective-permute-start | bytes 147464 | tf_op jit(solution)/shard_map/ppermute | solution.py:153
  199.9 0.7 copy-start.8
  199.9 1.3 copy-start
  209.5 12.2 %copy-start.9 = (bf16[8,64,384]{2,1,0:T(8,128)(2,1)}, bf16[8,64,384]{2,1,0:T(8,128)(2,1)S(1)}, u32[]{:S(2)}) copy-start(bf16[8,64,384]{2,1,0:T(8,128)(2,1)S(1)} %collective-permute-done.12.fk_ref) | copy-start | bytes 1179652
  221.6 0.7 copy-start.10
  238.6 59.4 %copy-start.12 = (bf16[2,64,384]{2,1,0:T(8,128)(2,1)S(1)}, bf16[2,64,384]{2,1,0:T(8,128)(2,1)}, u32[]{:S(2)}) copy-start(bf16[2,64,384]{2,1,0:T(8,128)(2,1)} %get-tuple-element.14) | copy-start | bytes 294916
  293.1 23.7 %all-to-all-start.5 = ((bf16[8,2,64,384]{3,2,1,0:T(8,128)(2,1)}), bf16[8,2,64,384]{3,2,1,0:T(8,128)(2,1)S(1)}, u32[]{:S(2)}, u32[]{:S(2)}) async-start(bf16[8,2,64,384]{3,2,1,0:T(8,128)(2,1)} %get-tuple-element.9), calls=%async_computation.5 | async-start | bytes 1572864 | tf_op jit(solution)/shard_map/all_to_all | solution.py:83
  298.1 7.4 %collective-permute-start.14 = (bf16[2,64,192]{2,1,0:T(8,128)(2,1)S(1)}, bf16[2,64,192]{2,1,0:T(8,128)(2,1)S(1)}, u32[]{:S(2)}, u32[]{:S(2)}) collective-permute-start(bf16[2,64,192]{2,1,0:T(8,128)(2,1)S(1)} %get-tuple-element.25), channel_id=1, source_target_pairs={{0,0},{1,8},{2,2},{3,10},{4,4},{5,12},{6,6},{7,14},{8,1},{9,9},{10... | collective-permute-start | bytes 147464 | tf_op jit(solution)/shard_map/ppermute | solution.py:273
  298.8 17.4 %collective-permute-start.15 = (bf16[2,64,192]{2,1,0:T(8,128)(2,1)S(1)}, bf16[2,64,192]{2,1,0:T(8,128)(2,1)S(1)}, u32[]{:S(2)}, u32[]{:S(2)}) collective-permute-start(bf16[2,64,192]{2,1,0:T(8,128)(2,1)S(1)} %get-tuple-element.26), channel_id=1, source_target_pairs={{0,1},{1,9},{2,3},{3,11},{4,5},{5,13},{6,7},{7,15},{8,0},{9,8},{10... | collective-permute-start | bytes 147464 | tf_op jit(solution)/shard_map/ppermute | solution.py:274
  316.9 0.9 copy-start.4

commit v6 on v5

--- a/solution.py
+++ b/solution.py
@@ -45,17 +45,18 @@
         at += count
 
 
-def to_blocks(first, count, *parts):
-    rows = parts[0].shape[1]
-    total = count * len(parts)
+def to_blocks(*parts):
+    rows = parts[0][0].shape[1]
+    total = sum(count for _, count, _ in parts)
+    specs = [pl.BlockSpec((count, rows, 4 * BLOCK), lambda c, at=at: (at, 0, c)) for _, count, at in parts]
     out = pl.pallas_call(
         copy_blocks,
         grid=(2,),
-        in_specs=[pl.BlockSpec((count, rows, 4 * BLOCK), lambda c: (first, 0, c))] * len(parts),
+        in_specs=specs,
         out_specs=pl.BlockSpec((4, 1, total, rows, BLOCK), lambda c: (0, c, 0, 0, 0)),
-        out_shape=jax.ShapeDtypeStruct((4, 2, total, rows, BLOCK), parts[0].dtype),
+        out_shape=jax.ShapeDtypeStruct((4, 2, total, rows, BLOCK), parts[0][0].dtype),
         name="to_blocks",
-    )(*parts)
+    )(*(x for x, _, _ in parts))
     return out.reshape(8, total, rows, BLOCK)
 
 
@@ -182,6 +183,7 @@
 
 
 def attention(sample, query_gradient, near, far_k, far_v):
+    far_k, place = far_k
     rows = near.shape[2]
     spec = pl.BlockSpec((8, rows, HEAD_SIZE), lambda n: (0, 0, n))
     return pl.pallas_call(
@@ -190,7 +192,7 @@
         in_specs=[
             pl.BlockSpec((8, 1, rows, HEAD_SIZE), lambda n: (0, sample, 0, n)),
             pl.BlockSpec((8, 2, rows, HEAD_SIZE), lambda n: (0, 0, 0, n)),
-            spec,
+            pl.BlockSpec((8, None, rows, HEAD_SIZE), lambda n: (0, place, 0, n)),
             spec,
         ],
         out_specs=spec,
@@ -282,17 +284,17 @@
 def layer(llm_query, llm_kv, connector, query, key, value, cotangent):
     swap = lambda x: lax.ppermute(x, "tp", SWAP_HALF)
     raw = swap(key[:1])
-    near = [exchange(to_blocks(s, 1, key, value)) for s in range(SAMPLE_COUNT)]
-    far = [[None, swap(near[0][:, 1])]]
-    far.append([swap(near[1][:, i]) for i in range(2)])
-    far[0][0] = exchange(to_blocks(0, 1, raw))[:, 0]
+    near = [exchange(to_blocks((key, 1, s), (value, 1, s))) for s in range(SAMPLE_COUNT)]
+    far_values = [swap(near[s][:, 1]) for s in range(SAMPLE_COUNT)]
+    far_keys = swap(near[1][:, :1])
     columns = gather_columns(connector)
     hidden = llm_hidden(llm_query, llm_kv)
-    query_gradient = exchange(to_blocks(0, 2, query, cotangent))
+    query_gradient = exchange(to_blocks((query, 2, 0), (cotangent, 2, 0), (raw, 1, 0)))
+    far_keys = [(query_gradient, 4), (far_keys, 0)]
     context = context_tokens(gather_rows(hidden), columns)
     out, carry = [], ()
     for s in range(SAMPLE_COUNT):
-        so = attention(s, query_gradient, near[s], *far[s])
+        so = attention(s, query_gradient, near[s], far_keys[s], far_values[s])
         result, partial = cross(s, so, query_gradient, context, carry)
         carry = (partial,)
         out.append(exchange(result))

time: 322 us -> 339 us (1.053)
  the two profiles are of different devices: /device:TPU:34 before, /device:TPU:82 now
where the time goes in v6:
time: 339 us; the launch traced here: 338 us
  starting transfers between devices  124 us (37%)
  waiting for transfers between devices  109 us (32%)
  blocking collectives  55.2 us (16%)
  Pallas kernels  30.8 us (9%)
  local copies, waits for them, and re-layouts  12.3 us (4%)
  other arithmetic  5.06 us (1%)
    ppermute x4, waiting for transfers between devices, layer(): swap = lambda x: lax.ppermute(x, 'tp', SWAP_HALF)  78 us
    all_to_all x1, blocking collectives, exchange(): lax.all_to_all(x, 'tp', split_axis=0, concat_axis=0, axis_index_groups=HA...  55.2 us
    all_to_all x6, starting transfers between devices, exchange(): lax.all_to_all(x, 'tp', split_axis=0, concat_axis=0, axis_index_groups=HA...  29.2 us
    ppermute x4, starting transfers between devices, layer(): swap = lambda x: lax.ppermute(x, 'tp', SWAP_HALF)  28.5 us
    ppermute x1, starting transfers between devices, llm_hidden(): take = lax.ppermute(give, 'tp', SWAP_HALF)  13.9 us
    pallas_call x2, Pallas kernels, attention(): pl.pallas_call(attention_kernel, grid=(3,), in_specs=[pl.BlockSpec((8, 1,...  12.9 us
    ppermute x1, starting transfers between devices, context_tokens(): there = lax.ppermute(mine, 'tp', SWAP_HALF)  12.1 us
    ppermute x1, waiting for transfers between devices, context_tokens(): there = lax.ppermute(mine, 'tp', SWAP_HALF)  10.5 us
  transfers between devices with their start and end apart: 22, of which 9 were waited for; matrix products, arithmetic and copies ran while one was open for 4% of the time, Pallas kernels for 5%

profile of v6, /device:TPU:82, one launch (start us, length us, event | category | flops | bytes accessed | tf_op | source)
XLA Modules:
  0.0 338.0 jit_solution(12407002781658064098)
XLA Ops:
  0.7 0.9 constant_dynamic-slice_fusion
  1.5 13.9 %collective-permute-start.2 = (bf16[2,20,512]{2,0,1:T(2,128)(2,1)S(1)}, bf16[2,20,512]{2,0,1:T(2,128)(2,1)S(1)}, u32[]{:S(2)}, u32[]{:S(2)}) collective-permute-start(bf16[2,20,512]{2,0,1:T(2,128)(2,1)S(1)} %get-tuple-element.28), channel_id=1, source_target_pairs={{0,8},{1,9},{2,10},{3,11},{4,12},{5,13},{6,14},{7,15},{8,0},{9,1},... | collective-permute-start | bytes 122888 | tf_op jit(solution)/shard_map/ppermute | solution.py:93
  15.5 3.4 collective-permute-start.7
  19.9 4.8 %all-to-all-start.2 = ((bf16[8,2,2,20,128]{4,2,3,1,0:T(2,128)(2,1)}), bf16[8,2,2,20,128]{4,2,3,1,0:T(2,128)(2,1)S(1)}, u32[]{:S(2)}, u32[]{:S(2)}) async-start(bf16[8,2,2,20,128]{4,2,3,1,0:T(2,128)(2,1)} %bitcast.12), calls=%async_computation.2 | async-start | bytes 327680 | tf_op jit(solution)/shard_map/all_to_all | solution.py:84
  24.9 0.9 reshape_squeeze.10
  25.8 2.0 to_blocks.4
  27.8 1.9 all-to-all-done.2
  29.7 4.9 %all-to-all-start.1 = ((bf16[8,2,64,384]{3,2,1,0:T(8,128)(2,1)}), bf16[8,2,64,384]{3,2,1,0:T(8,128)(2,1)S(1)}, u32[]{:S(2)}, u32[]{:S(2)}) async-start(bf16[8,2,64,384]{3,2,1,0:T(8,128)(2,1)} %bitcast.74), calls=%async_computation.1 | async-start | bytes 1572864 | tf_op jit(solution)/shard_map/all_to_all | solution.py:84
  36.2 7.6 %collective-permute-start.3 = (bf16[64,512]{1,0:T(8,128)(2,1)S(1)}, bf16[64,512]{1,0:T(8,128)(2,1)S(1)}, u32[]{:S(2)}, u32[]{:S(2)}) collective-permute-start(bf16[64,512]{1,0:T(8,128)(2,1)S(1)} %reshape.124), channel_id=1, source_target_pairs={{0,64},{16,80},{32,96},{48,112},{64,0},{80,16},{96,32},{112,48},{1... | collective-permute-start | bytes 196616 | tf_op jit(solution)/shard_map/ppermute | solution.py:125
  44.5 3.4 collective-permute-done.3
  48.4 3.2 collective-permute-start.4
  51.7 3.1 collective-permute-start.8
  54.8 2.5 collective-permute-start.5
  57.4 2.0 to_blocks.5
  59.4 3.5 %collective-permute-start.6 = (bf16[128,512]{1,0:T(8,128)(2,1)}, bf16[128,512]{1,0:T(8,128)(2,1)S(1)}, u32[]{:S(2)}, u32[]{:S(2)}) collective-permute-start(bf16[128,512]{1,0:T(8,128)(2,1)} %get-tuple-element.29), channel_id=1, source_target_pairs={{0,384},{16,400},{32,416},{48,432},{64,448},{80,464},{96,480},{112... | collective-permute-start | bytes 393224 | tf_op jit(solution)/shard_map/ppermute | solution.py:128
  62.9 4.8 %all-to-all-start.5 = ((bf16[8,2,64,384]{3,2,1,0:T(8,128)(2,1)}), bf16[8,2,64,384]{3,2,1,0:T(8,128)(2,1)S(1)}, u32[]{:S(2)}, u32[]{:S(2)}) async-start(bf16[8,2,64,384]{3,2,1,0:T(8,128)(2,1)} %bitcast.75), calls=%async_computation.5 | async-start | bytes 1572864 | tf_op jit(solution)/shard_map/all_to_all | solution.py:84
  67.7 0.9 constant_dynamic-update-slice_fusion.3
  70.0 1.1 copy.28
  71.1 8.3 %all-to-all-done.5.near_ref = bf16[8,2,64,384]{3,2,1,0:T(8,128)(2,1)S(1)} async-done(((bf16[8,2,64,384]{3,2,1,0:T(8,128)(2,1)}), bf16[8,2,64,384]{3,2,1,0:T(8,128)(2,1)S(1)}, u32[]{:S(2)}, u32[]{:S(2)}) %all-to-all-start.5) | async-done | bytes 786464 | tf_op jit(solution)/shard_map/all_to_all | solution.py:84
  79.4 4.9 %all-to-all-start.3 = ((bf16[8,2,2,64,192]{4,3,2,1,0:T(8,128)(2,1)}), bf16[8,2,2,64,192]{4,3,2,1,0:T(8,128)(2,1)S(1)}, u32[]{:S(2)}, u32[]{:S(2)}) async-start(bf16[8,2,2,64,192]{4,3,2,1,0:T(8,128)(2,1)} %bitcast.71), calls=%async_computation.3 | async-start | bytes 2097152 | tf_op jit(solution)/shard_map/all_to_all | solution.py:84
  84.3 10.7 %collective-permute-start = (bf16[1,64,3072]{2,1,0:T(8,128)(2,1)S(1)}, bf16[1,64,3072]{2,1,0:T(8,128)(2,1)S(1)}, u32[]{:S(2)}, u32[]{:S(2)}) collective-permute-start(bf16[1,64,3072]{2,1,0:T(8,128)(2,1)S(1)} %slice_bitcast_fusion.2), channel_id=1, source_target_pairs={{0,8},{1,9},{2,10},{3,11},{4,12},{5,13},{6,14},{7,15},{8,0},{9,1},... | collective-permute-start | bytes 1179656 | tf_op jit(solution)/shard_map/ppermute | solution.py:285
  95.1 26.6 %collective-permute-done.refs_2_ = bf16[1,64,3072]{2,1,0:T(8,128)(2,1)S(1)} collective-permute-done((bf16[1,64,3072]{2,1,0:T(8,128)(2,1)S(1)}, bf16[1,64,3072]{2,1,0:T(8,128)(2,1)S(1)}, u32[]{:S(2)}, u32[]{:S(2)}) %collective-permute-start) | collective-permute-done | bytes 393248 | tf_op jit(solution)/shard_map/ppermute | solution.py:285
  122.4 2.5 to_blocks.3
  125.0 1.0 copy-done.4
  126.0 4.8 %all-to-all-start = ((bf16[8,5,64,384]{3,2,1,0:T(8,128)(2,1)}), bf16[8,5,64,384]{3,2,1,0:T(8,128)(2,1)S(1)}, u32[]{:S(2)}, u32[]{:S(2)}) async-start(bf16[8,5,64,384]{3,2,1,0:T(8,128)(2,1)} %bitcast.66), calls=%async_computation | async-start | bytes 3932160 | tf_op jit(solution)/shard_map/all_to_all | solution.py:84
  130.8 2.1 reduce_sum.22
  132.9 12.1 %collective-permute-start.9 = (bf16[2,2,64,192]{3,2,1,0:T(8,128)(2,1)}, bf16[2,2,64,192]{3,2,1,0:T(8,128)(2,1)S(1)}, u32[]{:S(2)}, u32[]{:S(2)}) collective-permute-start(bf16[2,2,64,192]{3,2,1,0:T(8,128)(2,1)} %reduce_sum.22), channel_id=1, source_target_pairs={{0,8},{1,9},{2,10},{3,11},{4,12},{5,13},{6,14},{7,15},{8,0},{9,1},... | collective-permute-start | bytes 294920 | tf_op jit(solution)/shard_map/ppermute | solution.py:141
  145.0 2.5 collective-permute-start.1
  147.5 10.5 %collective-permute-done.9 = bf16[2,2,64,192]{3,2,1,0:T(8,128)(2,1)S(1)} collective-permute-done((bf16[2,2,64,192]{3,2,1,0:T(8,128)(2,1)}, bf16[2,2,64,192]{3,2,1,0:T(8,128)(2,1)S(1)}, u32[]{:S(2)}, u32[]{:S(2)}) %collective-permute-start.9) | collective-permute-done | bytes 98336 | tf_op jit(solution)/shard_map/ppermute | solution.py:141
  158.0 0.9 add_convert_fusion
  159.0 2.0 collective-permute-start.10
  161.0 4.8 %collective-permute-start.11 = (bf16[2,64,192]{2,1,0:T(8,128)(2,1)S(1)}, bf16[2,64,192]{2,1,0:T(8,128)(2,1)S(1)}, u32[]{:S(2)}, u32[]{:S(2)}) collective-permute-start(bf16[2,64,192]{2,1,0:T(8,128)(2,1)S(1)} %get-tuple-element.24), channel_id=1, source_target_pairs={{0,256},{1,384},{2,258},{3,386},{4,320},{5,448},{6,322},{7,450},{8... | collective-permute-start | bytes 147464 | tf_op jit(solution)/shard_map/ppermute | solution.py:154
  165.9 13.4 %collective-permute-start.12 = (bf16[8,1,64,384]{3,2,1,0:T(8,128)(2,1)S(1)}, bf16[8,1,64,384]{3,2,1,0:T(8,128)(2,1)S(1)}, u32[]{:S(2)}, u32[]{:S(2)}) collective-permute-start(bf16[8,1,64,384]{3,2,1,0:T(8,128)(2,1)S(1)} %get-tuple-element.18), channel_id=1, source_target_pairs={{0,8},{1,9},{2,10},{3,11},{4,12},{5,13},{6,14},{7,15},{8,0},{9,1},... | collective-permute-start | bytes 1179656 | tf_op jit(solution)/shard_map/ppermute | solution.py:285
  179.3 1.9 collective-permute-start.13
  182.1 21.8 %collective-permute-done.1.fv_ref = bf16[8,64,384]{2,1,0:T(8,128)(2,1)} collective-permute-done((bf16[8,64,384]{2,1,0:T(8,128)(2,1)S(1)}, bf16[8,64,384]{2,1,0:T(8,128)(2,1)}, u32[]{:S(2)}, u32[]{:S(2)}) %collective-permute-start.1) | collective-permute-done | bytes 393248 | tf_op jit(solution)/shard_map/ppermute | solution.py:285
  203.9 1.3 copy-done
  205.2 6.4 %latent_attention.2.so_ref = bf16[8,64,384]{2,1,0:T(8,128)(2,1)} custom-call(bf16[8,5,64,384]{3,2,1,0:T(8,128)(2,1)} %copy-done, bf16[8,2,64,384]{3,2,1,0:T(8,128)(2,1)} %copy-done.3, bf16[8,5,64,384]{3,2,1,0:T(8,128)(2,1)} %copy-done, bf16[8,64,384]{2,1,0:T(8,128)(2,1)} %collective-permute-done.1.fv_ref), custom_call_target="tpu_custom_call" | custom-call | tf_op jit(solution)/shard_map/latent_attention/pallas_call | solution.py:189
  211.7 4.5 %cross_attention.2 = (bf16[8,2,64,384]{3,2,1,0:T(8,128)(2,1)}, f32[2,64,384]{2,1,0:T(8,128)}) custom-call(bf16[8,64,384]{2,1,0:T(8,128)(2,1)} %latent_attention.2.so_ref, bf16[8,5,64,384]{3,2,1,0:T(8,128)(2,1)} %copy-done, bf16[2,64,384]{2,1,0:T(8,128)(2,1)} %pad_maximum_fusion.2.context_ref), custom_call_target="tpu_custom_call" | custom-call | tf_op jit(solution)/shard_map/cross_attention/pallas_call | solution.py:249
  216.1 17.2 %collective-permute-done.12.fk_ref = bf16[8,1,64,384]{3,2,1,0:T(8,128)(2,1)S(1)} collective-permute-done((bf16[8,1,64,384]{3,2,1,0:T(8,128)(2,1)S(1)}, bf16[8,1,64,384]{3,2,1,0:T(8,128)(2,1)S(1)}, u32[]{:S(2)}, u32[]{:S(2)}) %collective-permute-start.12) | collective-permute-done | bytes 393248 | tf_op jit(solution)/shard_map/ppermute | solution.py:285
  233.3 12.4 %collective-permute-done.13.fv_ref = bf16[8,64,384]{2,1,0:T(8,128)(2,1)S(1)} collective-permute-done((bf16[8,64,384]{2,1,0:T(8,128)(2,1)S(1)}, bf16[8,64,384]{2,1,0:T(8,128)(2,1)S(1)}, u32[]{:S(2)}, u32[]{:S(2)}) %collective-permute-start.13) | collective-permute-done | bytes 393248 | tf_op jit(solution)/shard_map/ppermute | solution.py:285
  246.5 6.4 %latent_attention.3.so_ref = bf16[8,64,384]{2,1,0:T(8,128)(2,1)} custom-call(bf16[8,5,64,384]{3,2,1,0:T(8,128)(2,1)} %copy-done, bf16[8,2,64,384]{3,2,1,0:T(8,128)(2,1)} %copy-done.1, bf16[8,1,64,384]{3,2,1,0:T(8,128)(2,1)} %copy-done.7, bf16[8,64,384]{2,1,0:T(8,128)(2,1)} %copy-done.8), custom_call_target="tpu_custom_call" | custom-call | tf_op jit(solution)/shard_map/latent_attention/pallas_call | solution.py:189
  252.9 4.5 %cross_attention.3 = (bf16[8,2,64,384]{3,2,1,0:T(8,128)(2,1)}, bf16[2,64,384]{2,1,0:T(8,128)(2,1)}) custom-call(bf16[8,64,384]{2,1,0:T(8,128)(2,1)} %latent_attention.3.so_ref, bf16[8,5,64,384]{3,2,1,0:T(8,128)(2,1)} %copy-done, bf16[2,64,384]{2,1,0:T(8,128)(2,1)} %pad_maximum_fusion.2.context_ref, f32[2,64,384]{2,1,0:T(8,128)} %get-tuple-element.10.refs_0_), custom_call_target="tpu_custom_call" | custom-call | tf_op jit(solution)/shard_map/cross_attention/pallas_call | solution.py:249
  257.4 55.2 %all_to_all.35 = bf16[8,2,64,384]{3,2,1,0:T(8,128)(2,1)} all-to-all(bf16[8,2,64,384]{3,2,1,0:T(8,128)(2,1)} %get-tuple-element.11), channel_id=1, replica_groups={{0,1,2,3,4,5,6,7},{8,9,10,11,12,13,14,15},{16,17,18,19,20,21,22,23},{24..., dimensions={0} | all-to-all | bytes 1572864 | tf_op jit(solution)/shard_map/all_to_all | solution.py:84
  312.6 4.9 %all-to-all-start.4 = ((bf16[8,2,64,384]{3,2,1,0:T(8,128)(2,1)}), bf16[8,2,64,384]{3,2,1,0:T(8,128)(2,1)S(1)}, u32[]{:S(2)}, u32[]{:S(2)}) async-start(bf16[8,2,64,384]{3,2,1,0:T(8,128)(2,1)} %get-tuple-element.9), calls=%async_computation.4 | async-start | bytes 1572864 | tf_op jit(solution)/shard_map/all_to_all | solution.py:84
  318.2 9.3 %collective-permute-start.15 = (bf16[2,64,192]{2,1,0:T(8,128)(2,1)S(1)}, bf16[2,64,192]{2,1,0:T(8,128)(2,1)S(1)}, u32[]{:S(2)}, u32[]{:S(2)}) collective-permute-start(bf16[2,64,192]{2,1,0:T(8,128)(2,1)S(1)} %get-tuple-element.26), channel_id=1, source_target_pairs={{0,1},{1,9},{2,3},{3,11},{4,5},{5,13},{6,7},{7,15},{8,0},{9,8},{10... | collective-permute-start | bytes 147464 | tf_op jit(solution)/shard_map/ppermute | solution.py:276
  327.6 6.6 %collective-permute-done.15 = bf16[2,64,192]{2,1,0:T(8,128)(2,1)S(1)} collective-permute-done((bf16[2,64,192]{2,1,0:T(8,128)(2,1)S(1)}, bf16[2,64,192]{2,1,0:T(8,128)(2,1)S(1)}, u32[]{:S(2)}, u32[]{:S(2)}) %collective-permute-start.15) | collective-permute-done | bytes 49184 | tf_op jit(solution)/shard_map/ppermute | solution.py:276
  334.8 0.9 copy-done.5
  335.7 2.3 from_blocks.1
  (68 shorter events, 9.2 us)
Async XLA Ops:
  1.5 17.4 %collective-permute-start.2 = (bf16[2,20,512]{2,0,1:T(2,128)(2,1)S(1)}, bf16[2,20,512]{2,0,1:T(2,128)(2,1)S(1)}, u32[]{:S(2)}, u32[]{:S(2)}) collective-permute-start(bf16[2,20,512]{2,0,1:T(2,128)(2,1)S(1)} %get-tuple-element.28), channel_id=1, source_target_pairs={{0,8},{1,9},{2,10},{3,11},{4,12},{5,13},{6,14},{7,15},{8,0},{9,1},... | collective-permute-start | bytes 122888 | tf_op jit(solution)/shard_map/ppermute | solution.py:93
  15.5 36.2 %collective-permute-start.7 = (bf16[1,512,192]{1,2,0:T(8,128)(2,1)}, bf16[1,512,192]{1,2,0:T(8,128)(2,1)S(1)}, u32[]{:S(2)}, u32[]{:S(2)}) collective-permute-start(bf16[1,512,192]{1,2,0:T(8,128)(2,1)} %bitcast.79), channel_id=1, source_target_pairs={{0,32},{16,48},{32,0},{48,16},{64,96},{80,112},{96,64},{112,80},{1... | collective-permute-start | bytes 589832 | tf_op jit(solution)/shard_map/ppermute | solution.py:119
  19.9 9.8 %all-to-all-start.2 = ((bf16[8,2,2,20,128]{4,2,3,1,0:T(2,128)(2,1)}), bf16[8,2,2,20,128]{4,2,3,1,0:T(2,128)(2,1)S(1)}, u32[]{:S(2)}, u32[]{:S(2)}) async-start(bf16[8,2,2,20,128]{4,2,3,1,0:T(2,128)(2,1)} %bitcast.12), calls=%async_computation.2 | async-start | bytes 327680 | tf_op jit(solution)/shard_map/all_to_all | solution.py:84
  29.7 33.1 %all-to-all-start.1 = ((bf16[8,2,64,384]{3,2,1,0:T(8,128)(2,1)}), bf16[8,2,64,384]{3,2,1,0:T(8,128)(2,1)S(1)}, u32[]{:S(2)}, u32[]{:S(2)}) async-start(bf16[8,2,64,384]{3,2,1,0:T(8,128)(2,1)} %bitcast.74), calls=%async_computation.1 | async-start | bytes 1572864 | tf_op jit(solution)/shard_map/all_to_all | solution.py:84
  34.6 17.0 %copy-start.6 = (bf16[512,192]{0,1:T(8,128)(2,1)S(1)}, bf16[512,192]{0,1:T(8,128)(2,1)}, u32[]{:S(2)}) copy-start(bf16[512,192]{0,1:T(8,128)(2,1)} %param.9) | copy-start | bytes 589828
  36.2 11.6 %collective-permute-start.3 = (bf16[64,512]{1,0:T(8,128)(2,1)S(1)}, bf16[64,512]{1,0:T(8,128)(2,1)S(1)}, u32[]{:S(2)}, u32[]{:S(2)}) collective-permute-start(bf16[64,512]{1,0:T(8,128)(2,1)S(1)} %reshape.124), channel_id=1, source_target_pairs={{0,64},{16,80},{32,96},{48,112},{64,0},{80,16},{96,32},{112,48},{1... | collective-permute-start | bytes 196616 | tf_op jit(solution)/shard_map/ppermute | solution.py:125
  48.4 19.3 %collective-permute-start.4 = (bf16[128,512]{1,0:T(8,128)(2,1)}, bf16[128,512]{1,0:T(8,128)(2,1)S(1)}, u32[]{:S(2)}, u32[]{:S(2)}) collective-permute-start(bf16[128,512]{1,0:T(8,128)(2,1)} %get-tuple-element.29), channel_id=1, source_target_pairs={{0,128},{16,144},{32,160},{48,176},{64,192},{80,208},{96,224},{112... | collective-permute-start | bytes 393224 | tf_op jit(solution)/shard_map/ppermute | solution.py:128
  51.7 17.0 %collective-permute-start.8 = (bf16[2,512,192]{1,2,0:T(8,128)(2,1)S(1)}, bf16[2,512,192]{1,2,0:T(8,128)(2,1)S(1)}, u32[]{:S(2)}, u32[]{:S(2)}) collective-permute-start(bf16[2,512,192]{1,2,0:T(8,128)(2,1)S(1)} %pad_maximum_fusion.1), channel_id=1, source_target_pairs={{0,16},{16,0},{32,48},{48,32},{64,80},{80,64},{96,112},{112,96},{1... | collective-permute-start | bytes 1179656 | tf_op jit(solution)/shard_map/ppermute | solution.py:119
  54.8 12.9 %collective-permute-start.5 = (bf16[128,512]{1,0:T(8,128)(2,1)}, bf16[128,512]{1,0:T(8,128)(2,1)}, u32[]{:S(2)}, u32[]{:S(2)}) collective-permute-start(bf16[128,512]{1,0:T(8,128)(2,1)} %get-tuple-element.29), channel_id=1, source_target_pairs={{0,256},{16,272},{32,288},{48,304},{64,320},{80,336},{96,352},{112... | collective-permute-start | bytes 393224 | tf_op jit(solution)/shard_map/ppermute | solution.py:128
  59.4 9.3 %collective-permute-start.6 = (bf16[128,512]{1,0:T(8,128)(2,1)}, bf16[128,512]{1,0:T(8,128)(2,1)S(1)}, u32[]{:S(2)}, u32[]{:S(2)}) collective-permute-start(bf16[128,512]{1,0:T(8,128)(2,1)} %get-tuple-element.29), channel_id=1, source_target_pairs={{0,384},{16,400},{32,416},{48,432},{64,448},{80,464},{96,480},{112... | collective-permute-start | bytes 393224 | tf_op jit(solution)/shard_map/ppermute | solution.py:128
  62.9 82.1 %copy-start.3 = (bf16[8,2,64,384]{3,2,1,0:T(8,128)(2,1)}, bf16[8,2,64,384]{3,2,1,0:T(8,128)(2,1)S(1)}, u32[]{:S(2)}) copy-start(bf16[8,2,64,384]{3,2,1,0:T(8,128)(2,1)S(1)} %all-to-all-done.1.near_ref) | copy-start | bytes 2359300
  62.9 16.5 %all-to-all-start.5 = ((bf16[8,2,64,384]{3,2,1,0:T(8,128)(2,1)}), bf16[8,2,64,384]{3,2,1,0:T(8,128)(2,1)S(1)}, u32[]{:S(2)}, u32[]{:S(2)}) async-start(bf16[8,2,64,384]{3,2,1,0:T(8,128)(2,1)} %bitcast.75), calls=%async_computation.5 | async-start | bytes 1572864 | tf_op jit(solution)/shard_map/all_to_all | solution.py:84
  70.0 14.3 %copy-start.2 = (bf16[1,2,64,3072]{3,2,1,0:T(8,128)(2,1)S(1)}, bf16[1,2,64,3072]{3,2,1,0:T(8,128)(2,1)}, u32[]{:S(2)}) copy-start(bf16[1,2,64,3072]{3,2,1,0:T(8,128)(2,1)} %param.11) | copy-start | bytes 2359300
  79.4 86.5 %copy-start.1 = (bf16[8,2,64,384]{3,2,1,0:T(8,128)(2,1)}, bf16[8,2,64,384]{3,2,1,0:T(8,128)(2,1)S(1)}, u32[]{:S(2)}) copy-start(bf16[8,2,64,384]{3,2,1,0:T(8,128)(2,1)S(1)} %all-to-all-done.5.near_ref) | copy-start | bytes 2359300
  79.4 45.6 %all-to-all-start.3 = ((bf16[8,2,2,64,192]{4,3,2,1,0:T(8,128)(2,1)}), bf16[8,2,2,64,192]{4,3,2,1,0:T(8,128)(2,1)S(1)}, u32[]{:S(2)}, u32[]{:S(2)}) async-start(bf16[8,2,2,64,192]{4,3,2,1,0:T(8,128)(2,1)} %bitcast.71), calls=%async_computation.3 | async-start | bytes 2097152 | tf_op jit(solution)/shard_map/all_to_all | solution.py:84
  84.3 37.4 %collective-permute-start = (bf16[1,64,3072]{2,1,0:T(8,128)(2,1)S(1)}, bf16[1,64,3072]{2,1,0:T(8,128)(2,1)S(1)}, u32[]{:S(2)}, u32[]{:S(2)}) collective-permute-start(bf16[1,64,3072]{2,1,0:T(8,128)(2,1)S(1)} %slice_bitcast_fusion.2), channel_id=1, source_target_pairs={{0,8},{1,9},{2,10},{3,11},{4,12},{5,13},{6,14},{7,15},{8,0},{9,1},... | collective-permute-start | bytes 1179656 | tf_op jit(solution)/shard_map/ppermute | solution.py:285
  121.7 0.7 copy-start.9
  125.0 1.0 copy-start.4
  126.0 78.0 %all-to-all-start = ((bf16[8,5,64,384]{3,2,1,0:T(8,128)(2,1)}), bf16[8,5,64,384]{3,2,1,0:T(8,128)(2,1)S(1)}, u32[]{:S(2)}, u32[]{:S(2)}) async-start(bf16[8,5,64,384]{3,2,1,0:T(8,128)(2,1)} %bitcast.66), calls=%async_computation | async-start | bytes 3932160 | tf_op jit(solution)/shard_map/all_to_all | solution.py:84
  132.9 25.2 %collective-permute-start.9 = (bf16[2,2,64,192]{3,2,1,0:T(8,128)(2,1)}, bf16[2,2,64,192]{3,2,1,0:T(8,128)(2,1)S(1)}, u32[]{:S(2)}, u32[]{:S(2)}) collective-permute-start(bf16[2,2,64,192]{3,2,1,0:T(8,128)(2,1)} %reduce_sum.22), channel_id=1, source_target_pairs={{0,8},{1,9},{2,10},{3,11},{4,12},{5,13},{6,14},{7,15},{8,0},{9,1},... | collective-permute-start | bytes 294920 | tf_op jit(solution)/shard_map/ppermute | solution.py:141
  145.0 58.9 %collective-permute-start.1 = (bf16[8,64,384]{2,1,0:T(8,128)(2,1)S(1)}, bf16[8,64,384]{2,1,0:T(8,128)(2,1)}, u32[]{:S(2)}, u32[]{:S(2)}) collective-permute-start(bf16[8,64,384]{2,1,0:T(8,128)(2,1)S(1)} %slice_bitcast_fusion.1), channel_id=1, source_target_pairs={{0,8},{1,9},{2,10},{3,11},{4,12},{5,13},{6,14},{7,15},{8,0},{9,1},... | collective-permute-start | bytes 1179656 | tf_op jit(solution)/shard_map/ppermute | solution.py:285
  159.0 22.3 %collective-permute-start.10 = (bf16[2,64,192]{2,1,0:T(8,128)(2,1)S(1)}, bf16[2,64,192]{2,1,0:T(8,128)(2,1)S(1)}, u32[]{:S(2)}, u32[]{:S(2)}) collective-permute-start(bf16[2,64,192]{2,1,0:T(8,128)(2,1)S(1)} %get-tuple-element.23), channel_id=1, source_target_pairs={{0,0},{1,128},{2,2},{3,130},{4,64},{5,192},{6,66},{7,194},{8,8},{9... | collective-permute-start | bytes 147464 | tf_op jit(solution)/shard_map/ppermute | solution.py:154
  161.0 20.3 %collective-permute-start.11 = (bf16[2,64,192]{2,1,0:T(8,128)(2,1)S(1)}, bf16[2,64,192]{2,1,0:T(8,128)(2,1)S(1)}, u32[]{:S(2)}, u32[]{:S(2)}) collective-permute-start(bf16[2,64,192]{2,1,0:T(8,128)(2,1)S(1)} %get-tuple-element.24), channel_id=1, source_target_pairs={{0,256},{1,384},{2,258},{3,386},{4,320},{5,448},{6,322},{7,450},{8... | collective-permute-start | bytes 147464 | tf_op jit(solution)/shard_map/ppermute | solution.py:154
  165.9 67.4 %collective-permute-start.12 = (bf16[8,1,64,384]{3,2,1,0:T(8,128)(2,1)S(1)}, bf16[8,1,64,384]{3,2,1,0:T(8,128)(2,1)S(1)}, u32[]{:S(2)}, u32[]{:S(2)}) collective-permute-start(bf16[8,1,64,384]{3,2,1,0:T(8,128)(2,1)S(1)} %get-tuple-element.18), channel_id=1, source_target_pairs={{0,8},{1,9},{2,10},{3,11},{4,12},{5,13},{6,14},{7,15},{8,0},{9,1},... | collective-permute-start | bytes 1179656 | tf_op jit(solution)/shard_map/ppermute | solution.py:285
  179.3 66.4 %collective-permute-start.13 = (bf16[8,64,384]{2,1,0:T(8,128)(2,1)S(1)}, bf16[8,64,384]{2,1,0:T(8,128)(2,1)S(1)}, u32[]{:S(2)}, u32[]{:S(2)}) collective-permute-start(bf16[8,64,384]{2,1,0:T(8,128)(2,1)S(1)} %get-tuple-element.17), channel_id=1, source_target_pairs={{0,8},{1,9},{2,10},{3,11},{4,12},{5,13},{6,14},{7,15},{8,0},{9,1},... | collective-permute-start | bytes 1179656 | tf_op jit(solution)/shard_map/ppermute | solution.py:285
  203.9 1.3 copy-start
  233.3 12.4 %copy-start.7 = (bf16[8,1,64,384]{3,2,1,0:T(8,128)(2,1)}, bf16[8,1,64,384]{3,2,1,0:T(8,128)(2,1)S(1)}, u32[]{:S(2)}) copy-start(bf16[8,1,64,384]{3,2,1,0:T(8,128)(2,1)S(1)} %collective-permute-done.12.fk_ref) | copy-start | bytes 1179652
  245.7 0.8 copy-start.8
  257.4 60.1 %copy-start.10 = (bf16[2,64,384]{2,1,0:T(8,128)(2,1)S(1)}, bf16[2,64,384]{2,1,0:T(8,128)(2,1)}, u32[]{:S(2)}) copy-start(bf16[2,64,384]{2,1,0:T(8,128)(2,1)} %get-tuple-element.14) | copy-start | bytes 294916
  312.6 22.2 %all-to-all-start.4 = ((bf16[8,2,64,384]{3,2,1,0:T(8,128)(2,1)}), bf16[8,2,64,384]{3,2,1,0:T(8,128)(2,1)S(1)}, u32[]{:S(2)}, u32[]{:S(2)}) async-start(bf16[8,2,64,384]{3,2,1,0:T(8,128)(2,1)} %get-tuple-element.9), calls=%async_computation.4 | async-start | bytes 1572864 | tf_op jit(solution)/shard_map/all_to_all | solution.py:84
  317.6 10.0 %collective-permute-start.14 = (bf16[2,64,192]{2,1,0:T(8,128)(2,1)S(1)}, bf16[2,64,192]{2,1,0:T(8,128)(2,1)S(1)}, u32[]{:S(2)}, u32[]{:S(2)}) collective-permute-start(bf16[2,64,192]{2,1,0:T(8,128)(2,1)S(1)} %get-tuple-element.25), channel_id=1, source_target_pairs={{0,0},{1,8},{2,2},{3,10},{4,4},{5,12},{6,6},{7,14},{8,1},{9,9},{10... | collective-permute-start | bytes 147464 | tf_op jit(solution)/shard_map/ppermute | solution.py:275
  318.2 15.9 %collective-permute-start.15 = (bf16[2,64,192]{2,1,0:T(8,128)(2,1)S(1)}, bf16[2,64,192]{2,1,0:T(8,128)(2,1)S(1)}, u32[]{:S(2)}, u32[]{:S(2)}) collective-permute-start(bf16[2,64,192]{2,1,0:T(8,128)(2,1)S(1)} %get-tuple-element.26), channel_id=1, source_target_pairs={{0,1},{1,9},{2,3},{3,11},{4,5},{5,13},{6,7},{7,15},{8,0},{9,8},{10... | collective-permute-start | bytes 147464 | tf_op jit(solution)/shard_map/ppermute | solution.py:276
  334.8 0.9 copy-start.5
